TPU v7x, 128 devices: a whole 4x4x4 slice. The times are simulated.
128 devices in a mesh: wide: 32 (over z, y, core), narrow: 4 (over x).
Axes of the slice: x: 4, y: 4, z: 4, core: 2. Of those that a mesh axis runs over, the one named last changes fastest.
Arguments:
- modal_unknowns: float32 [180, 262144], P(None, ('wide', 'narrow')), may hold values from -6 to 6
- timestep_metric_scaling: float32 [3, 262144], P(None, ('wide', 'narrow')), may hold values from 0.15 to 0.45
- surface_measure_quotient: float32 [4, 262144], P(None, ('wide', 'narrow')), may hold values from 0.5 to 1.5
- elastic_directional_derivs: float32 [3, 9, 9], replicated, may hold values from -2 to 2
- predictor_derivatives: float32 [3, 20, 20], replicated, may hold values from -1.25 to 1.25
- interior_gradient_tables: float32 [3, 20, 20], replicated, may hold values from -1.25 to 1.25
- interior_restriction: float32 [4, 10, 20], replicated, may hold values from -1.25 to 1.25
- surface_raise_tables: float32 [4, 20, 10], replicated, may hold values from -2 to 2
- riemann_numerical_tables: float32 [2, 9, 9], replicated, may hold values from -2 to 2
- boundary_polynomials_sampled: float32 [16, 10], replicated, may hold values from -2 to 2
- quadrature_gather_weights: float32 [16, 10], replicated, may hold values from -1.5 to 1.5
- thermal_diffusion_resolvent: float32 [64, 64], replicated, as said below
- hydraulic_diffusion_resolvent: float32 [64, 64], replicated, as said below
- thermal_field: float32 [64, 1048576], P(None, ('wide', 'narrow')), may hold values from -6 to 6
- fluid_load: float32 [64, 1048576], P(None, ('wide', 'narrow')), may hold values from -6 to 6
- earlier_sliding_speed: float32 [1048576], P(('wide', 'narrow')), may hold values from 0.05 to 2
- instant_sensitivity_a: float32 [1048576], P(('wide', 'narrow')), may hold values from 0.2 to 1
- aging_memory_theta: float32 [1048576], P(('wide', 'narrow')), may hold values from 0.2 to 0.8
- outbound_ghost_indices: int32 [6, 65536], P(None, ('wide', 'narrow')), may hold values from 0 to 8191
- boundary_entry_index: int32 [4, 262144], P(None, ('wide', 'narrow')), may hold values from 0 to 11263, as said below
- rupture_side_index: int32 [65536], P(('wide', 'narrow')), may hold values from -1 to 8191, as said below
- rupture_seat_partition: int32 [65536], P(('wide', 'narrow')), may hold values from -1 to 127, as said below
Outputs:
- advanced_unknowns: float32 [180, 262144], P(None, ('wide', 'narrow'))
- new_temperature: float32 [64, 1048576], P(None, ('wide', 'narrow'))
- new_pressure: float32 [64, 1048576], P(None, ('wide', 'narrow'))
- new_rate: float32 [1048576], P(('wide', 'narrow'))
Inputs may be any that keep to these rules, and one draw needn't show every extreme that they name: `boundary_entry_index`: points only into lists that exist for the partition: list k of the narrow group for k other than its own narrow index, the lower wide list only if w > 0, the upper only if w < 32 - 1. Slot s of a list is used only below a ragged count of that list; each partition uses one list in full. `rupture_side_index`: distinct faces of the partition; the live slots of a partition come first, the rest are -1 here and in rupture_seat_partition. `rupture_seat_partition`: slots i and i' of one partition share an owner when i // 4 == i' // 4 and have distinct owners otherwise; some partition has all 512 slots live; live counts are skewed, the busiest some three times the mean. `thermal_diffusion_resolvent`: dense with a dominant positive diagonal. `hydraulic_diffusion_resolvent`: dense with a dominant positive diagonal.
All inputs are finite; a program needn't handle non-finite values.
Results may differ from a plain program's by a relative error of at most 0.0003.
Values sent between devices are 32-bit elements; how exact they have to be, the bound alone decides.
No kernel may reach another device: no remote copies, remote signals or barrier semaphores. Data moves between devices by JAX's collectives and lax.ppermute only.
A program may use at most 128 MiB of HBM per device.

v0:
```python
import jax
import jax.numpy as jnp
import numpy as np
from jax import lax
from jax.experimental import pallas as pl
from jax.experimental.pallas import tpu as pltpu
from jax.sharding import PartitionSpec as P

NEWTON = 4
Q, NB, NJ, NG = 9, 20, 10, 16
LANES = 128
ROWS = Q * NB
HIGHEST = lax.Precision.HIGHEST
F32 = jnp.float32
BF16 = jnp.bfloat16
VMEM = pltpu.MemorySpace.VMEM
SMEM = pltpu.MemorySpace.SMEM
LIMIT = pltpu.CompilerParams(vmem_limit_bytes=56 * 1024 * 1024)


def tables():
    e = np.zeros((ROWS, Q), np.float32)
    f = np.zeros((ROWS, NB), np.float32)
    for q in range(Q):
        for b in range(NB):
            e[q * NB + b, q] = 1
            f[q * NB + b, b] = 1
    g = np.zeros((LANES, Q), np.float32)
    h = np.zeros((LANES, NJ), np.float32)
    for q in range(Q):
        for j in range(NJ):
            g[q * NJ + j, q] = 1
            h[q * NJ + j, j] = 1
    tile = np.zeros((LANES, NG), np.float32)
    for lane in range(LANES):
        tile[lane, lane % NG] = 1
    side = np.zeros((LANES, 4), np.float32)
    for q, column, low, high in ((3, 0, 0.5, 0.5), (6, 0, -0.5, 0.5), (0, 1, 0.5, 0.5), (7, 1, -0.5, 0.5)):
        side[q * NJ : (q + 1) * NJ, column] = low
        side[q * NJ : (q + 1) * NJ, 2 + column] = high
    mid = np.zeros((2, Q, Q), np.float32)
    mid[:] = 0.5 * np.eye(Q)
    mid[0, 6, 3] = -0.5
    mid[1, 6, 3] = 0.5
    linear = np.stack([g @ mid[0] @ g.T, g @ mid[1] @ g.T])
    slip = np.zeros((1, LANES), np.float32)
    slip[0, 3 * NJ : 4 * NJ] = -1.0
    slip[0, 6 * NJ : 7 * NJ] = 0.5
    pair = np.zeros((64, LANES), np.float32)
    for s in range(LANES):
        pair[s // 2, s] = 1
    return e, f, g, h, tile, side, linear, slip, pair


def dot(a, b, ca=1, cb=0, precision=HIGHEST):
    return lax.dot_general(
        a, b, (((ca,), (cb,)), ((), ())), precision=precision, preferred_element_type=F32
    )


def halves(x):
    high = x.astype(BF16)
    return high, (x - high.astype(F32)).astype(BF16)


def dot3(ah, al, bh, bl, cb=0):
    d = lambda a, b: lax.dot_general(
        a, b, (((1,), (cb,)), ((), ())), preferred_element_type=F32
    )
    return d(ah, bh) + (d(ah, bl) + d(al, bh))


def prepare_kernel(
    a, pd, kd, rs, sr, rt, bp, qg, cc, e, f, g, h, tile, side, linear, slip,
    mp_h, mp_l, mi_h, mi_l, wt_h, wt_l, wf_h, wf_l, ws_h, ws_l, wl, lin, vm,
):
    e_, f_, g_, h_ = e[...], f[...], g[...], h[...]

    def put(high, low, at, value):
        top, bottom = halves(value)
        high[at] = top
        low[at] = bottom

    for d in range(3):
        left = dot(dot(e_, a[d]), e_, 1, 1)
        put(mp_h, mp_l, d, -left * dot(dot(f_, pd[d]), f_, 1, 1))
        put(mi_h, mi_l, d, left * dot(dot(f_, kd[d]), f_, 1, 1))
    same = dot(e_, g_, 1, 1)
    r0 = dot(dot(e_, rt[0]), g_, 1, 1)
    r1 = dot(dot(e_, rt[1]), g_, 1, 1)
    for face in range(4):
        put(wt_h, wt_l, face, same * dot(dot(f_, rs[face], 1, 1), h_, 1, 1))
        lift = dot(dot(f_, sr[face]), h_, 1, 1)
        put(wf_h, wf_l, face, r0 * lift)
        put(wf_h, wf_l, 4 + face, r1 * lift)
        put(ws_h, ws_l, face, (r0 + r1) * lift)
    hb = dot(dot(h_, bp[...], 1, 1), tile[...], 1, 1)
    for i in range(4):
        wl[i] = hb * side[:, i : i + 1]
    hch = dot(dot(h_, cc[...]), h_, 1, 1)
    lin[0] = hch * linear[0]
    lin[1] = hch * linear[1]
    vm[...] = dot(dot(tile[...], qg[...]), h_, 1, 1) * slip[...]


def predictor_kernel(u, t, mp_h, mp_l, wt_h, wt_l, integral, faces, padded):
    times = t[...]
    current = u[...]
    total = current
    factor = 1.0
    for degree in range(1, 4):
        xh, xl = halves(current)
        current = (
            dot3(mp_h[0], mp_l[0], xh, xl) * times[0:1]
            + dot3(mp_h[1], mp_l[1], xh, xl) * times[1:2]
            + dot3(mp_h[2], mp_l[2], xh, xl) * times[2:3]
        )
        factor = factor * (degree + 1)
        total = total + current * (1.0 / factor)
    integral[...] = total
    padded[...] = jnp.zeros(padded.shape, F32)
    padded[0:ROWS, :] = total
    turned = padded[...].T[:, 0:ROWS]
    xh, xl = halves(turned)
    for face in range(4):
        faces[face] = dot3(xh, xl, wt_h[face], wt_l[face])


def volume_kernel(u, t, integral, mi_h, mi_l, partial):
    times = t[...]
    xh, xl = halves(integral[...])
    partial[...] = (
        u[...]
        + dot3(mi_h[0], mi_l[0], xh, xl) * times[0:1]
        + dot3(mi_h[1], mi_l[1], xh, xl) * times[1:2]
        + dot3(mi_h[2], mi_l[2], xh, xl) * times[2:3]
    )


def send_kernel(index, faces, group, lower, upper):
    for r in range(6):
        target, base = (group, r * 512) if r < 4 else ((lower, 0) if r == 4 else (upper, 0))

        def body(i, carry, r=r, target=target, base=base):
            for k in range(16):
                n = i * 16 + k
                target[pl.ds(base + n, 1), :] = faces[pl.ds(index[r, n], 1), :]
            return carry

        lax.fori_loop(0, 32, body, 0)


def thermal_kernel(th, fl, speed, shape, tr, hr, new_th, new_fl, top):
    v = speed[...]
    old = th[...]
    warmed = old + shape[...] * (0.5 * v * v)
    ah, al = halves(tr[...])
    xh, xl = halves(warmed)
    fresh = dot3(ah, al, xh, xl)
    new_th[...] = fresh
    bh, bl = halves(hr[...])
    yh, yl = halves(fl[...] + 0.5 * (fresh - old))
    pressure = dot3(bh, bl, yh, yl)
    new_fl[...] = pressure
    for r in range(top.shape[0]):
        top[r : r + 1, :] = pressure[0:1, r * LANES : (r + 1) * LANES]


def payload_kernel(slot, entry, faces, group, lower, upper, payload, table):
    count = faces.shape[0]
    extent = count + group.shape[0] + lower.shape[0] + upper.shape[0]
    table[0:count, :] = faces[...]
    at = count
    for part in (group, lower, upper):
        table[at : at + part.shape[0], :] = part[...]
        at += part.shape[0]
    table[extent : extent + 8, :] = jnp.zeros((8, LANES), F32)

    def body(o, carry):
        for k in range(4):
            face = slot[o, k]
            live = face >= 0
            safe = jnp.maximum(face, 0)
            inner = jnp.where(live, face, extent)
            outer = jnp.where(live, entry[lax.shift_right_logical(safe, 11), safe & 2047], extent)
            payload[pl.ds(o * 8 + k, 1), :] = table[pl.ds(inner, 1), :]
            payload[pl.ds(o * 8 + 4 + k, 1), :] = table[pl.ds(outer, 1), :]
        return carry

    lax.fori_loop(0, slot.shape[0], body, 0)


def outside_kernel(
    entry, faces, group, lower, upper, partial, area, wf_h, wf_l, base, table, outside
):
    count = faces.shape[0]
    table[0:count, :] = faces[...]
    at = count
    for part in (group, lower, upper):
        table[at : at + part.shape[0], :] = part[...]
        at += part.shape[0]
    elems = count // 4
    result = partial[...]
    for face in range(4):

        def body(i, carry, face=face):
            for k in range(16):
                n = i * 16 + k
                outside[pl.ds(n, 1), :] = table[pl.ds(entry[face, n], 1), :]
            return carry

        lax.fori_loop(0, elems // 16, body, 0)
        th, tl = halves(table[face * elems : (face + 1) * elems, :])
        oh, ol = halves(outside[...])
        flux = dot3(wf_h[face], wf_l[face], th, tl, 1) + dot3(
            wf_h[4 + face], wf_l[4 + face], oh, ol, 1
        )
        result = result - flux * area[face : face + 1, :]
    base[...] = result


def fault_kernel(arrived, top, speed, sense, memory, wl, lin, vm, pair, imposed, rate):
    lanes = lax.shift_right_logical(lax.broadcasted_iota(jnp.int32, (LANES, LANES), 1), 4)
    half = (lax.broadcasted_iota(jnp.int32, (LANES, LANES), 0) & 1) * 4
    locked = jnp.zeros((LANES, LANES), F32)
    normal = jnp.zeros((LANES, LANES), F32)
    for k in range(4):
        minus = arrived[pl.ds(k, LANES, stride=8), :]
        plus = arrived[pl.ds(4 + k, LANES, stride=8), :]
        mine = lanes == half + k
        locked = locked + jnp.where(mine, dot(minus, wl[0]) + dot(plus, wl[2]), 0.0)
        normal = normal + jnp.where(mine, dot(minus, wl[1]) + dot(plus, wl[3]), 0.0)
    locked = dot(pair[...], locked)
    normal = dot(pair[...], normal)
    excess = 2.0 + normal - top[...]
    effective = jnp.maximum(excess, 0.0) + jnp.log1p(jnp.exp(-jnp.abs(excess)))
    strength = effective * sense[...]
    weight = 0.5 * jnp.exp(memory[...] / sense[...])
    v = speed[...]
    for _ in range(NEWTON):
        scaled = weight * v
        root = jnp.sqrt(1.0 + scaled * scaled)
        size = jnp.log(jnp.abs(scaled) + root)
        mismatch = locked - v - strength * jnp.where(scaled < 0.0, -size, size)
        slope = -1.0 - strength * weight / root
        v = v - mismatch / slope
    rate[...] = v
    spread = dot(pair[...], v, 0, 0)
    for k in range(4):
        minus = arrived[pl.ds(k, LANES, stride=8), :]
        plus = arrived[pl.ds(4 + k, LANES, stride=8), :]
        mine = jnp.where(lanes == half + k, spread, 0.0)
        imposed[pl.ds(k, LANES, stride=4), :] = (
            dot(minus, lin[0]) + dot(plus, lin[1]) + dot(mine, vm[...])
        )


def finish_kernel(slot, returned, base, area, ws_h, ws_l, out, spread):
    count = spread.shape[0] - 8
    elems = count // 4
    spread[...] = jnp.zeros(spread.shape, F32)

    def body(o, carry):
        for k in range(4):
            face = slot[o, k]
            target = jnp.where(face >= 0, face, count)
            spread[pl.ds(target, 1), :] = returned[pl.ds(o * 4 + k, 1), :]
        return carry

    lax.fori_loop(0, slot.shape[0], body, 0)
    result = base[...]
    for face in range(4):
        zh, zl = halves(spread[face * elems : (face + 1) * elems, :])
        result = result - dot3(ws_h[face], ws_l[face], zh, zl, 1) * area[face : face + 1, :]
    out[...] = result


def shaped(shape, dtype=F32):
    return jax.ShapeDtypeStruct(shape, dtype)


def whole(count, smem=()):
    return [pl.BlockSpec(memory_space=SMEM if i in smem else VMEM) for i in range(count)]


def shift(array, axis, by):
    peers = lax.axis_size(axis)
    pairs = [(i, i + by) for i in range(peers) if 0 <= i + by < peers]
    return lax.ppermute(array, axis, pairs)


def per_device(
    modal_unknowns,
    timestep_metric_scaling,
    surface_measure_quotient,
    elastic_directional_derivs,
    predictor_derivatives,
    interior_gradient_tables,
    interior_restriction,
    surface_raise_tables,
    riemann_numerical_tables,
    boundary_polynomials_sampled,
    quadrature_gather_weights,
    thermal_diffusion_resolvent,
    hydraulic_diffusion_resolvent,
    thermal_field,
    fluid_load,
    earlier_sliding_speed,
    instant_sensitivity_a,
    aging_memory_theta,
    outbound_ghost_indices,
    boundary_entry_index,
    rupture_side_index,
    rupture_seat_partition,
):
    elems = modal_unknowns.shape[1]
    faces_total = 4 * elems
    devices = lax.axis_size(("wide", "narrow"))
    points = thermal_field.shape[1]
    e, f, g, h, tile, side, linear, slip, pair = tables()
    cross = lax.dot_general(
        boundary_polynomials_sampled,
        quadrature_gather_weights,
        (((0,), (0,)), ((), ())),
        precision=HIGHEST,
    )

    owners = rupture_seat_partition.reshape(devices, 4)[:, 0]
    listed = (owners[None, :] == jnp.arange(devices, dtype=jnp.int32)[:, None])[:, :, None]
    slot = jnp.sum(jnp.where(listed, rupture_side_index.reshape(devices, 4)[None] + 1, 0), axis=1) - 1
    ruptured = jnp.any(
        rupture_side_index[:, None, None]
        == jnp.arange(faces_total, dtype=jnp.int32).reshape(1, 4, elems),
        axis=0,
    )
    open_area = jnp.where(ruptured, 0.0, surface_measure_quotient)

    wide = (ROWS, LANES)
    (mp_h, mp_l, mi_h, mi_l, wt_h, wt_l, wf_h, wf_l, ws_h, ws_l, wl, lin, vm) = pl.pallas_call(
        prepare_kernel,
        in_specs=whole(17),
        out_specs=whole(13),
        out_shape=[shaped((3, ROWS, ROWS), BF16)] * 4
        + [shaped((4,) + wide, BF16)] * 2
        + [shaped((8,) + wide, BF16)] * 2
        + [shaped((4,) + wide, BF16)] * 2
        + [shaped((4, LANES, LANES)), shaped((2, LANES, LANES)), shaped((LANES, LANES))],
        compiler_params=LIMIT,
        name="prepare",
    )(
        elastic_directional_derivs,
        predictor_derivatives,
        interior_gradient_tables,
        interior_restriction,
        surface_raise_tables,
        riemann_numerical_tables,
        boundary_polynomials_sampled,
        quadrature_gather_weights,
        cross,
        e, f, g, h, tile, side, linear, slip,
    )

    step = 512
    column = lambda rows: pl.BlockSpec((rows, step), lambda i: (0, i))
    fixed = lambda shape: pl.BlockSpec(shape, lambda i: (0,) * len(shape))
    square = fixed((3, ROWS, ROWS))
    integral, face_rows = pl.pallas_call(
        predictor_kernel,
        grid=(elems // step,),
        in_specs=[column(ROWS), column(3), square, square, fixed((4,) + wide), fixed((4,) + wide)],
        out_specs=[column(ROWS), pl.BlockSpec((4, step, LANES), lambda i: (0, i, 0))],
        out_shape=[shaped((ROWS, elems)), shaped((4, elems, LANES))],
        scratch_shapes=[pltpu.VMEM((256, step), F32)],
        compiler_params=LIMIT,
        name="predictor",
    )(modal_unknowns, timestep_metric_scaling, mp_h, mp_l, wt_h, wt_l)
    face_rows = face_rows.reshape(faces_total, LANES)

    group_out, lower_out, upper_out = pl.pallas_call(
        send_kernel,
        in_specs=whole(2, (0,)),
        out_specs=whole(3),
        out_shape=[shaped((2048, LANES)), shaped((512, LANES)), shaped((512, LANES))],
        compiler_params=LIMIT,
        name="halo_rows",
    )(outbound_ghost_indices, face_rows)
    group = lax.all_to_all(group_out, "narrow", split_axis=0, concat_axis=0, tiled=True)
    lower = shift(lower_out, "wide", 1)
    upper = shift(upper_out, "wide", -1)

    width = 1024
    block = pl.BlockSpec((64, width), lambda i: (0, i))
    depth = jnp.arange(64).astype(F32) / 8.0
    curve = jnp.exp(-depth * depth)[:, None]
    new_temperature, new_pressure, top = pl.pallas_call(
        thermal_kernel,
        grid=(points // width,),
        in_specs=[
            block, block, pl.BlockSpec((1, width), lambda i: (0, i)),
            fixed((64, 1)), fixed((64, 64)), fixed((64, 64)),
        ],
        out_specs=[block, block, pl.BlockSpec((width // LANES, LANES), lambda i: (i, 0))],
        out_shape=[shaped((64, points)), shaped((64, points)), shaped((points // LANES, LANES))],
        compiler_params=LIMIT,
        name="thermal",
    )(
        thermal_field, fluid_load, earlier_sliding_speed.reshape(1, points), curve,
        thermal_diffusion_resolvent, hydraulic_diffusion_resolvent,
    )

    partial = pl.pallas_call(
        volume_kernel,
        grid=(elems // step,),
        in_specs=[column(ROWS), column(3), column(ROWS), square, square],
        out_specs=column(ROWS),
        out_shape=shaped((ROWS, elems)),
        compiler_params=LIMIT,
        name="volume",
    )(modal_unknowns, timestep_metric_scaling, integral, mi_h, mi_l)

    extent = faces_total + 3072
    payload = pl.pallas_call(
        payload_kernel,
        in_specs=whole(6, (0, 1)),
        out_specs=whole(1)[0],
        out_shape=shaped((devices * 8, LANES)),
        scratch_shapes=[pltpu.VMEM((extent + 8, LANES), F32)],
        compiler_params=LIMIT,
        name="payload",
    )(slot, boundary_entry_index, face_rows, group, lower, upper)
    arrived = lax.all_to_all(payload, ("wide", "narrow"), split_axis=0, concat_axis=0, tiled=True)

    base = pl.pallas_call(
        outside_kernel,
        in_specs=whole(9, (0,)),
        out_specs=whole(1)[0],
        out_shape=shaped((ROWS, elems)),
        scratch_shapes=[pltpu.VMEM((extent, LANES), F32), pltpu.VMEM((elems, LANES), F32)],
        compiler_params=LIMIT,
        name="outside",
    )(boundary_entry_index, face_rows, group, lower, upper, partial, open_area, wf_h, wf_l)

    flat = lambda x: x.reshape(points // LANES, LANES)
    imposed, rate = pl.pallas_call(
        fault_kernel,
        in_specs=whole(9),
        out_specs=whole(2),
        out_shape=[shaped((devices * 4, LANES)), shaped((points // LANES, LANES))],
        compiler_params=LIMIT,
        name="fault",
    )(
        arrived, top, flat(earlier_sliding_speed), flat(instant_sensitivity_a),
        flat(aging_memory_theta), wl, lin, vm, pair,
    )
    returned = lax.all_to_all(imposed, ("wide", "narrow"), split_axis=0, concat_axis=0, tiled=True)

    advanced = pl.pallas_call(
        finish_kernel,
        in_specs=whole(6, (0,)),
        out_specs=whole(1)[0],
        out_shape=shaped((ROWS, elems)),
        scratch_shapes=[pltpu.VMEM((faces_total + 8, LANES), F32)],
        compiler_params=LIMIT,
        name="finish",
    )(slot, returned, base, surface_measure_quotient, ws_h, ws_l)
    return advanced, new_temperature, new_pressure, rate.reshape(points)


def solution(mesh):
    split = P(None, ("wide", "narrow"))
    flat = P(("wide", "narrow"))
    return jax.shard_map(
        per_device,
        mesh=mesh,
        in_specs=(split,) * 3 + (P(),) * 10 + (split,) * 2 + (flat,) * 3 + (split,) * 2 + (flat,) * 2,
        out_specs=(split, split, split, flat),
        check_vma=False,
    )
```

profile of v0, /device:TPU:1, one launch (start us, length us, event | category | flops | bytes accessed | tf_op | source)
XLA Modules:
  0.0 148.8 jit_solution(367880768152422425)
XLA Ops:
  0.6 1.4 copy.57.sr
  2.1 1.3 copy.56.rs
  3.4 1.3 copy.55.a
  4.8 1.3 copy.58.rt
  6.1 1.5 %fusion.1.cc = f32[10,10]{1,0:T(8,128)} fusion(f32[16,10]{1,0:T(8,128)} %bp.1, f32[16,10]{1,0:T(8,128)} %qg.1), kind=kOutput, calls=%fused_computation.11 | convolution fusion | flops 19200 | bytes 1680 | tf_op jit(solution)/shard_map/dot_general | solution.py:321
  7.6 8.8 %prepare.1 = (bf16[3,180,180]{2,1,0:T(8,128)(2,1)}, bf16[3,180,180]{2,1,0:T(8,128)(2,1)}, bf16[3,180,180]{2,1,0:T(8,128)(2,1)}, bf16[3,180,180]{2,1,0:T(8,128)(2...) custom-call(f32[3,9,9]{2,1,0:T(8,128)} %copy.55.a, ...), custom_call_target="tpu_custom_call" | custom-call | tf_op jit(solution)/shard_map/prepare/pallas_call | solution.py:339
  16.3 13.9 %predictor.1 = (f32[180,2048]{1,0:T(8,128)}, f32[4,2048,128]{2,1,0:T(8,128)}) custom-call(f32[180,2048]{1,0:T(8,128)} %u.3, f32[3,2048]{1,0:T(4,128)} %t.3, bf16[3,180,180]{2,1,0:T(8,128)(2,1)} %get-tuple-element.27.mp_h, bf16[3,180,180]{2,1,0:T(8,128)(2,1)} %get-tuple-element.28.mp_l, bf16[4,180,128]{2,1,0:T(8,128)(2,1)} %get-tuple-element.29.wt_h, ...), custom_call_target="tpu_custom_call" | custom-call | tf_op jit(solution)/shard_map/predictor/pallas_call | solution.py:367
  30.2 10.7 %halo_rows.1 = (f32[2048,128]{1,0:T(8,128)}, f32[512,128]{1,0:T(8,128)}, f32[512,128]{1,0:T(8,128)}) custom-call(s32[6,512]{1,0:T(8,128)} %index.1, f32[8192,128]{1,0:T(8,128)} %bitcast.14), custom_call_target="tpu_custom_call" | custom-call | tf_op jit(solution)/shard_map/halo_rows/pallas_call | solution.py:379
  40.9 0.0 copy-start.7
  40.9 0.0 copy-start.6
  40.9 4.7 %collective-permute-start = (f32[512,128]{1,0:T(8,128)}, f32[512,128]{1,0:T(8,128)S(1)}, u32[]{:S(2)}, u32[]{:S(2)}) collective-permute-start(f32[512,128]{1,0:T(8,128)} %get-tuple-element.33), channel_id=1, source_target_pairs={{0,4},{4,8},{8,12},{12,16},{16,20},{20,24},{24,28},{28,32},{32,36}... | collective-permute-start | bytes 786440 | tf_op jit(solution)/shard_map/ppermute | solution.py:289
  45.7 1.9 %collective-permute-start.1 = (f32[512,128]{1,0:T(8,128)}, f32[512,128]{1,0:T(8,128)S(1)}, u32[]{:S(2)}, u32[]{:S(2)}) collective-permute-start(f32[512,128]{1,0:T(8,128)} %get-tuple-element.34), channel_id=1, source_target_pairs={{4,0},{8,4},{12,8},{16,12},{20,16},{24,20},{28,24},{32,28},{36,32}... | collective-permute-start | bytes 786440 | tf_op jit(solution)/shard_map/ppermute | solution.py:289
  47.6 4.0 %all-to-all-start = ((f32[4,512,128]{2,1,0:T(8,128)}), f32[4,512,128]{2,1,0:T(8,128)S(1)}, u32[]{:S(2)}, u32[]{:S(2)}) async-start(f32[4,512,128]{2,1,0:T(8,128)} %bitcast.22), calls=%async_computation | async-start | bytes 2097152 | tf_op jit(solution)/shard_map/all_to_all | solution.py:387
  51.6 0.0 copy-done.7
  51.6 0.1 reshape.101
  51.7 0.1 slice_reduce_fusion
  51.8 0.0 copy-done.6
  51.9 0.1 add.23
  52.0 0.1 copy.53
  52.0 0.1 copy.59
  52.2 0.6 fusion.shape
  52.8 0.1 select_reduce_fusion
  52.9 0.1 copy.54
  53.0 5.3 %volume.1.partial = f32[180,2048]{1,0:T(8,128)} custom-call(f32[180,2048]{1,0:T(8,128)} %u.3, f32[3,2048]{1,0:T(4,128)} %t.3, f32[180,2048]{1,0:T(8,128)} %get-tuple-element.40.integral, bf16[3,180,180]{2,1,0:T(8,128)(2,1)} %get-tuple-element.41.mi_h, bf16[3,180,180]{2,1,0:T(8,128)(2,1)} %get-tuple-element.42.mi_l), custom_call_target="tpu_custom_call" | custom-call | tf_op jit(solution)/shard_map/volume/pallas_call | solution.py:411
  58.4 8.1 %thermal.1 = (f32[64,8192]{1,0:T(8,128)}, f32[64,8192]{1,0:T(8,128)}, f32[64,128]{1,0:T(8,128)}) custom-call(f32[64,8192]{1,0:T(8,128)} %th.1, f32[64,8192]{1,0:T(8,128)} %fl.1, f32[1,8192]{1,0:T(1,128)} %bitcast.24, f32[64,1]{1,0:T(8,128)} %fusion.shape, f32[64,64]{1,0:T(8,128)} %tr.1, f32[64,64]{1,0:T(8,128)} %hr.1), custom_call_target="tpu_custom_call" | custom-call | tf_op jit(solution)/shard_map/thermal/pallas_call | solution.py:395
  66.5 0.6 broadcast_add_fusion.slot
  67.1 0.0 collective-permute-done.lower
  67.1 0.0 copy-start.3
  67.2 0.0 collective-permute-done.1.upper
  67.2 0.0 copy-start.4
  67.2 0.0 all-to-all-done
  67.2 0.0 copy-start
  67.2 0.7 copy-done.3
  67.9 0.1 copy-done.4
  68.0 0.3 copy-done
  68.3 8.1 %payload.1 = f32[1024,128]{1,0:T(8,128)} custom-call(s32[128,4]{1,0:T(8,128)} %broadcast_add_fusion.slot, s32[4,2048]{1,0:T(4,128)} %entry.3, f32[8192,128]{1,0:T(8,128)} %bitcast.15, f32[2048,128]{1,0:T(8,128)} %bitcast.17, f32[512,128]{1,0:T(8,128)} %copy-done.3, f32[512,128]{1,0:T(8,128)} %copy-done.4), custom_call_target="tpu_custom_call" | custom-call | tf_op jit(solution)/shard_map/payload/pallas_call | solution.py:422
  76.4 0.0 copy-start.5
  76.4 11.3 %all-to-all-start.1 = ((f32[128,8,128]{2,1,0:T(8,128)}), f32[128,8,128]{2,1,0:T(8,128)S(1)}, u32[]{:S(2)}, u32[]{:S(2)}) async-start(f32[128,8,128]{2,1,0:T(8,128)} %bitcast.19), calls=%async_computation.1 | async-start | bytes 1048576 | tf_op jit(solution)/shard_map/all_to_all | solution.py:431
  87.7 2.3 %compare_reduce_fusion = pred[4,2048]{1,0:T(4,128)(4,1)S(1)} fusion(s32[4,2048]{1,0:T(4,128)S(1)} %multiply_add_fusion, s32[512]{0:T(512)S(1)} %copy-done.6), kind=kLoop, calls=%fused_computation | loop fusion | flops 8380416 | bytes 43008 | tf_op jit(solution)/shard_map/reduce_or | solution.py:331
  90.0 11.7 %all-to-all-done.1 = f32[128,8,128]{2,1,0:T(8,128)S(1)} async-done(((f32[128,8,128]{2,1,0:T(8,128)}), f32[128,8,128]{2,1,0:T(8,128)S(1)}, u32[]{:S(2)}, u32[]{:S(2)}) %all-to-all-start.1) | async-done | bytes 524320 | tf_op jit(solution)/shard_map/all_to_all | solution.py:431
  101.7 0.0 copy-start.1
  101.7 0.8 copy-done.1
  102.4 4.2 %fault.1 = (f32[512,128]{1,0:T(8,128)}, f32[64,128]{1,0:T(8,128)}) custom-call(f32[1024,128]{1,0:T(8,128)} %bitcast.20, f32[64,128]{1,0:T(8,128)} %get-tuple-element.35.top, f32[64,128]{1,0:T(8,128)} %bitcast.25, f32[64,128]{1,0:T(8,128)} %bitcast.26, f32[64,128]{1,0:T(8,128)} %bitcast.27, f32[4,128,128]{2,1,0:T(8,128)} %get-tuple-element.36.wl, ...), custom_call_target="tpu_custom_call" | custom-call | tf_op jit(solution)/shard_map/fault/pallas_call | solution.py:444
  106.7 3.7 %all-to-all-start.2 = ((f32[128,4,128]{2,1,0:T(4,128)}), f32[128,4,128]{2,1,0:T(4,128)S(1)}, u32[]{:S(2)}, u32[]{:S(2)}) async-start(f32[128,4,128]{2,1,0:T(4,128)} %bitcast.23), calls=%async_computation.2 | async-start | bytes 524288 | tf_op jit(solution)/shard_map/all_to_all | solution.py:455
  110.4 0.0 copy-done.5
  110.4 0.6 broadcast_select_fusion.area
  111.1 29.5 %outside.1.base = f32[180,2048]{1,0:T(8,128)} custom-call(s32[4,2048]{1,0:T(4,128)} %entry.3, f32[8192,128]{1,0:T(8,128)} %bitcast.16, f32[2048,128]{1,0:T(8,128)} %bitcast.18, f32[512,128]{1,0:T(8,128)} %copy-done.3, f32[512,128]{1,0:T(8,128)} %copy-done.4, f32[180,2048]{1,0:T(8,128)} %volume.1.partial, f32[4,2048]{1,0:T(4,128)} %broadcast_select_fusion.area, ...), custom_call_target="tpu_custom_call" | custom-call | tf_op jit(solution)/shard_map/outside/pallas_call | solution.py:433
  140.6 0.0 all-to-all-done.2
  140.6 0.0 copy-start.2
  140.6 0.7 copy-done.2
  141.3 7.5 %finish.1 = f32[180,2048]{1,0:T(8,128)} custom-call(s32[128,4]{1,0:T(8,128)} %broadcast_add_fusion.slot, f32[512,128]{1,0:T(8,128)} %bitcast.21, f32[180,2048]{1,0:T(8,128)} %outside.1.base, f32[4,2048]{1,0:T(4,128)} %area.1, bf16[4,180,128]{2,1,0:T(8,128)(2,1)} %get-tuple-element.45.ws_h, bf16[4,180,128]{2,1,0:T(8,128)(2,1)} %get-tuple-element.46.ws_l), custom_call_target="tpu_custom_call" | custom-call | tf_op jit(solution)/shard_map/finish/pallas_call | solution.py:457
  (4 shorter events, 0.1 us)
Async XLA Ops:
  40.9 10.7 %copy-start.7 = (s32[512]{0:T(512)S(1)}, s32[512]{0:T(512)}, u32[]{:S(2)}) copy-start(s32[512]{0:T(512)} %param.52) | copy-start | bytes 6148
  40.9 10.9 %copy-start.6 = (s32[512]{0:T(512)S(1)}, s32[512]{0:T(512)}, u32[]{:S(2)}) copy-start(s32[512]{0:T(512)} %param.51) | copy-start | bytes 6148
  40.9 26.2 %collective-permute-start = (f32[512,128]{1,0:T(8,128)}, f32[512,128]{1,0:T(8,128)S(1)}, u32[]{:S(2)}, u32[]{:S(2)}) collective-permute-start(f32[512,128]{1,0:T(8,128)} %get-tuple-element.33), channel_id=1, source_target_pairs={{0,4},{4,8},{8,12},{12,16},{16,20},{20,24},{24,28},{28,32},{32,36}... | collective-permute-start | bytes 786440 | tf_op jit(solution)/shard_map/ppermute | solution.py:289
  45.7 21.5 %collective-permute-start.1 = (f32[512,128]{1,0:T(8,128)}, f32[512,128]{1,0:T(8,128)S(1)}, u32[]{:S(2)}, u32[]{:S(2)}) collective-permute-start(f32[512,128]{1,0:T(8,128)} %get-tuple-element.34), channel_id=1, source_target_pairs={{4,0},{8,4},{12,8},{16,12},{20,16},{24,20},{28,24},{32,28},{36,32}... | collective-permute-start | bytes 786440 | tf_op jit(solution)/shard_map/ppermute | solution.py:289
  47.6 19.6 %all-to-all-start = ((f32[4,512,128]{2,1,0:T(8,128)}), f32[4,512,128]{2,1,0:T(8,128)S(1)}, u32[]{:S(2)}, u32[]{:S(2)}) async-start(f32[4,512,128]{2,1,0:T(8,128)} %bitcast.22), calls=%async_computation | async-start | bytes 2097152 | tf_op jit(solution)/shard_map/all_to_all | solution.py:387
  67.1 0.7 copy-start.3
  67.2 0.8 copy-start.4
  67.2 1.1 copy-start
  76.4 34.1 %copy-start.5 = (f32[4,2048]{1,0:T(4,128)S(1)}, f32[4,2048]{1,0:T(4,128)}, u32[]{:S(2)}) copy-start(f32[4,2048]{1,0:T(4,128)} %area.1) | copy-start | bytes 98308
  76.4 25.3 %all-to-all-start.1 = ((f32[128,8,128]{2,1,0:T(8,128)}), f32[128,8,128]{2,1,0:T(8,128)S(1)}, u32[]{:S(2)}, u32[]{:S(2)}) async-start(f32[128,8,128]{2,1,0:T(8,128)} %bitcast.19), calls=%async_computation.1 | async-start | bytes 1048576 | tf_op jit(solution)/shard_map/all_to_all | solution.py:431
  101.7 0.8 copy-start.1
  106.7 33.9 %all-to-all-start.2 = ((f32[128,4,128]{2,1,0:T(4,128)}), f32[128,4,128]{2,1,0:T(4,128)S(1)}, u32[]{:S(2)}, u32[]{:S(2)}) async-start(f32[128,4,128]{2,1,0:T(4,128)} %bitcast.23), calls=%async_computation.2 | async-start | bytes 524288 | tf_op jit(solution)/shard_map/all_to_all | solution.py:455
  140.6 0.7 copy-start.2
where the time goes:
time: 150 us; the launch traced here: 149 us
  Pallas kernels  96.1 us (64%)
  starting transfers between devices  25.7 us (17%)
  waiting for transfers between devices  11.7 us (8%)
  local copies, waits for them, and re-layouts  8.62 us (6%)
  other arithmetic  4.35 us (3%)
  matrix products  1.52 us (1%)
    pallas_call x1, Pallas kernels, per_device(): pl.pallas_call(outside_kernel, in_specs=whole(9, (0,)), out_specs=whole(1...  29.5 us
    pallas_call x1, Pallas kernels, per_device(): pl.pallas_call(predictor_kernel, grid=(elems // step,), in_specs=[column(...  13.9 us
    all_to_all x1, waiting for transfers between devices, per_device(): lax.all_to_all(payload, ('wide', 'narrow'), split_axis=0, concat_axis=0,...  11.7 us
    all_to_all x1, starting transfers between devices, per_device(): lax.all_to_all(payload, ('wide', 'narrow'), split_axis=0, concat_axis=0,...  11.3 us
    pallas_call x1, Pallas kernels, per_device(): pl.pallas_call(send_kernel, in_specs=whole(2, (0,)), out_specs=whole(3),...  10.7 us
    pallas_call x1, Pallas kernels, per_device(): pl.pallas_call(prepare_kernel, in_specs=whole(17), out_specs=whole(13), o...  8.76 us
    pallas_call x1, Pallas kernels, per_device(): pl.pallas_call(thermal_kernel, grid=(points // width,), in_specs=[block,...  8.11 us
    pallas_call x1, Pallas kernels, per_device(): pl.pallas_call(payload_kernel, in_specs=whole(6, (0, 1)), out_specs=whole...  8.06 us
  transfers between devices with their start and end apart: 5, of which 1 were waited for; matrix products, arithmetic and copies ran while one was open for 3% of the time, Pallas kernels for 29%

commit v1 on v0

v1 whole, which is shorter than its diff:
```python
import jax
import jax.numpy as jnp
import numpy as np
from jax import lax
from jax.experimental import pallas as pl
from jax.experimental.pallas import tpu as pltpu
from jax.sharding import PartitionSpec as P

NEWTON = 4
Q, NB, NJ, NG = 9, 20, 10, 16
LANES = 128
ROWS = Q * NB
PAD = 192
HIGHEST = lax.Precision.HIGHEST
F32 = jnp.float32
BF16 = jnp.bfloat16
VMEM = pltpu.MemorySpace.VMEM
SMEM = pltpu.MemorySpace.SMEM
LIMIT = pltpu.CompilerParams(vmem_limit_bytes=56 * 1024 * 1024)


def tables():
    e = np.zeros((ROWS, Q), np.float32)
    f = np.zeros((ROWS, NB), np.float32)
    for q in range(Q):
        for b in range(NB):
            e[q * NB + b, q] = 1
            f[q * NB + b, b] = 1
    g = np.zeros((LANES, Q), np.float32)
    h = np.zeros((LANES, NJ), np.float32)
    for q in range(Q):
        for j in range(NJ):
            g[q * NJ + j, q] = 1
            h[q * NJ + j, j] = 1
    tile = np.zeros((LANES, NG), np.float32)
    for lane in range(LANES):
        tile[lane, lane % NG] = 1
    side = np.zeros((LANES, 4), np.float32)
    for q, column, low, high in ((3, 0, 0.5, 0.5), (6, 0, -0.5, 0.5), (0, 1, 0.5, 0.5), (7, 1, -0.5, 0.5)):
        side[q * NJ : (q + 1) * NJ, column] = low
        side[q * NJ : (q + 1) * NJ, 2 + column] = high
    mid = np.zeros((2, Q, Q), np.float32)
    mid[:] = 0.5 * np.eye(Q)
    mid[0, 6, 3] = -0.5
    mid[1, 6, 3] = 0.5
    linear = np.stack([g @ mid[0] @ g.T, g @ mid[1] @ g.T])
    slip = np.zeros((1, LANES), np.float32)
    slip[0, 3 * NJ : 4 * NJ] = -1.0
    slip[0, 6 * NJ : 7 * NJ] = 0.5
    pair = np.zeros((64, LANES), np.float32)
    for s in range(LANES):
        pair[s // 2, s] = 1
    return e, f, g, h, tile, side, linear, slip, pair


def dot(a, b, ca=1, cb=0, precision=HIGHEST):
    return lax.dot_general(
        a, b, (((ca,), (cb,)), ((), ())), precision=precision, preferred_element_type=F32
    )


def halves(x):
    high = x.astype(BF16)
    return high, (x - high.astype(F32)).astype(BF16)


def single(a, b, cb=0):
    return lax.dot_general(a, b, (((1,), (cb,)), ((), ())), preferred_element_type=F32)


def put(out, at, value, half):
    high, low = halves(value)
    rows, lanes = value.shape
    out[at[0] + (slice(at[1], at[1] + rows), slice(at[2], at[2] + lanes))] = high
    out[at[0] + (slice(half + at[1], half + at[1] + rows), slice(at[2], at[2] + lanes))] = low


def stacked(weights, x, cb=0):
    xh, xl = halves(x)
    half = weights.shape[0] // 2
    both = single(weights, xh, cb)
    return both[0:half] + (both[half:] + single(weights[0:half], xl, cb))


def prepare_kernel(a, pd, rs, e, f, g, h, mp, wt):
    e_, f_, g_, h_ = e[...], f[...], g[...], h[...]
    mp[...] = jnp.zeros(mp.shape, BF16)
    for d in range(3):
        left = dot(dot(e_, a[:, d, :]), e_, 1, 1)
        put(mp, ((), d * PAD, 0), -left * dot(dot(f_, pd[d]), f_, 1, 1), 3 * PAD)
    same = dot(e_, g_, 1, 1)
    for face in range(4):
        high, low = halves(same * dot(dot(f_, rs[:, face, :], 1, 1), h_, 1, 1))
        wt[0, :, face * LANES : (face + 1) * LANES] = high
        wt[1, :, face * LANES : (face + 1) * LANES] = low


def prepare_rest_kernel(
    a, kd, sr, rt, bp, qg, e, f, g, h, tile, side, linear, slip, mi, wf, ws, wm, wp, vm
):
    e_, f_, g_, h_ = e[...], f[...], g[...], h[...]
    mi[...] = jnp.zeros(mi.shape, BF16)
    wf[...] = jnp.zeros(wf.shape, BF16)
    ws[...] = jnp.zeros(ws.shape, BF16)
    for d in range(3):
        left = dot(dot(e_, a[:, d, :]), e_, 1, 1)
        put(mi, ((), d * PAD, 0), left * dot(dot(f_, kd[d]), f_, 1, 1), 3 * PAD)
    r0 = dot(dot(e_, rt[:, 0, :]), g_, 1, 1)
    r1 = dot(dot(e_, rt[:, 1, :]), g_, 1, 1)
    for face in range(4):
        lift = dot(dot(f_, sr[:, face, :], 1, 1), h_, 1, 1)
        put(wf, ((face,), 0, 0), r0 * lift, PAD)
        put(wf, ((face,), 0, LANES), r1 * lift, PAD)
        put(ws, ((face,), 0, 0), (r0 + r1) * lift, PAD)
    hb = dot(dot(h_, bp[...], 1, 1), tile[...], 1, 1)
    hch = dot(dot(h_, dot(bp[...], qg[...], 0, 0)), h_, 1, 1)
    for out, at in ((wm, 0), (wp, 1)):
        out[:, 0:LANES] = hb * side[:, 2 * at : 2 * at + 1]
        out[:, LANES : 2 * LANES] = hb * side[:, 2 * at + 1 : 2 * at + 2]
        out[:, 2 * LANES :] = hch * linear[at]
    vm[...] = dot(dot(tile[...], qg[...]), h_, 1, 1) * slip[...]


def directional(weights, x, times):
    y = stacked(weights, x)
    return (
        y[0:ROWS] * times[0:1]
        + y[PAD : PAD + ROWS] * times[1:2]
        + y[2 * PAD : 2 * PAD + ROWS] * times[2:3]
    )


def predictor_kernel(u, t, mp, wt, integral, faces, padded):
    times = t[...]
    current = u[...]
    total = current
    factor = 1.0
    for degree in range(1, 4):
        current = directional(mp[...], current, times)
        factor = factor * (degree + 1)
        total = total + current * (1.0 / factor)
    integral[...] = total
    padded[...] = jnp.zeros(padded.shape, F32)
    padded[0:ROWS, :] = total
    xh, xl = halves(padded[...].T[:, 0:ROWS])
    rows = single(xh, wt[0]) + (single(xh, wt[1]) + single(xl, wt[0]))
    for face in range(4):
        faces[face] = rows[:, face * LANES : (face + 1) * LANES]


def volume_kernel(u, t, integral, mi, partial):
    partial[...] = u[...] + directional(mi[...], integral[...], t[...])


def take_rows(index, start, count, source, target, base):
    def body(i, carry):
        first = i * 16
        rows = [source[pl.ds(index[start + first + k], 1), :] for k in range(16)]
        for k in range(16):
            target[pl.ds(base + first + k, 1), :] = rows[k]
        return carry

    lax.fori_loop(0, count // 16, body, 0)


def send_kernel(index, faces, group, lower, upper):
    take_rows(index, 0, 2048, faces, group, 0)
    take_rows(index, 2048, 512, faces, lower, 0)
    take_rows(index, 2560, 512, faces, upper, 0)


def thermal_kernel(th, fl, speed, shape, tr, hr, new_th, new_fl, top):
    v = speed[...]
    old = th[...]
    warmed = old + shape[...] * (0.5 * v * v)
    fresh = stacked(jnp.concatenate(halves(tr[...]), axis=0), warmed)
    new_th[...] = fresh
    pressure = stacked(jnp.concatenate(halves(hr[...]), axis=0), fl[...] + 0.5 * (fresh - old))
    new_fl[...] = pressure
    for r in range(top.shape[0]):
        top[r : r + 1, :] = pressure[0:1, r * LANES : (r + 1) * LANES]


def fill(table, parts, sems):
    at = 0
    copies = []
    for i, part in enumerate(parts):
        rows = part.shape[0]
        copies.append(pltpu.make_async_copy(part, table.at[pl.ds(at, rows)], sems.at[i]))
        at += rows
    for copy in copies:
        copy.start()
    for copy in copies:
        copy.wait()


def live_blocks(seat):
    return lax.fori_loop(
        0, seat.shape[0] // 4, lambda i, c: c + (seat[i * 4] >= 0).astype(jnp.int32), 0
    )


def payload_kernel(face, seat, entry, faces, group, lower, upper, payload, table, sems):
    extent = table.shape[0] - 8
    payload[...] = jnp.zeros(payload.shape, F32)
    table[extent : extent + 8, :] = jnp.zeros((8, LANES), F32)
    blocks = live_blocks(seat)
    fill(table, (faces, group, lower, upper), sems)

    def body(i, carry):
        owner = seat[i * 4]
        rows = []
        for k in range(4):
            column = face[i * 4 + k]
            live = column >= 0
            rows.append(table[pl.ds(jnp.where(live, column, extent), 1), :])
            outer = jnp.where(live, entry[jnp.maximum(column, 0)], extent)
            rows.append(table[pl.ds(outer, 1), :])
        for k in range(4):
            payload[pl.ds(owner * 8 + k, 1), :] = rows[2 * k]
            payload[pl.ds(owner * 8 + 4 + k, 1), :] = rows[2 * k + 1]
        return carry

    lax.fori_loop(0, blocks, body, 0)


def outside_kernel(first, entry, faces, group, lower, upper, partial, area, wf, base, table, outside, sems):
    fill(table, (faces, group, lower, upper), sems)
    elems = faces.shape[0] // 4
    result = partial[...]
    for face in (first, first + 1):
        take_rows(entry, face * elems, elems, table, outside, 0)
        rows = jnp.concatenate([table[face * elems : (face + 1) * elems, :], outside[...]], axis=1)
        flux = stacked(wf[face], rows, 1)
        result = result - flux[0:ROWS] * area[face : face + 1, :]
    base[...] = result


def fault_kernel(arrived, top, speed, sense, memory, wm, wp, vm, pair, imposed, rate):
    lanes = lax.shift_right_logical(lax.broadcasted_iota(jnp.int32, (LANES, LANES), 1), 4)
    half = (lax.broadcasted_iota(jnp.int32, (LANES, LANES), 0) & 1) * 4
    pick = lambda at: jnp.concatenate(
        [arrived[pl.ds(at + k, LANES, stride=8), :] for k in range(4)], axis=0
    )
    linear = dot(pick(0), wm[...]) + dot(pick(4), wp[...])
    locked = jnp.zeros((LANES, LANES), F32)
    normal = jnp.zeros((LANES, LANES), F32)
    for k in range(4):
        mine = lanes == half + k
        part = linear[k * LANES : (k + 1) * LANES]
        locked = locked + jnp.where(mine, part[:, 0:LANES], 0.0)
        normal = normal + jnp.where(mine, part[:, LANES : 2 * LANES], 0.0)
    locked = dot(pair[...], locked)
    normal = dot(pair[...], normal)
    excess = 2.0 + normal - top[...]
    effective = jnp.maximum(excess, 0.0) + jnp.log1p(jnp.exp(-jnp.abs(excess)))
    strength = effective * sense[...]
    weight = 0.5 * jnp.exp(memory[...] / sense[...])
    v = speed[...]
    for _ in range(NEWTON):
        scaled = weight * v
        root = jnp.sqrt(1.0 + scaled * scaled)
        size = jnp.log(jnp.abs(scaled) + root)
        mismatch = locked - v - strength * jnp.where(scaled < 0.0, -size, size)
        slope = -1.0 - strength * weight / root
        v = v - mismatch / slope
    rate[...] = v
    spread = dot(pair[...], v, 0, 0)
    mine = jnp.concatenate(
        [jnp.where(lanes == half + k, spread, 0.0) for k in range(4)], axis=0
    )
    result = linear[:, 2 * LANES :] + dot(mine, vm[...])
    for k in range(4):
        imposed[pl.ds(k, LANES, stride=4), :] = result[k * LANES : (k + 1) * LANES]


def finish_kernel(face, seat, returned, base, area, ws, out, spread, held, sems):
    copy = pltpu.make_async_copy(base, held, sems.at[0])
    copy.start()
    count = spread.shape[0] - 8
    elems = count // 4
    spread[...] = jnp.zeros(spread.shape, F32)

    def body(i, carry):
        owner = seat[i * 4]
        rows = [returned[pl.ds(owner * 4 + k, 1), :] for k in range(4)]
        for k in range(4):
            column = face[i * 4 + k]
            spread[pl.ds(jnp.where(column >= 0, column, count), 1), :] = rows[k]
        return carry

    lax.fori_loop(0, live_blocks(seat), body, 0)
    copy.wait()
    result = held[...]
    for at in range(4):
        flux = stacked(ws[at], spread[at * elems : (at + 1) * elems, :], 1)
        result = result - flux[0:ROWS] * area[at : at + 1, :]
    out[...] = result


def shaped(shape, dtype=F32):
    return jax.ShapeDtypeStruct(shape, dtype)


def whole(count, smem=(), left=()):
    space = lambda i: SMEM if i in smem else pl.ANY if i in left else VMEM
    return [pl.BlockSpec(memory_space=space(i)) for i in range(count)]


def shift(array, axis, by):
    peers = lax.axis_size(axis)
    pairs = [(i, i + by) for i in range(peers) if 0 <= i + by < peers]
    return lax.ppermute(array, axis, pairs)


def per_device(
    modal_unknowns,
    timestep_metric_scaling,
    surface_measure_quotient,
    elastic_directional_derivs,
    predictor_derivatives,
    interior_gradient_tables,
    interior_restriction,
    surface_raise_tables,
    riemann_numerical_tables,
    boundary_polynomials_sampled,
    quadrature_gather_weights,
    thermal_diffusion_resolvent,
    hydraulic_diffusion_resolvent,
    thermal_field,
    fluid_load,
    earlier_sliding_speed,
    instant_sensitivity_a,
    aging_memory_theta,
    outbound_ghost_indices,
    boundary_entry_index,
    rupture_side_index,
    rupture_seat_partition,
):
    elems = modal_unknowns.shape[1]
    faces_total = 4 * elems
    devices = lax.axis_size(("wide", "narrow"))
    points = thermal_field.shape[1]
    e, f, g, h, tile, side, linear, slip, pair = tables()
    ruptured = jnp.any(
        rupture_side_index[:, None, None]
        == jnp.arange(faces_total, dtype=jnp.int32).reshape(1, 4, elems),
        axis=0,
    )
    open_area = jnp.where(ruptured, 0.0, surface_measure_quotient)
    entry = boundary_entry_index.reshape(-1)
    elastic = jnp.transpose(elastic_directional_derivs, (1, 0, 2))

    mp, wt = pl.pallas_call(
        prepare_kernel,
        in_specs=whole(7),
        out_specs=whole(2),
        out_shape=[shaped((6 * PAD, ROWS), BF16), shaped((2, ROWS, 4 * LANES), BF16)],
        compiler_params=LIMIT,
        name="prepare",
    )(
        elastic, predictor_derivatives, jnp.transpose(interior_restriction, (1, 0, 2)), e, f, g, h
    )

    step = 512
    column = lambda rows: pl.BlockSpec((rows, step), lambda i: (0, i))
    fixed = lambda shape: pl.BlockSpec(shape, lambda i: (0,) * len(shape))
    integral, face_rows = pl.pallas_call(
        predictor_kernel,
        grid=(elems // step,),
        in_specs=[column(ROWS), column(3), fixed((6 * PAD, ROWS)), fixed((2, ROWS, 4 * LANES))],
        out_specs=[column(ROWS), pl.BlockSpec((4, step, LANES), lambda i: (0, i, 0))],
        out_shape=[shaped((ROWS, elems)), shaped((4, elems, LANES))],
        scratch_shapes=[pltpu.VMEM((256, step), F32)],
        compiler_params=LIMIT,
        name="predictor",
    )(modal_unknowns, timestep_metric_scaling, mp, wt)
    face_rows = face_rows.reshape(faces_total, LANES)

    group_out, lower_out, upper_out = pl.pallas_call(
        send_kernel,
        in_specs=whole(2, (0,)),
        out_specs=whole(3),
        out_shape=[shaped((2048, LANES)), shaped((512, LANES)), shaped((512, LANES))],
        compiler_params=LIMIT,
        name="halo_rows",
    )(outbound_ghost_indices.reshape(-1), face_rows)
    group = lax.all_to_all(group_out, "narrow", split_axis=0, concat_axis=0, tiled=True)
    lower = shift(lower_out, "wide", 1)
    upper = shift(upper_out, "wide", -1)

    tensors, sensitivity, _ = lax.optimization_barrier(
        (riemann_numerical_tables, thermal_diffusion_resolvent, lower_out)
    )
    mi, wf, ws, wm, wp, vm = pl.pallas_call(
        prepare_rest_kernel,
        in_specs=whole(14),
        out_specs=whole(6),
        out_shape=[
            shaped((6 * PAD, ROWS), BF16),
            shaped((4, 2 * PAD, 2 * LANES), BF16),
            shaped((4, 2 * PAD, LANES), BF16),
            shaped((LANES, 3 * LANES)),
            shaped((LANES, 3 * LANES)),
            shaped((LANES, LANES)),
        ],
        compiler_params=LIMIT,
        name="prepare_rest",
    )(
        elastic,
        interior_gradient_tables,
        jnp.transpose(surface_raise_tables, (2, 0, 1)),
        jnp.transpose(tensors, (1, 0, 2)),
        boundary_polynomials_sampled,
        quadrature_gather_weights,
        e, f, g, h, tile, side, linear, slip,
    )

    width = 2048
    block = pl.BlockSpec((64, width), lambda i: (0, i))
    depth = np.arange(64, dtype=np.float32) / 8.0
    curve = np.exp(-depth * depth)[:, None].astype(np.float32)
    new_temperature, new_pressure, top = pl.pallas_call(
        thermal_kernel,
        grid=(points // width,),
        in_specs=[
            block, block, pl.BlockSpec((1, width), lambda i: (0, i)),
            fixed((64, 1)), fixed((64, 64)), fixed((64, 64)),
        ],
        out_specs=[block, block, pl.BlockSpec((width // LANES, LANES), lambda i: (i, 0))],
        out_shape=[shaped((64, points)), shaped((64, points)), shaped((points // LANES, LANES))],
        compiler_params=LIMIT,
        name="thermal",
    )(
        thermal_field, fluid_load, earlier_sliding_speed.reshape(1, points), curve,
        sensitivity, hydraulic_diffusion_resolvent,
    )

    partial = pl.pallas_call(
        volume_kernel,
        grid=(elems // step,),
        in_specs=[column(ROWS), column(3), column(ROWS), fixed((6 * PAD, ROWS))],
        out_specs=column(ROWS),
        out_shape=shaped((ROWS, elems)),
        compiler_params=LIMIT,
        name="volume",
    )(modal_unknowns, timestep_metric_scaling, integral, mi)

    faults, partial, top = lax.optimization_barrier((rupture_side_index, partial, top))
    extent = faces_total + 3072
    payload = pl.pallas_call(
        payload_kernel,
        in_specs=whole(7, (0, 1, 2), (3, 4, 5, 6)),
        out_specs=whole(1)[0],
        out_shape=shaped((devices * 8, LANES)),
        scratch_shapes=[pltpu.VMEM((extent + 8, LANES), F32), pltpu.SemaphoreType.DMA((4,))],
        compiler_params=LIMIT,
        name="payload",
    )(faults, rupture_seat_partition, entry, face_rows, group, lower, upper)
    arrived = lax.all_to_all(payload, ("wide", "narrow"), split_axis=0, concat_axis=0, tiled=True)

    def half(first, value):
        return pl.pallas_call(
            lambda *refs: outside_kernel(first, *refs),
            in_specs=whole(8, (0,), (1, 2, 3, 4)),
            out_specs=whole(1)[0],
            out_shape=shaped((ROWS, elems)),
            scratch_shapes=[
                pltpu.VMEM((extent, LANES), F32),
                pltpu.VMEM((elems, LANES), F32),
                pltpu.SemaphoreType.DMA((4,)),
            ],
            compiler_params=LIMIT,
            name="outside" + str(first),
        )(entry, face_rows, group, lower, upper, value, open_area, wf)

    partial, payload = lax.optimization_barrier((partial, payload))
    base = half(0, partial)
    base, top = lax.optimization_barrier((base, top))
    flat = lambda x: x.reshape(points // LANES, LANES)
    imposed, rate = pl.pallas_call(
        fault_kernel,
        in_specs=whole(9),
        out_specs=whole(2),
        out_shape=[shaped((devices * 4, LANES)), shaped((points // LANES, LANES))],
        compiler_params=LIMIT,
        name="fault",
    )(
        arrived, top, flat(earlier_sliding_speed), flat(instant_sensitivity_a),
        flat(aging_memory_theta), wm, wp, vm, pair,
    )
    returned = lax.all_to_all(imposed, ("wide", "narrow"), split_axis=0, concat_axis=0, tiled=True)
    base, rate = lax.optimization_barrier((base, rate))
    base = half(2, base)

    advanced = pl.pallas_call(
        finish_kernel,
        in_specs=whole(6, (0, 1), (3,)),
        out_specs=whole(1)[0],
        out_shape=shaped((ROWS, elems)),
        scratch_shapes=[
            pltpu.VMEM((faces_total + 8, LANES), F32),
            pltpu.VMEM((ROWS, elems), F32),
            pltpu.SemaphoreType.DMA((1,)),
        ],
        compiler_params=LIMIT,
        name="finish",
    )(rupture_side_index, rupture_seat_partition, returned, base, surface_measure_quotient, ws)
    return advanced, new_temperature, new_pressure, rate.reshape(points)


def solution(mesh):
    split = P(None, ("wide", "narrow"))
    flat = P(("wide", "narrow"))
    return jax.shard_map(
        per_device,
        mesh=mesh,
        in_specs=(split,) * 3 + (P(),) * 10 + (split,) * 2 + (flat,) * 3 + (split,) * 2 + (flat,) * 2,
        out_specs=(split, split, split, flat),
        check_vma=False,
    )
```

time: 150 us -> 126 us (0.84)
  Pallas kernels: 96.1 us -> 82.7 us
  waiting for transfers between devices: 11.7 us -> 0.01 us
  starting transfers between devices: 25.7 us -> 33 us
  local copies, waits for them, and re-layouts: 8.62 us -> 4.56 us
  matrix products: 1.52 us -> 0 us
    all_to_all x1, waiting for transfers between devices: 11.7 us -> 0.01 us  [per_device(): lax.all_to_all(payload, ('wide', 'narrow'), split_axis=0, concat_axis=0,...]
    pallas_call x4 -> x6, Pallas kernels: 53.8 us -> 47.7 us  [the longest x2 23.3 us: half(): pl.pallas_call(lambda *refs: outside_kernel(first, *refs), in_specs=whole...]
    all_to_all x1, starting transfers between devices: 3.74 us -> 9.76 us  [per_device(): lax.all_to_all(imposed, ('wide', 'narrow'), split_axis=0, concat_axis=0,...]
    unnamed x20 -> x21, local copies, waits for them, and re-layouts: 8.04 us -> 3.24 us
    pallas_call x1, Pallas kernels: 10.7 us -> 6.66 us  [per_device(): pl.pallas_call(send_kernel, in_specs=whole(2, (0,)), out_specs=whole(3),...]
    pallas_call x1, Pallas kernels: 8.11 us -> 5.8 us  [per_device(): pl.pallas_call(thermal_kernel, grid=(points // width,), in_specs=[block,...]
    pallas_call x1, Pallas kernels: 13.9 us -> 12.2 us  [per_device(): pl.pallas_call(predictor_kernel, grid=(elems // step,), in_specs=[column(...]
    dot_general x1 -> x0, matrix products: 1.52 us -> none  [per_device(): lax.dot_general(boundary_polynomials_sampled, quadrature_gather_weights,...]
  transfers between devices with their start and end apart: 5 -> 5, of which waited for: 1 -> 0; matrix products, arithmetic and copies ran while one was open for 3% -> 3% of each run, Pallas kernels for 29% -> 33%
where the time goes in v1:
time: 126 us; the launch traced here: 124 us
  Pallas kernels  82.7 us (66%)
  starting transfers between devices  33 us (26%)
  local copies, waits for them, and re-layouts  4.56 us (4%)
  other arithmetic  2.9 us (2%)
    pallas_call x2, Pallas kernels, half(): pl.pallas_call(lambda *refs: outside_kernel(first, *refs), in_specs=whole...  23.3 us
    all_to_all x1, starting transfers between devices, per_device(): lax.all_to_all(payload, ('wide', 'narrow'), split_axis=0, concat_axis=0,...  12.3 us
    pallas_call x1, Pallas kernels, per_device(): pl.pallas_call(predictor_kernel, grid=(elems // step,), in_specs=[column(...  12.2 us
    all_to_all x1, starting transfers between devices, per_device(): lax.all_to_all(imposed, ('wide', 'narrow'), split_axis=0, concat_axis=0,...  9.76 us
    pallas_call x1, Pallas kernels, per_device(): pl.pallas_call(prepare_rest_kernel, in_specs=whole(14), out_specs=whole(6...  6.75 us
    pallas_call x1, Pallas kernels, per_device(): pl.pallas_call(send_kernel, in_specs=whole(2, (0,)), out_specs=whole(3),...  6.66 us
    pallas_call x1, Pallas kernels, per_device(): pl.pallas_call(finish_kernel, in_specs=whole(6, (0, 1), (3,)), out_specs=...  6.25 us
    ppermute x2, starting transfers between devices, shift(): return lax.ppermute(array, axis, pairs)  5.96 us
  transfers between devices with their start and end apart: 5, of which 0 were waited for; matrix products, arithmetic and copies ran while one was open for 3% of the time, Pallas kernels for 33%

profile of v1, /device:TPU:1, one launch (start us, length us, event | category | flops | bytes accessed | tf_op | source)
XLA Modules:
  0.0 124.1 jit_solution(10506977737000458697)
XLA Ops:
  0.6 1.3 %reshape.56.index = s32[3072]{0:T(1024)} reshape(s32[6,512]{1,0:T(8,128)} %param.50) | data formatting | bytes 24576 | tf_op jit(solution)/shard_map/reshape | solution.py:387
  1.9 5.5 %prepare.1 = (bf16[1152,180]{1,0:T(8,128)(2,1)}, bf16[2,180,512]{2,1,0:T(8,128)(2,1)}) custom-call(f32[9,3,9]{2,1,0:T(4,128)} %bitcast.35, f32[3,20,20]{2,1,0:T(8,128)} %pd.1, f32[10,4,20]{2,1,0:T(4,128)} %bitcast.40, f32[180,9]{1,0:T(8,128)} %constant.26.clone.e, f32[180,20]{1,0:T(8,128)} %constant.27.clone.f, f32[128,9]{1,0:T(8,128)} %constant.28.clone.g, ...), custom_call_target="tpu_custom_call" | custom-call | tf_op jit(solution)/shard_map/prepare/pallas_call | solution.py:354
  7.4 12.2 %predictor.1 = (f32[180,2048]{1,0:T(8,128)}, f32[4,2048,128]{2,1,0:T(8,128)}) custom-call(f32[180,2048]{1,0:T(8,128)} %u.3, f32[3,2048]{1,0:T(4,128)} %t.3, bf16[1152,180]{1,0:T(8,128)(2,1)} %get-tuple-element.32.mp, bf16[2,180,512]{2,1,0:T(8,128)(2,1)} %get-tuple-element.33.wt), custom_call_target="tpu_custom_call" | custom-call | tf_op jit(solution)/shard_map/predictor/pallas_call | solution.py:368
  19.7 6.7 %halo_rows.1 = (f32[2048,128]{1,0:T(8,128)}, f32[512,128]{1,0:T(8,128)}, f32[512,128]{1,0:T(8,128)}) custom-call(s32[3072]{0:T(1024)} %reshape.56.index, f32[8192,128]{1,0:T(8,128)} %bitcast.18), custom_call_target="tpu_custom_call" | custom-call | tf_op jit(solution)/shard_map/halo_rows/pallas_call | solution.py:380
  26.3 0.0 copy-start.9
  26.3 0.0 copy-start.8
  26.3 0.0 copy-start.6
  26.3 5.0 %all-to-all-start = ((f32[4,512,128]{2,1,0:T(8,128)}), f32[4,512,128]{2,1,0:T(8,128)S(1)}, u32[]{:S(2)}, u32[]{:S(2)}) async-start(f32[4,512,128]{2,1,0:T(8,128)} %bitcast.28), calls=%async_computation | async-start | bytes 2097152 | tf_op jit(solution)/shard_map/all_to_all | solution.py:388
  31.3 0.0 copy-done.9
  31.3 2.9 %collective-permute-start.1 = (f32[512,128]{1,0:T(8,128)S(1)}, f32[512,128]{1,0:T(8,128)S(1)}, u32[]{:S(2)}, u32[]{:S(2)}) collective-permute-start(f32[512,128]{1,0:T(8,128)S(1)} %copy-done.9), channel_id=1, source_target_pairs={{4,0},{8,4},{12,8},{16,12},{20,16},{24,20},{28,24},{32,28},{36,32}... | collective-permute-start | bytes 786440 | tf_op jit(solution)/shard_map/ppermute | solution.py:313
  34.2 0.0 copy-done.8
  34.2 3.1 %collective-permute-start = (f32[512,128]{1,0:T(8,128)S(1)}, f32[512,128]{1,0:T(8,128)S(1)}, u32[]{:S(2)}, u32[]{:S(2)}) collective-permute-start(f32[512,128]{1,0:T(8,128)S(1)} %copy-done.8), channel_id=1, source_target_pairs={{0,4},{4,8},{8,12},{12,16},{16,20},{20,24},{24,28},{28,32},{32,36}... | collective-permute-start | bytes 786440 | tf_op jit(solution)/shard_map/ppermute | solution.py:313
  37.3 0.0 copy-done.6
  37.3 0.6 copy.36
  37.9 6.7 %prepare_rest.1 = (bf16[1152,180]{1,0:T(8,128)(2,1)}, bf16[4,384,256]{2,1,0:T(8,128)(2,1)}, bf16[4,384,128]{2,1,0:T(8,128)(2,1)}, f32[128,384]{1,0:T(8,128)}, f32[128,384]{1,0:T(8,128)}, /*index=5*/f32[128,128]{1,0:T(8,128)}) custom-call(f32[9,3,9]{2,1,0:T(4,128)} %bitcast.36, f32[3,20,20]{2,1,0:T(8,128)} %kd.1, f32[10,4,20]{2,1,0:T(4,128)} %bitcast.41, ...), custom_call_target="tpu_custom_call" | custom-call | tf_op jit(solution)/shard_map/prepare_rest/pallas_call | solution.py:395
  44.7 5.4 %volume.1.refs_5_ = f32[180,2048]{1,0:T(8,128)} custom-call(f32[180,2048]{1,0:T(8,128)} %u.3, f32[3,2048]{1,0:T(4,128)} %t.3, f32[180,2048]{1,0:T(8,128)} %get-tuple-element.34.integral, bf16[1152,180]{1,0:T(8,128)(2,1)} %get-tuple-element.38.mi), custom_call_target="tpu_custom_call" | custom-call | tf_op jit(solution)/shard_map/volume/pallas_call | solution.py:439
  50.1 5.8 %thermal.1 = (f32[64,8192]{1,0:T(8,128)}, f32[64,8192]{1,0:T(8,128)}, f32[64,128]{1,0:T(8,128)}) custom-call(f32[64,8192]{1,0:T(8,128)} %th.1, f32[64,8192]{1,0:T(8,128)} %fl.1, f32[1,8192]{1,0:T(1,128)} %bitcast.33, f32[64,1]{1,0:T(8,128)} %constant.34.clone.shape, f32[64,64]{1,0:T(8,128)} %tr, f32[64,64]{1,0:T(8,128)} %hr.1), custom_call_target="tpu_custom_call" | custom-call | tf_op jit(solution)/shard_map/thermal/pallas_call | solution.py:423
  55.9 0.0 collective-permute-done.1.upper.refs_4_
  55.9 0.0 copy-start.1
  55.9 0.0 collective-permute-done.lower.refs_3_
  55.9 0.0 copy-start.2
  55.9 0.0 all-to-all-done
  56.0 0.0 copy-start
  56.0 0.7 copy-done.1
  56.6 0.1 copy-done.2
  56.8 0.3 copy-done
  57.1 0.0 copy-start.7
  57.1 0.0 copy-start.5
  57.1 5.9 %payload.1 = f32[1024,128]{1,0:T(8,128)} custom-call(s32[512]{0:T(512)} %face.2, s32[512]{0:T(512)} %seat.3, s32[8192]{0:T(1024)} %bitcast.29, f32[8192,128]{1,0:T(8,128)} %bitcast.19, f32[2048,128]{1,0:T(8,128)} %bitcast.22, f32[512,128]{1,0:T(8,128)} %copy-done.2, f32[512,128]{1,0:T(8,128)} %copy-done.1), custom_call_target="tpu_custom_call" | custom-call | tf_op jit(solution)/shard_map/payload/pallas_call | solution.py:451
  63.0 12.3 %all-to-all-start.1 = ((f32[128,8,128]{2,1,0:T(8,128)}), f32[128,8,128]{2,1,0:T(8,128)S(1)}, u32[]{:S(2)}, u32[]{:S(2)}) async-start(f32[128,8,128]{2,1,0:T(8,128)} %bitcast.26), calls=%async_computation.1 | async-start | bytes 1048576 | tf_op jit(solution)/shard_map/all_to_all | solution.py:460
  75.3 0.0 copy-done.7
  75.3 2.3 %compare_reduce_fusion = pred[4,2048]{1,0:T(4,128)(4,1)S(1)} fusion(s32[4,2048]{1,0:T(4,128)S(1)} %multiply_add_fusion, s32[512]{0:T(512)S(1)} %copy-done.7), kind=kLoop, calls=%fused_computation | loop fusion | flops 8380416 | bytes 43008 | tf_op jit(solution)/shard_map/reduce_or | solution.py:345
  77.6 0.0 copy-done.5
  77.6 0.6 broadcast_select_fusion.refs_6_
  78.2 11.6 %outside0.1.refs_5_ = f32[180,2048]{1,0:T(8,128)} custom-call(s32[8192]{0:T(1024)} %bitcast.30, f32[8192,128]{1,0:T(8,128)} %bitcast.20, f32[2048,128]{1,0:T(8,128)} %bitcast.23, f32[512,128]{1,0:T(8,128)} %copy-done.2, f32[512,128]{1,0:T(8,128)} %copy-done.1, f32[180,2048]{1,0:T(8,128)} %volume.1.refs_5_, f32[4,2048]{1,0:T(4,128)} %broadcast_select_fusion.refs_6_, ...), custom_call_target="tpu_custom_call" | custom-call | tf_op jit(solution)/shard_map/outside0/pallas_call | solution.py:463
  89.8 0.0 all-to-all-done.1
  89.9 0.0 copy-start.3
  89.9 0.8 copy-done.3
  90.7 4.9 %fault.1 = (f32[512,128]{1,0:T(8,128)}, f32[64,128]{1,0:T(8,128)}) custom-call(f32[1024,128]{1,0:T(8,128)} %bitcast.25, f32[64,128]{1,0:T(8,128)} %get-tuple-element.48.top, f32[64,128]{1,0:T(8,128)} %bitcast.34, f32[64,128]{1,0:T(8,128)} %bitcast.37, f32[64,128]{1,0:T(8,128)} %bitcast.38, f32[128,384]{1,0:T(8,128)} %get-tuple-element.49.wm, ...), custom_call_target="tpu_custom_call" | custom-call | tf_op jit(solution)/shard_map/fault/pallas_call | solution.py:481
  95.5 9.8 %all-to-all-start.2 = ((f32[128,4,128]{2,1,0:T(4,128)}), f32[128,4,128]{2,1,0:T(4,128)S(1)}, u32[]{:S(2)}, u32[]{:S(2)}) async-start(f32[128,4,128]{2,1,0:T(4,128)} %bitcast.32), calls=%async_computation.2 | async-start | bytes 524288 | tf_op jit(solution)/shard_map/all_to_all | solution.py:492
  105.3 11.7 %outside2.1.base = f32[180,2048]{1,0:T(8,128)} custom-call(s32[8192]{0:T(1024)} %bitcast.31, f32[8192,128]{1,0:T(8,128)} %bitcast.21, f32[2048,128]{1,0:T(8,128)} %bitcast.24, f32[512,128]{1,0:T(8,128)} %copy-done.2, f32[512,128]{1,0:T(8,128)} %copy-done.1, f32[180,2048]{1,0:T(8,128)} %outside0.1.refs_5_, f32[4,2048]{1,0:T(4,128)} %broadcast_select_fusion.refs_6_, ...), custom_call_target="tpu_custom_call" | custom-call | tf_op jit(solution)/shard_map/outside2/pallas_call | solution.py:463
  117.0 0.0 all-to-all-done.2
  117.0 0.0 copy-start.4
  117.0 0.7 copy-done.4
  117.7 6.2 %finish.1 = f32[180,2048]{1,0:T(8,128)} custom-call(s32[512]{0:T(512)} %face.2, s32[512]{0:T(512)} %seat.3, f32[512,128]{1,0:T(8,128)} %bitcast.27, f32[180,2048]{1,0:T(8,128)} %outside2.1.base, f32[4,2048]{1,0:T(4,128)} %area.1, bf16[4,384,128]{2,1,0:T(8,128)(2,1)} %get-tuple-element.56.ws), custom_call_target="tpu_custom_call" | custom-call | tf_op jit(solution)/shard_map/finish/pallas_call | solution.py:496
  (1 shorter events, 0.0 us)
Async XLA Ops:
  26.3 5.0 %copy-start.9 = (f32[512,128]{1,0:T(8,128)S(1)}, f32[512,128]{1,0:T(8,128)}, u32[]{:S(2)}) copy-start(f32[512,128]{1,0:T(8,128)} %get-tuple-element.43) | copy-start | bytes 786436
  26.3 7.9 %copy-start.8 = (f32[512,128]{1,0:T(8,128)S(1)}, f32[512,128]{1,0:T(8,128)}, u32[]{:S(2)}) copy-start(f32[512,128]{1,0:T(8,128)} %get-tuple-element.36) | copy-start | bytes 786436
  26.3 11.0 %copy-start.6 = (s32[4,2048]{1,0:T(4,128)S(1)}, s32[4,2048]{1,0:T(4,128)}, u32[]{:S(2)}) copy-start(s32[4,2048]{1,0:T(4,128)} %param.51) | copy-start | bytes 98308
  26.3 29.6 %all-to-all-start = ((f32[4,512,128]{2,1,0:T(8,128)}), f32[4,512,128]{2,1,0:T(8,128)S(1)}, u32[]{:S(2)}, u32[]{:S(2)}) async-start(f32[4,512,128]{2,1,0:T(8,128)} %bitcast.28), calls=%async_computation | async-start | bytes 2097152 | tf_op jit(solution)/shard_map/all_to_all | solution.py:388
  31.3 24.6 %collective-permute-start.1 = (f32[512,128]{1,0:T(8,128)S(1)}, f32[512,128]{1,0:T(8,128)S(1)}, u32[]{:S(2)}, u32[]{:S(2)}) collective-permute-start(f32[512,128]{1,0:T(8,128)S(1)} %copy-done.9), channel_id=1, source_target_pairs={{4,0},{8,4},{12,8},{16,12},{20,16},{24,20},{28,24},{32,28},{36,32}... | collective-permute-start | bytes 786440 | tf_op jit(solution)/shard_map/ppermute | solution.py:313
  34.2 21.7 %collective-permute-start = (f32[512,128]{1,0:T(8,128)S(1)}, f32[512,128]{1,0:T(8,128)S(1)}, u32[]{:S(2)}, u32[]{:S(2)}) collective-permute-start(f32[512,128]{1,0:T(8,128)S(1)} %copy-done.8), channel_id=1, source_target_pairs={{0,4},{4,8},{8,12},{12,16},{16,20},{20,24},{24,28},{28,32},{32,36}... | collective-permute-start | bytes 786440 | tf_op jit(solution)/shard_map/ppermute | solution.py:313
  55.9 0.7 copy-start.1
  55.9 0.8 copy-start.2
  56.0 1.1 copy-start
  57.1 18.2 %copy-start.7 = (s32[512]{0:T(512)S(1)}, s32[512]{0:T(512)}, u32[]{:S(2)}) copy-start(s32[512]{0:T(512)} %face.2) | copy-start | bytes 6148
  57.1 20.5 %copy-start.5 = (f32[4,2048]{1,0:T(4,128)S(1)}, f32[4,2048]{1,0:T(4,128)}, u32[]{:S(2)}) copy-start(f32[4,2048]{1,0:T(4,128)} %area.1) | copy-start | bytes 98308
  63.0 26.9 %all-to-all-start.1 = ((f32[128,8,128]{2,1,0:T(8,128)}), f32[128,8,128]{2,1,0:T(8,128)S(1)}, u32[]{:S(2)}, u32[]{:S(2)}) async-start(f32[128,8,128]{2,1,0:T(8,128)} %bitcast.26), calls=%async_computation.1 | async-start | bytes 1048576 | tf_op jit(solution)/shard_map/all_to_all | solution.py:460
  89.9 0.8 copy-start.3
  95.5 21.5 %all-to-all-start.2 = ((f32[128,4,128]{2,1,0:T(4,128)}), f32[128,4,128]{2,1,0:T(4,128)S(1)}, u32[]{:S(2)}, u32[]{:S(2)}) async-start(f32[128,4,128]{2,1,0:T(4,128)} %bitcast.32), calls=%async_computation.2 | async-start | bytes 524288 | tf_op jit(solution)/shard_map/all_to_all | solution.py:492
  117.0 0.7 copy-start.4

commit v2 on v1

--- a/solution.py
+++ b/solution.py
@@ -68,6 +68,12 @@
     return lax.dot_general(a, b, (((1,), (cb,)), ((), ())), preferred_element_type=F32)
 
 
+def triple(a, b):
+    ah, al = halves(a)
+    bh, bl = halves(b)
+    return single(ah, bh) + (single(ah, bl) + single(al, bh))
+
+
 def put(out, at, value, half):
     high, low = halves(value)
     rows, lanes = value.shape
@@ -82,36 +88,59 @@
     return both[0:half] + (both[half:] + single(weights[0:half], xl, cb))
 
 
+def spread_rows(select, x):
+    xh, xl = halves(x)
+    return single(select, xh) + single(select, xl)
+
+
+def grid_of(rows_of, x, lanes_of):
+    return spread_rows(rows_of, dot(x, lanes_of, 1, 1))
+
+
 def prepare_kernel(a, pd, rs, e, f, g, h, mp, wt):
     e_, f_, g_, h_ = e[...], f[...], g[...], h[...]
+    eb, fb = e_.astype(BF16), f_.astype(BF16)
     mp[...] = jnp.zeros(mp.shape, BF16)
     for d in range(3):
-        left = dot(dot(e_, a[:, d, :]), e_, 1, 1)
-        put(mp, ((), d * PAD, 0), -left * dot(dot(f_, pd[d]), f_, 1, 1), 3 * PAD)
-    same = dot(e_, g_, 1, 1)
+        left = grid_of(eb, a[:, d, :], e_)
+        put(mp, ((), d * PAD, 0), -left * grid_of(fb, pd[d], f_), 3 * PAD)
+    same = single(eb, g_.astype(BF16), 1)
     for face in range(4):
-        high, low = halves(same * dot(dot(f_, rs[:, face, :], 1, 1), h_, 1, 1))
+        lift = spread_rows(fb, dot(rs[:, face, :], h_, 0, 1))
+        high, low = halves(same * lift)
         wt[0, :, face * LANES : (face + 1) * LANES] = high
         wt[1, :, face * LANES : (face + 1) * LANES] = low
 
 
 def prepare_rest_kernel(
-    a, kd, sr, rt, bp, qg, e, f, g, h, tile, side, linear, slip, mi, wf, ws, wm, wp, vm
+    face, area, a, kd, sr, rt, bp, qg, e, f, g, h, tile, side, linear, slip,
+    open_area, mi, wf, ws, wm, wp, vm,
 ):
     e_, f_, g_, h_ = e[...], f[...], g[...], h[...]
+    eb, fb = e_.astype(BF16), f_.astype(BF16)
+    index = face[...]
+    high = lax.shift_right_arithmetic(index, 7)
+    rows = lax.broadcasted_iota(jnp.int32, (64, index.shape[1]), 0)
+    lanes = lax.broadcasted_iota(jnp.int32, (LANES, index.shape[1]), 0)
+    upper = jnp.where(rows == high, 1.0, 0.0).astype(BF16)
+    lower = jnp.where(lanes == (index & 127), 1.0, 0.0).astype(BF16)
+    closed = single(upper, lower, 1)
+    for r in range(64):
+        at = (slice(r // 16, r // 16 + 1), slice(r % 16 * LANES, (r % 16 + 1) * LANES))
+        open_area[at] = jnp.where(closed[r : r + 1] > 0.5, 0.0, area[at])
     mi[...] = jnp.zeros(mi.shape, BF16)
     wf[...] = jnp.zeros(wf.shape, BF16)
     ws[...] = jnp.zeros(ws.shape, BF16)
     for d in range(3):
-        left = dot(dot(e_, a[:, d, :]), e_, 1, 1)
-        put(mi, ((), d * PAD, 0), left * dot(dot(f_, kd[d]), f_, 1, 1), 3 * PAD)
-    r0 = dot(dot(e_, rt[:, 0, :]), g_, 1, 1)
-    r1 = dot(dot(e_, rt[:, 1, :]), g_, 1, 1)
-    for face in range(4):
-        lift = dot(dot(f_, sr[:, face, :], 1, 1), h_, 1, 1)
-        put(wf, ((face,), 0, 0), r0 * lift, PAD)
-        put(wf, ((face,), 0, LANES), r1 * lift, PAD)
-        put(ws, ((face,), 0, 0), (r0 + r1) * lift, PAD)
+        left = grid_of(eb, a[:, d, :], e_)
+        put(mi, ((), d * PAD, 0), left * grid_of(fb, kd[d], f_), 3 * PAD)
+    r0 = grid_of(eb, rt[:, 0, :], g_)
+    r1 = grid_of(eb, rt[:, 1, :], g_)
+    for n in range(4):
+        lift = spread_rows(fb, dot(sr[:, n, :], h_, 0, 1))
+        put(wf, ((n,), 0, 0), r0 * lift, PAD)
+        put(wf, ((n,), 0, LANES), r1 * lift, PAD)
+        put(ws, ((n,), 0, 0), (r0 + r1) * lift, PAD)
     hb = dot(dot(h_, bp[...], 1, 1), tile[...], 1, 1)
     hch = dot(dot(h_, dot(bp[...], qg[...], 0, 0)), h_, 1, 1)
     for out, at in ((wm, 0), (wp, 1)):
@@ -152,21 +181,25 @@
     partial[...] = u[...] + directional(mi[...], integral[...], t[...])
 
 
-def take_rows(index, start, count, source, target, base):
+def take_rows(index, row, source, target, base):
     def body(i, carry):
-        first = i * 16
-        rows = [source[pl.ds(index[start + first + k], 1), :] for k in range(16)]
-        for k in range(16):
-            target[pl.ds(base + first + k, 1), :] = rows[k]
+        first = pl.multiple_of(i * LANES, LANES)
+        listed = index.at[row, pl.ds(first, LANES)]
+        place = target.at[pl.ds(base + first, LANES)]
+        for at in range(0, LANES, 16):
+            rows = [source[pl.ds(listed[at + k], 1), :] for k in range(16)]
+            for k in range(16):
+                place[at + k : at + k + 1, :] = rows[k]
         return carry
 
-    lax.fori_loop(0, count // 16, body, 0)
+    lax.fori_loop(0, index.shape[1] // LANES, body, 0)
 
 
 def send_kernel(index, faces, group, lower, upper):
-    take_rows(index, 0, 2048, faces, group, 0)
-    take_rows(index, 2048, 512, faces, lower, 0)
-    take_rows(index, 2560, 512, faces, upper, 0)
+    for peer in range(4):
+        take_rows(index, peer, faces, group, peer * index.shape[1])
+    take_rows(index, 4, faces, lower, 0)
+    take_rows(index, 5, faces, upper, 0)
 
 
 def thermal_kernel(th, fl, speed, shape, tr, hr, new_th, new_fl, top):
@@ -214,7 +247,9 @@
             column = face[i * 4 + k]
             live = column >= 0
             rows.append(table[pl.ds(jnp.where(live, column, extent), 1), :])
-            outer = jnp.where(live, entry[jnp.maximum(column, 0)], extent)
+            safe = jnp.maximum(column, 0)
+            outer = entry[lax.shift_right_logical(safe, 11), safe & 2047]
+            outer = jnp.where(live, outer, extent)
             rows.append(table[pl.ds(outer, 1), :])
         for k in range(4):
             payload[pl.ds(owner * 8 + k, 1), :] = rows[2 * k]
@@ -229,7 +264,7 @@
     elems = faces.shape[0] // 4
     result = partial[...]
     for face in (first, first + 1):
-        take_rows(entry, face * elems, elems, table, outside, 0)
+        take_rows(entry, face, table, outside, 0)
         rows = jnp.concatenate([table[face * elems : (face + 1) * elems, :], outside[...]], axis=1)
         flux = stacked(wf[face], rows, 1)
         result = result - flux[0:ROWS] * area[face : face + 1, :]
@@ -242,7 +277,7 @@
     pick = lambda at: jnp.concatenate(
         [arrived[pl.ds(at + k, LANES, stride=8), :] for k in range(4)], axis=0
     )
-    linear = dot(pick(0), wm[...]) + dot(pick(4), wp[...])
+    linear = triple(pick(0), wm[...]) + triple(pick(4), wp[...])
     locked = jnp.zeros((LANES, LANES), F32)
     normal = jnp.zeros((LANES, LANES), F32)
     for k in range(4):
@@ -269,7 +304,7 @@
     mine = jnp.concatenate(
         [jnp.where(lanes == half + k, spread, 0.0) for k in range(4)], axis=0
     )
-    result = linear[:, 2 * LANES :] + dot(mine, vm[...])
+    result = linear[:, 2 * LANES :] + triple(mine, vm[...])
     for k in range(4):
         imposed[pl.ds(k, LANES, stride=4), :] = result[k * LANES : (k + 1) * LANES]
 
@@ -342,13 +377,7 @@
     devices = lax.axis_size(("wide", "narrow"))
     points = thermal_field.shape[1]
     e, f, g, h, tile, side, linear, slip, pair = tables()
-    ruptured = jnp.any(
-        rupture_side_index[:, None, None]
-        == jnp.arange(faces_total, dtype=jnp.int32).reshape(1, 4, elems),
-        axis=0,
-    )
-    open_area = jnp.where(ruptured, 0.0, surface_measure_quotient)
-    entry = boundary_entry_index.reshape(-1)
+    entry = boundary_entry_index
     elastic = jnp.transpose(elastic_directional_derivs, (1, 0, 2))
 
     mp, wt = pl.pallas_call(
@@ -384,7 +413,7 @@
         out_shape=[shaped((2048, LANES)), shaped((512, LANES)), shaped((512, LANES))],
         compiler_params=LIMIT,
         name="halo_rows",
-    )(outbound_ghost_indices.reshape(-1), face_rows)
+    )(outbound_ghost_indices, face_rows)
     group = lax.all_to_all(group_out, "narrow", split_axis=0, concat_axis=0, tiled=True)
     lower = shift(lower_out, "wide", 1)
     upper = shift(upper_out, "wide", -1)
@@ -392,11 +421,12 @@
     tensors, sensitivity, _ = lax.optimization_barrier(
         (riemann_numerical_tables, thermal_diffusion_resolvent, lower_out)
     )
-    mi, wf, ws, wm, wp, vm = pl.pallas_call(
+    open_area, mi, wf, ws, wm, wp, vm = pl.pallas_call(
         prepare_rest_kernel,
-        in_specs=whole(14),
-        out_specs=whole(6),
+        in_specs=whole(16),
+        out_specs=whole(7),
         out_shape=[
+            shaped((4, elems)),
             shaped((6 * PAD, ROWS), BF16),
             shaped((4, 2 * PAD, 2 * LANES), BF16),
             shaped((4, 2 * PAD, LANES), BF16),
@@ -407,6 +437,8 @@
         compiler_params=LIMIT,
         name="prepare_rest",
     )(
+        rupture_side_index.reshape(1, -1),
+        surface_measure_quotient,
         elastic,
         interior_gradient_tables,
         jnp.transpose(surface_raise_tables, (2, 0, 1)),

time: 126 us -> 121 us (0.960); the launches traced: 124 us -> 121 us
  starting transfers between devices: 33 us -> 27.6 us
  waiting for transfers between devices: 0.01 us -> 3.75 us
  other arithmetic: 2.9 us -> 0 us
  Pallas kernels: 82.7 us -> 85.6 us
  local copies, waits for them, and re-layouts: 4.56 us -> 2.66 us
    pallas_call x1, Pallas kernels: 5.89 us -> 9.55 us  [per_device(): pl.pallas_call(payload_kernel, in_specs=whole(7, (0, 1, 2), (3, 4, 5, 6))...]
    all_to_all x1, starting transfers between devices: 9.76 us -> 6.56 us  [per_device(): lax.all_to_all(imposed, ('wide', 'narrow'), split_axis=0, concat_axis=0,...]
    all_to_all x1, waiting for transfers between devices: 0.01 us -> 3.2 us  [per_device(): lax.all_to_all(payload, ('wide', 'narrow'), split_axis=0, concat_axis=0,...]
    reduce_or x1 -> x0, other arithmetic: 2.26 us -> none  [per_device(): jnp.any(rupture_side_index[:, None, None] == jnp.arange(faces_total, dtyp...]
    all_to_all x1, starting transfers between devices: 12.3 us -> 10.1 us  [per_device(): lax.all_to_all(payload, ('wide', 'narrow'), split_axis=0, concat_axis=0,...]
    pallas_call x2, Pallas kernels: 23.3 us -> 21.6 us  [half(): pl.pallas_call(lambda *refs: outside_kernel(first, *refs), in_specs=whole...]
    reshape x1 -> x0, local copies, waits for them, and re-layouts: 1.32 us -> none  [per_device(): outbound_ghost_indices.reshape(-1)]
    unnamed x21 -> x14, local copies, waits for them, and re-layouts: 3.24 us -> 2.66 us
  transfers between devices with their start and end apart: 5 -> 5, of which waited for: 0 -> 2; matrix products, arithmetic and copies ran while one was open for 3% -> 0% of each run, Pallas kernels for 33% -> 34%
where the time goes in v2:
time: 121 us
  Pallas kernels  85.6 us (71%)
  starting transfers between devices  27.6 us (23%)
  waiting for transfers between devices  3.75 us (3%)
  local copies, waits for them, and re-layouts  2.66 us (2%)
    pallas_call x2, Pallas kernels, half(): pl.pallas_call(lambda *refs: outside_kernel(first, *refs), in_specs=whole...  21.6 us
    pallas_call x1, Pallas kernels, per_device(): pl.pallas_call(predictor_kernel, grid=(elems // step,), in_specs=[column(...  12.2 us
    all_to_all x1, starting transfers between devices, per_device(): lax.all_to_all(payload, ('wide', 'narrow'), split_axis=0, concat_axis=0,...  10.1 us
    pallas_call x1, Pallas kernels, per_device(): pl.pallas_call(payload_kernel, in_specs=whole(7, (0, 1, 2), (3, 4, 5, 6))...  9.55 us
    pallas_call x1, Pallas kernels, per_device(): pl.pallas_call(prepare_rest_kernel, in_specs=whole(16), out_specs=whole(7...  7.98 us
    pallas_call x1, Pallas kernels, per_device(): pl.pallas_call(finish_kernel, in_specs=whole(6, (0, 1), (3,)), out_specs=...  7.32 us
    all_to_all x1, starting transfers between devices, per_device(): lax.all_to_all(imposed, ('wide', 'narrow'), split_axis=0, concat_axis=0,...  6.56 us
    ppermute x2, starting transfers between devices, shift(): return lax.ppermute(array, axis, pairs)  5.95 us
  transfers between devices with their start and end apart: 5, of which 2 were waited for; matrix products, arithmetic and copies ran while one was open for 0% of the time, Pallas kernels for 34%

profile of v2, /device:TPU:1, one launch (start us, length us, event | category | flops | bytes accessed | tf_op | source)
XLA Modules:
  0.0 120.5 jit_solution(13320548736202732766)
XLA Ops:
  0.6 5.8 %prepare.1 = (bf16[1152,180]{1,0:T(8,128)(2,1)}, bf16[2,180,512]{2,1,0:T(8,128)(2,1)}) custom-call(f32[9,3,9]{2,1,0:T(4,128)} %bitcast.31, f32[3,20,20]{2,1,0:T(8,128)} %pd.1, f32[10,4,20]{2,1,0:T(4,128)} %bitcast.35, f32[180,9]{1,0:T(8,128)} %constant.20.clone.e, f32[180,20]{1,0:T(8,128)} %constant.21.clone.f, f32[128,9]{1,0:T(8,128)} %constant.22.clone.g, ...), custom_call_target="tpu_custom_call" | custom-call | tf_op jit(solution)/shard_map/prepare/pallas_call | solution.py:383
  6.4 12.2 %predictor.1 = (f32[180,2048]{1,0:T(8,128)}, f32[4,2048,128]{2,1,0:T(8,128)}) custom-call(f32[180,2048]{1,0:T(8,128)} %u.3, f32[3,2048]{1,0:T(4,128)} %t.3, bf16[1152,180]{1,0:T(8,128)(2,1)} %get-tuple-element.33.mp, bf16[2,180,512]{2,1,0:T(8,128)(2,1)} %get-tuple-element.34.wt), custom_call_target="tpu_custom_call" | custom-call | tf_op jit(solution)/shard_map/predictor/pallas_call | solution.py:397
  18.7 5.9 %halo_rows.1 = (f32[2048,128]{1,0:T(8,128)}, f32[512,128]{1,0:T(8,128)}, f32[512,128]{1,0:T(8,128)}) custom-call(s32[6,512]{1,0:T(8,128)} %index.1, f32[8192,128]{1,0:T(8,128)} %bitcast.17), custom_call_target="tpu_custom_call" | custom-call | tf_op jit(solution)/shard_map/halo_rows/pallas_call | solution.py:409
  24.6 0.0 copy-start.6
  24.6 0.0 copy-start.5
  24.6 5.0 %all-to-all-start = ((f32[4,512,128]{2,1,0:T(8,128)}), f32[4,512,128]{2,1,0:T(8,128)S(1)}, u32[]{:S(2)}, u32[]{:S(2)}) async-start(f32[4,512,128]{2,1,0:T(8,128)} %bitcast.27), calls=%async_computation | async-start | bytes 2097152 | tf_op jit(solution)/shard_map/all_to_all | solution.py:417
  29.6 0.0 copy-done.6
  29.6 2.9 %collective-permute-start.1 = (f32[512,128]{1,0:T(8,128)S(1)}, f32[512,128]{1,0:T(8,128)S(1)}, u32[]{:S(2)}, u32[]{:S(2)}) collective-permute-start(f32[512,128]{1,0:T(8,128)S(1)} %copy-done.6), channel_id=1, source_target_pairs={{4,0},{8,4},{12,8},{16,12},{20,16},{24,20},{28,24},{32,28},{36,32}... | collective-permute-start | bytes 786440 | tf_op jit(solution)/shard_map/ppermute | solution.py:348
  32.4 0.0 copy-done.5
  32.4 3.1 %collective-permute-start = (f32[512,128]{1,0:T(8,128)S(1)}, f32[512,128]{1,0:T(8,128)S(1)}, u32[]{:S(2)}, u32[]{:S(2)}) collective-permute-start(f32[512,128]{1,0:T(8,128)S(1)} %copy-done.5), channel_id=1, source_target_pairs={{0,4},{4,8},{8,12},{12,16},{16,20},{20,24},{24,28},{28,32},{32,36}... | collective-permute-start | bytes 786440 | tf_op jit(solution)/shard_map/ppermute | solution.py:348
  35.6 8.0 %prepare_rest.1 = (f32[4,2048]{1,0:T(4,128)}, bf16[1152,180]{1,0:T(8,128)(2,1)}, bf16[4,384,256]{2,1,0:T(8,128)(2,1)}, bf16[4,384,128]{2,1,0:T(8,128)(2,1)}, f32...) custom-call(s32[1,512]{1,0:T(1,128)} %bitcast.37, f32[4,2048]{1,0:T(4,128)} %area.3, f32[9,3,9]{2,1,0:T(4,128)} %bitcast.32, ...), custom_call_target="tpu_custom_call" | custom-call | tf_op jit(solution)/shard_map/prepare_rest/pallas_call | solution.py:424
  43.5 5.4 %volume.1.refs_5_ = f32[180,2048]{1,0:T(8,128)} custom-call(f32[180,2048]{1,0:T(8,128)} %u.3, f32[3,2048]{1,0:T(4,128)} %t.3, f32[180,2048]{1,0:T(8,128)} %get-tuple-element.35.integral, bf16[1152,180]{1,0:T(8,128)(2,1)} %get-tuple-element.39.mi), custom_call_target="tpu_custom_call" | custom-call | tf_op jit(solution)/shard_map/volume/pallas_call | solution.py:471
  49.0 5.8 %thermal.1 = (f32[64,8192]{1,0:T(8,128)}, f32[64,8192]{1,0:T(8,128)}, f32[64,128]{1,0:T(8,128)}) custom-call(f32[64,8192]{1,0:T(8,128)} %th.1, f32[64,8192]{1,0:T(8,128)} %fl.1, f32[1,8192]{1,0:T(1,128)} %bitcast.29, f32[64,1]{1,0:T(8,128)} %constant.28.clone.shape, f32[64,64]{1,0:T(8,128)} %tr, f32[64,64]{1,0:T(8,128)} %hr.1), custom_call_target="tpu_custom_call" | custom-call | tf_op jit(solution)/shard_map/thermal/pallas_call | solution.py:455
  54.8 0.0 collective-permute-done.1.upper.refs_4_
  54.8 0.0 copy-start.1
  54.8 0.0 collective-permute-done.lower.refs_3_
  54.8 0.0 copy-start.2
  54.8 0.0 all-to-all-done
  54.8 0.0 copy-start
  54.8 0.7 copy-done.1
  55.5 0.1 copy-done.2
  55.6 0.3 copy-done
  55.9 9.6 %payload.1 = f32[1024,128]{1,0:T(8,128)} custom-call(s32[512]{0:T(512)} %face.2, s32[512]{0:T(512)} %seat.3, s32[4,2048]{1,0:T(4,128)} %refs_0_.3, f32[8192,128]{1,0:T(8,128)} %bitcast.18, f32[2048,128]{1,0:T(8,128)} %bitcast.21, f32[512,128]{1,0:T(8,128)} %copy-done.2, f32[512,128]{1,0:T(8,128)} %copy-done.1), custom_call_target="tpu_custom_call" | custom-call | tf_op jit(solution)/shard_map/payload/pallas_call | solution.py:483
  65.5 10.1 %all-to-all-start.1 = ((f32[128,8,128]{2,1,0:T(8,128)}), f32[128,8,128]{2,1,0:T(8,128)S(1)}, u32[]{:S(2)}, u32[]{:S(2)}) async-start(f32[128,8,128]{2,1,0:T(8,128)} %bitcast.25), calls=%async_computation.1 | async-start | bytes 1048576 | tf_op jit(solution)/shard_map/all_to_all | solution.py:492
  75.6 10.8 %outside0.1.refs_5_ = f32[180,2048]{1,0:T(8,128)} custom-call(s32[4,2048]{1,0:T(4,128)} %refs_0_.3, f32[8192,128]{1,0:T(8,128)} %bitcast.19, f32[2048,128]{1,0:T(8,128)} %bitcast.22, f32[512,128]{1,0:T(8,128)} %copy-done.2, f32[512,128]{1,0:T(8,128)} %copy-done.1, f32[180,2048]{1,0:T(8,128)} %volume.1.refs_5_, f32[4,2048]{1,0:T(4,128)} %get-tuple-element.47.refs_6_, ...), custom_call_target="tpu_custom_call" | custom-call | tf_op jit(solution)/shard_map/outside0/pallas_call | solution.py:495
  86.4 3.2 %all-to-all-done.1 = f32[128,8,128]{2,1,0:T(8,128)S(1)} async-done(((f32[128,8,128]{2,1,0:T(8,128)}), f32[128,8,128]{2,1,0:T(8,128)S(1)}, u32[]{:S(2)}, u32[]{:S(2)}) %all-to-all-start.1) | async-done | bytes 524320 | tf_op jit(solution)/shard_map/all_to_all | solution.py:492
  89.6 0.0 copy-start.3
  89.6 0.8 copy-done.3
  90.4 4.0 %fault.1 = (f32[512,128]{1,0:T(8,128)}, f32[64,128]{1,0:T(8,128)}) custom-call(f32[1024,128]{1,0:T(8,128)} %bitcast.24, f32[64,128]{1,0:T(8,128)} %get-tuple-element.50.top, f32[64,128]{1,0:T(8,128)} %bitcast.30, f32[64,128]{1,0:T(8,128)} %bitcast.33, f32[64,128]{1,0:T(8,128)} %bitcast.34, f32[128,384]{1,0:T(8,128)} %get-tuple-element.51.wm, ...), custom_call_target="tpu_custom_call" | custom-call | tf_op jit(solution)/shard_map/fault/pallas_call | solution.py:513
  94.4 6.6 %all-to-all-start.2 = ((f32[128,4,128]{2,1,0:T(4,128)}), f32[128,4,128]{2,1,0:T(4,128)S(1)}, u32[]{:S(2)}, u32[]{:S(2)}) async-start(f32[128,4,128]{2,1,0:T(4,128)} %bitcast.28), calls=%async_computation.2 | async-start | bytes 524288 | tf_op jit(solution)/shard_map/all_to_all | solution.py:524
  101.0 10.8 %outside2.1.base = f32[180,2048]{1,0:T(8,128)} custom-call(s32[4,2048]{1,0:T(4,128)} %refs_0_.3, f32[8192,128]{1,0:T(8,128)} %bitcast.20, f32[2048,128]{1,0:T(8,128)} %bitcast.23, f32[512,128]{1,0:T(8,128)} %copy-done.2, f32[512,128]{1,0:T(8,128)} %copy-done.1, f32[180,2048]{1,0:T(8,128)} %outside0.1.refs_5_, f32[4,2048]{1,0:T(4,128)} %get-tuple-element.47.refs_6_, ...), custom_call_target="tpu_custom_call" | custom-call | tf_op jit(solution)/shard_map/outside2/pallas_call | solution.py:495
  111.8 0.5 all-to-all-done.2
  112.3 0.0 copy-start.4
  112.3 0.7 copy-done.4
  113.1 7.3 %finish.1 = f32[180,2048]{1,0:T(8,128)} custom-call(s32[512]{0:T(512)} %face.2, s32[512]{0:T(512)} %seat.3, f32[512,128]{1,0:T(8,128)} %bitcast.26, f32[180,2048]{1,0:T(8,128)} %outside2.1.base, f32[4,2048]{1,0:T(4,128)} %area.3, bf16[4,384,128]{2,1,0:T(8,128)(2,1)} %get-tuple-element.58.ws), custom_call_target="tpu_custom_call" | custom-call | tf_op jit(solution)/shard_map/finish/pallas_call | solution.py:528
Async XLA Ops:
  24.6 5.0 %copy-start.6 = (f32[512,128]{1,0:T(8,128)S(1)}, f32[512,128]{1,0:T(8,128)}, u32[]{:S(2)}) copy-start(f32[512,128]{1,0:T(8,128)} %get-tuple-element.44) | copy-start | bytes 786436
  24.6 7.8 %copy-start.5 = (f32[512,128]{1,0:T(8,128)S(1)}, f32[512,128]{1,0:T(8,128)}, u32[]{:S(2)}) copy-start(f32[512,128]{1,0:T(8,128)} %get-tuple-element.37) | copy-start | bytes 786436
  24.6 30.2 %all-to-all-start = ((f32[4,512,128]{2,1,0:T(8,128)}), f32[4,512,128]{2,1,0:T(8,128)S(1)}, u32[]{:S(2)}, u32[]{:S(2)}) async-start(f32[4,512,128]{2,1,0:T(8,128)} %bitcast.27), calls=%async_computation | async-start | bytes 2097152 | tf_op jit(solution)/shard_map/all_to_all | solution.py:417
  29.6 25.2 %collective-permute-start.1 = (f32[512,128]{1,0:T(8,128)S(1)}, f32[512,128]{1,0:T(8,128)S(1)}, u32[]{:S(2)}, u32[]{:S(2)}) collective-permute-start(f32[512,128]{1,0:T(8,128)S(1)} %copy-done.6), channel_id=1, source_target_pairs={{4,0},{8,4},{12,8},{16,12},{20,16},{24,20},{28,24},{32,28},{36,32}... | collective-permute-start | bytes 786440 | tf_op jit(solution)/shard_map/ppermute | solution.py:348
  32.4 22.3 %collective-permute-start = (f32[512,128]{1,0:T(8,128)S(1)}, f32[512,128]{1,0:T(8,128)S(1)}, u32[]{:S(2)}, u32[]{:S(2)}) collective-permute-start(f32[512,128]{1,0:T(8,128)S(1)} %copy-done.5), channel_id=1, source_target_pairs={{0,4},{4,8},{8,12},{12,16},{16,20},{20,24},{24,28},{28,32},{32,36}... | collective-permute-start | bytes 786440 | tf_op jit(solution)/shard_map/ppermute | solution.py:348
  54.8 0.7 copy-start.1
  54.8 0.8 copy-start.2
  54.8 1.1 copy-start
  65.5 24.1 %all-to-all-start.1 = ((f32[128,8,128]{2,1,0:T(8,128)}), f32[128,8,128]{2,1,0:T(8,128)S(1)}, u32[]{:S(2)}, u32[]{:S(2)}) async-start(f32[128,8,128]{2,1,0:T(8,128)} %bitcast.25), calls=%async_computation.1 | async-start | bytes 1048576 | tf_op jit(solution)/shard_map/all_to_all | solution.py:492
  89.6 0.8 copy-start.3
  94.4 17.9 %all-to-all-start.2 = ((f32[128,4,128]{2,1,0:T(4,128)}), f32[128,4,128]{2,1,0:T(4,128)S(1)}, u32[]{:S(2)}, u32[]{:S(2)}) async-start(f32[128,4,128]{2,1,0:T(4,128)} %bitcast.28), calls=%async_computation.2 | async-start | bytes 524288 | tf_op jit(solution)/shard_map/all_to_all | solution.py:524
  112.3 0.7 copy-start.4

commit v3 on v2

--- a/solution.py
+++ b/solution.py
@@ -16,7 +16,7 @@
 BF16 = jnp.bfloat16
 VMEM = pltpu.MemorySpace.VMEM
 SMEM = pltpu.MemorySpace.SMEM
-LIMIT = pltpu.CompilerParams(vmem_limit_bytes=56 * 1024 * 1024)
+LIMIT = pltpu.CompilerParams(vmem_limit_bytes=24 * 1024 * 1024)
 
 
 def tables():
@@ -233,40 +233,55 @@
     )
 
 
-def payload_kernel(face, seat, entry, faces, group, lower, upper, payload, table, sems):
+def payload_kernel(face, seat, entry, faces, group, lower, upper, payload, table, buffer, sems):
     extent = table.shape[0] - 8
-    payload[...] = jnp.zeros(payload.shape, F32)
+    buffer[...] = jnp.zeros(buffer.shape, F32)
     table[extent : extent + 8, :] = jnp.zeros((8, LANES), F32)
     blocks = live_blocks(seat)
     fill(table, (faces, group, lower, upper), sems)
+    spare = buffer.shape[0] - 8
 
     def body(i, carry):
-        owner = seat[i * 4]
         rows = []
-        for k in range(4):
-            column = face[i * 4 + k]
+        for k in range(16):
+            column = face[i * 16 + k]
             live = column >= 0
-            rows.append(table[pl.ds(jnp.where(live, column, extent), 1), :])
             safe = jnp.maximum(column, 0)
             outer = entry[lax.shift_right_logical(safe, 11), safe & 2047]
-            outer = jnp.where(live, outer, extent)
-            rows.append(table[pl.ds(outer, 1), :])
-        for k in range(4):
-            payload[pl.ds(owner * 8 + k, 1), :] = rows[2 * k]
-            payload[pl.ds(owner * 8 + 4 + k, 1), :] = rows[2 * k + 1]
+            rows.append(table[pl.ds(jnp.where(live, column, extent), 1), :])
+            rows.append(table[pl.ds(jnp.where(live, outer, extent), 1), :])
+        for n in range(4):
+            owner = seat[i * 16 + n * 4]
+            first = jnp.where(owner >= 0, owner * 8, spare)
+            for k in range(4):
+                buffer[pl.ds(first + k, 1), :] = rows[8 * n + 2 * k]
+                buffer[pl.ds(first + 4 + k, 1), :] = rows[8 * n + 2 * k + 1]
         return carry
 
-    lax.fori_loop(0, blocks, body, 0)
-
-
-def outside_kernel(first, entry, faces, group, lower, upper, partial, area, wf, base, table, outside, sems):
-    fill(table, (faces, group, lower, upper), sems)
-    elems = faces.shape[0] // 4
-    result = partial[...]
-    for face in (first, first + 1):
+    lax.fori_loop(0, lax.shift_right_logical(blocks + 3, 2), body, 0)
+    copy = pltpu.make_async_copy(buffer.at[pl.ds(0, spare)], payload, sems.at[0])
+    copy.start()
+    copy.wait()
+
+
+def outside_kernel(first, entry, table, partial, area, wf, base, outside, held, weights, sems):
+    copies = (
+        pltpu.make_async_copy(wf.at[pl.ds(first, 2)], weights, sems.at[0]),
+        pltpu.make_async_copy(partial, held, sems.at[1]),
+    )
+    for copy in copies:
+        copy.start()
+    elems = outside.shape[0]
+    result = None
+    for n in range(2):
+        face = first + n
         take_rows(entry, face, table, outside, 0)
         rows = jnp.concatenate([table[face * elems : (face + 1) * elems, :], outside[...]], axis=1)
-        flux = stacked(wf[face], rows, 1)
+        if n == 0:
+            for copy in copies:
+                copy.wait()
+            result = held[...]
+        flux = stacked(weights[n], rows, 1)
         result = result - flux[0:ROWS] * area[face : face + 1, :]
     base[...] = result
 
@@ -317,14 +332,16 @@
     spread[...] = jnp.zeros(spread.shape, F32)
 
     def body(i, carry):
-        owner = seat[i * 4]
-        rows = [returned[pl.ds(owner * 4 + k, 1), :] for k in range(4)]
-        for k in range(4):
-            column = face[i * 4 + k]
+        rows = []
+        for n in range(4):
+            owner = jnp.maximum(seat[i * 16 + n * 4], 0)
+            rows += [returned[pl.ds(owner * 4 + k, 1), :] for k in range(4)]
+        for k in range(16):
+            column = face[i * 16 + k]
             spread[pl.ds(jnp.where(column >= 0, column, count), 1), :] = rows[k]
         return carry
 
-    lax.fori_loop(0, live_blocks(seat), body, 0)
+    lax.fori_loop(0, lax.shift_right_logical(live_blocks(seat) + 3, 2), body, 0)
     copy.wait()
     result = held[...]
     for at in range(4):
@@ -340,6 +357,10 @@
 def whole(count, smem=(), left=()):
     space = lambda i: SMEM if i in smem else pl.ANY if i in left else VMEM
     return [pl.BlockSpec(memory_space=space(i)) for i in range(count)]
+
+
+def local(array):
+    return pltpu.with_memory_space_constraint(array, VMEM)
 
 
 def shift(array, axis, by):
@@ -480,31 +501,34 @@
 
     faults, partial, top = lax.optimization_barrier((rupture_side_index, partial, top))
     extent = faces_total + 3072
-    payload = pl.pallas_call(
+    payload, table = pl.pallas_call(
         payload_kernel,
         in_specs=whole(7, (0, 1, 2), (3, 4, 5, 6)),
-        out_specs=whole(1)[0],
-        out_shape=shaped((devices * 8, LANES)),
-        scratch_shapes=[pltpu.VMEM((extent + 8, LANES), F32), pltpu.SemaphoreType.DMA((4,))],
+        out_specs=whole(2, (), (0,)),
+        out_shape=[shaped((devices * 8, LANES)), pltpu.VMEM((extent + 8, LANES), F32)],
+        scratch_shapes=[pltpu.VMEM((devices * 8 + 8, LANES), F32), pltpu.SemaphoreType.DMA((4,))],
         compiler_params=LIMIT,
         name="payload",
-    )(faults, rupture_seat_partition, entry, face_rows, group, lower, upper)
+    )(faults, rupture_seat_partition, entry, face_rows, local(group), local(lower), local(upper))
     arrived = lax.all_to_all(payload, ("wide", "narrow"), split_axis=0, concat_axis=0, tiled=True)
+
+    entry = boundary_entry_index
 
     def half(first, value):
         return pl.pallas_call(
             lambda *refs: outside_kernel(first, *refs),
-            in_specs=whole(8, (0,), (1, 2, 3, 4)),
+            in_specs=whole(5, (0,), (2, 4)),
             out_specs=whole(1)[0],
             out_shape=shaped((ROWS, elems)),
             scratch_shapes=[
-                pltpu.VMEM((extent, LANES), F32),
                 pltpu.VMEM((elems, LANES), F32),
-                pltpu.SemaphoreType.DMA((4,)),
+                pltpu.VMEM((ROWS, elems), F32),
+                pltpu.VMEM((2, 2 * PAD, 2 * LANES), BF16),
+                pltpu.SemaphoreType.DMA((2,)),
             ],
             compiler_params=LIMIT,
             name="outside" + str(first),
-        )(entry, face_rows, group, lower, upper, value, open_area, wf)
+        )(entry, local(table), value, open_area, wf)
 
     partial, payload = lax.optimization_barrier((partial, payload))
     base = half(0, partial)
@@ -518,7 +542,7 @@
         compiler_params=LIMIT,
         name="fault",
     )(
-        arrived, top, flat(earlier_sliding_speed), flat(instant_sensitivity_a),
+        local(arrived), top, flat(earlier_sliding_speed), flat(instant_sensitivity_a),
         flat(aging_memory_theta), wm, wp, vm, pair,
     )
     returned = lax.all_to_all(imposed, ("wide", "narrow"), split_axis=0, concat_axis=0, tiled=True)
@@ -537,7 +561,7 @@
         ],
         compiler_params=LIMIT,
         name="finish",
-    )(rupture_side_index, rupture_seat_partition, returned, base, surface_measure_quotient, ws)
+    )(rupture_side_index, rupture_seat_partition, local(returned), base, surface_measure_quotient, ws)
     return advanced, new_temperature, new_pressure, rate.reshape(points)
 
 

time: 121 us -> 126 us (1.041)
  local copies, waits for them, and re-layouts: 2.66 us -> 28.3 us
  Pallas kernels: 85.6 us -> 60.7 us
  starting transfers between devices: 27.6 us -> 30.7 us
    unnamed x14 -> x126, local copies, waits for them, and re-layouts: 2.66 us -> 28.3 us
    pallas_call x2, Pallas kernels: 21.6 us -> 14.1 us  [half(): pl.pallas_call(lambda *refs: outside_kernel(first, *refs), in_specs=whole...]
    pallas_call x1, Pallas kernels: 9.55 us -> 5.86 us  [per_device(): pl.pallas_call(payload_kernel, in_specs=whole(7, (0, 1, 2), (3, 4, 5, 6))...]
    all_to_all x1, starting transfers between devices: 10.1 us -> 13.1 us  [per_device(): lax.all_to_all(payload, ('wide', 'narrow'), split_axis=0, concat_axis=0,...]
    pallas_call x1, Pallas kernels: 5.42 us -> 2.85 us  [per_device(): pl.pallas_call(volume_kernel, grid=(elems // step,), in_specs=[column(ROW...]
    pallas_call x1, Pallas kernels: 7.98 us -> 5.98 us  [per_device(): pl.pallas_call(prepare_rest_kernel, in_specs=whole(16), out_specs=whole(7...]
    pallas_call x1, Pallas kernels: 12.2 us -> 10.3 us  [per_device(): pl.pallas_call(predictor_kernel, grid=(elems // step,), in_specs=[column(...]
    pallas_call x1, Pallas kernels: 5.8 us -> 4.03 us  [per_device(): pl.pallas_call(prepare_kernel, in_specs=whole(7), out_specs=whole(2), out...]
  transfers between devices with their start and end apart: 5 -> 5, of which waited for: 2 -> 2; matrix products, arithmetic and copies ran while one was open for 0% -> 0% of each run, Pallas kernels for 34% -> 22%
where the time goes in v3:
time: 126 us; the launch traced here: 125 us
  Pallas kernels  60.7 us (48%)
  starting transfers between devices  30.7 us (24%)
  local copies, waits for them, and re-layouts  28.3 us (22%)
  waiting for transfers between devices  3.65 us (3%)
  between operations  1.4 us (1%)
    unnamed x126, local copies, waits for them, and re-layouts  28.3 us
    pallas_call x2, Pallas kernels, half(): pl.pallas_call(lambda *refs: outside_kernel(first, *refs), in_specs=whole...  14.1 us
    all_to_all x1, starting transfers between devices, per_device(): lax.all_to_all(payload, ('wide', 'narrow'), split_axis=0, concat_axis=0,...  13.1 us
    pallas_call x1, Pallas kernels, per_device(): pl.pallas_call(predictor_kernel, grid=(elems // step,), in_specs=[column(...  10.3 us
    all_to_all x1, starting transfers between devices, per_device(): lax.all_to_all(imposed, ('wide', 'narrow'), split_axis=0, concat_axis=0,...  6.66 us
    pallas_call x1, Pallas kernels, per_device(): pl.pallas_call(finish_kernel, in_specs=whole(6, (0, 1), (3,)), out_specs=...  6.22 us
    pallas_call x1, Pallas kernels, per_device(): pl.pallas_call(prepare_rest_kernel, in_specs=whole(16), out_specs=whole(7...  5.98 us
    ppermute x2, starting transfers between devices, shift(): return lax.ppermute(array, axis, pairs)  5.95 us
  transfers between devices with their start and end apart: 5, of which 2 were waited for; matrix products, arithmetic and copies ran while one was open for 0% of the time, Pallas kernels for 22%

profile of v3, /device:TPU:1, one launch (start us, length us, event | category | flops | bytes accessed | tf_op | source)
XLA Modules:
  0.0 124.7 jit_solution(13736092470003369733)
XLA Ops:
  0.6 0.0 copy-start.18
  0.6 0.9 copy-done.18
  1.5 0.9 copy-done.20
  2.4 0.8 copy-done.25
  3.3 0.8 copy-done.27
  4.1 0.7 copy-done.38
  4.8 0.8 copy-done.44
  5.6 0.7 copy-done.54
  6.3 4.0 %prepare.1 = (bf16[1152,180]{1,0:T(8,128)(2,1)S(1)}, bf16[2,180,512]{2,1,0:T(8,128)(2,1)S(1)}) custom-call(f32[9,3,9]{2,1,0:T(4,128)S(1)} %bitcast.23, f32[3,20,20]{2,1,0:T(8,128)S(1)} %copy-done.44, f32[10,4,20]{2,1,0:T(4,128)S(1)} %bitcast.27, f32[180,9]{1,0:T(8,128)S(1)} %copy-done.20, f32[180,20]{1,0:T(8,128)S(1)} %copy-done.18, ...), custom_call_target="tpu_custom_call" | custom-call | tf_op jit(solution)/shard_map/prepare/pallas_call | solution.py:404
  10.4 0.0 copy-start.5
  10.4 1.4 %copy-done.5 = f32[180,2048]{1,0:T(8,128)S(1)} copy-done((f32[180,2048]{1,0:T(8,128)S(1)}, f32[180,2048]{1,0:T(8,128)}, u32[]{:S(2)}) %copy-start.5) | copy-done | bytes 1474584
  11.7 0.8 copy-done.31
  12.5 10.3 %predictor.1 = (f32[180,2048]{1,0:T(8,128)S(1)}, f32[4,2048,128]{2,1,0:T(8,128)S(1)}) custom-call(f32[180,2048]{1,0:T(8,128)S(1)} %copy-done.5, f32[3,2048]{1,0:T(4,128)S(1)} %copy-done.31, bf16[1152,180]{1,0:T(8,128)(2,1)S(1)} %get-tuple-element.35.mp, bf16[2,180,512]{2,1,0:T(8,128)(2,1)S(1)} %get-tuple-element.36.wt), custom_call_target="tpu_custom_call" | custom-call | tf_op jit(solution)/shard_map/predictor/pallas_call | solution.py:418
  22.9 0.0 copy-start.14
  22.9 1.1 copy-done.14
  24.0 0.0 copy-start.55
  24.0 0.0 copy-start.58
  24.0 0.0 copy-start.60
  24.0 0.0 copy-start.61
  24.0 4.5 %halo_rows.1 = (f32[2048,128]{1,0:T(8,128)}, f32[512,128]{1,0:T(8,128)}, f32[512,128]{1,0:T(8,128)}) custom-call(s32[6,512]{1,0:T(8,128)S(1)} %copy-done.57, f32[8192,128]{1,0:T(8,128)S(1)} %bitcast.17), custom_call_target="tpu_custom_call" | custom-call | tf_op jit(solution)/shard_map/halo_rows/pallas_call | solution.py:430
  28.6 0.0 copy-start.28
  28.6 0.0 copy-start.35
  28.6 0.0 copy-start.37
  28.6 0.0 copy-start.39
  28.7 0.0 copy-start.42
  28.7 0.0 copy-start.56
  28.7 0.0 copy-start.62
  28.7 0.0 copy-start.6
  28.7 5.0 %all-to-all-start = ((f32[4,512,128]{2,1,0:T(8,128)}), f32[4,512,128]{2,1,0:T(8,128)}, u32[]{:S(2)}, u32[]{:S(2)}) async-start(f32[4,512,128]{2,1,0:T(8,128)} %bitcast.7), calls=%async_computation | async-start | bytes 2097152 | tf_op jit(solution)/shard_map/all_to_all | solution.py:438
  33.7 2.9 %collective-permute-start.1 = (f32[512,128]{1,0:T(8,128)}, f32[512,128]{1,0:T(8,128)S(1)}, u32[]{:S(2)}, u32[]{:S(2)}) collective-permute-start(f32[512,128]{1,0:T(8,128)} %get-tuple-element.46), channel_id=1, source_target_pairs={{4,0},{8,4},{12,8},{16,12},{20,16},{24,20},{28,24},{32,28},{36,32}... | collective-permute-start | bytes 786440 | tf_op jit(solution)/shard_map/ppermute | solution.py:369
  36.6 3.1 %collective-permute-start = (f32[512,128]{1,0:T(8,128)}, f32[512,128]{1,0:T(8,128)S(1)}, u32[]{:S(2)}, u32[]{:S(2)}) collective-permute-start(f32[512,128]{1,0:T(8,128)} %get-tuple-element.39), channel_id=1, source_target_pairs={{0,4},{4,8},{8,12},{12,16},{16,20},{20,24},{24,28},{28,32},{32,36}... | collective-permute-start | bytes 786440 | tf_op jit(solution)/shard_map/ppermute | solution.py:369
  39.8 6.0 %prepare_rest.1 = (f32[4,2048]{1,0:T(4,128)S(1)}, bf16[1152,180]{1,0:T(8,128)(2,1)S(1)}, bf16[4,384,256]{2,1,0:T(8,128)(2,1)S(1)}, bf16[4,384,128]{2,1,0:T(8,128...) custom-call(s32[1,512]{1,0:T(1,128)S(1)} %bitcast.29, ...), custom_call_target="tpu_custom_call" | custom-call | tf_op jit(solution)/shard_map/prepare_rest/pallas_call | solution.py:445
  45.8 0.9 copy-done.9
  46.7 0.7 copy-done.29
  47.4 0.6 copy-done.40
  48.0 1.5 %copy-done.15 = f32[180,2048]{1,0:T(8,128)S(1)} copy-done((f32[180,2048]{1,0:T(8,128)S(1)}, f32[180,2048]{1,0:T(8,128)}, u32[]{:S(2)}) %copy-start.15) | copy-done | bytes 1474584
  49.6 0.0 copy-start.47
  49.6 0.0 copy-start.48
  49.6 2.8 %volume.1.refs_2_ = f32[180,2048]{1,0:T(8,128)S(1)} custom-call(f32[180,2048]{1,0:T(8,128)S(1)} %copy-done.6, f32[3,2048]{1,0:T(4,128)S(1)} %copy-done.32, f32[180,2048]{1,0:T(8,128)S(1)} %copy-done.15, bf16[1152,180]{1,0:T(8,128)(2,1)S(1)} %get-tuple-element.41.mi), custom_call_target="tpu_custom_call" | custom-call | tf_op jit(solution)/shard_map/volume/pallas_call | solution.py:492
  52.5 0.0 copy-start.22
  52.5 4.1 %thermal.1 = (f32[64,8192]{1,0:T(8,128)}, f32[64,8192]{1,0:T(8,128)}, f32[64,128]{1,0:T(8,128)S(1)}) custom-call(f32[64,8192]{1,0:T(8,128)S(1)} %copy-done.12, f32[64,8192]{1,0:T(8,128)S(1)} %copy-done.13, f32[1,8192]{1,0:T(1,128)S(1)} %bitcast.21, f32[64,1]{1,0:T(8,128)S(1)} %copy-done.48, f32[64,64]{1,0:T(8,128)S(1)} %copy-done.46, f32[64,64]{1,0:T(8,128)S(1)} %copy-done.47), custom_call_target="tpu_custom_call" | custom-call | tf_op jit(solution)/shard_map/thermal/pallas_call | solution.py:476
  56.6 0.6 copy-done.52
  57.2 0.7 copy-done.23
  58.0 2.2 %copy-done.4 = f32[4,2048,128]{2,1,0:T(8,128)S(1)} copy-done((f32[4,2048,128]{2,1,0:T(8,128)S(1)}, f32[4,2048,128]{2,1,0:T(8,128)}, u32[]{:S(2)}) %copy-start.4) | copy-done | bytes 4194328
  60.1 0.9 copy-done.24
  61.1 5.9 %payload.1 = (f32[1024,128]{1,0:T(8,128)}, f32[11272,128]{1,0:T(8,128)S(1)}) custom-call(s32[512]{0:T(512)S(1)} %copy-done.56, s32[512]{0:T(512)S(1)} %copy-done.59, s32[4,2048]{1,0:T(4,128)S(1)} %copy-done.22, f32[8192,128]{1,0:T(8,128)S(1)} %bitcast.18, f32[2048,128]{1,0:T(8,128)} %bitcast.8.group, f32[512,128]{1,0:T(8,128)S(1)} %copy-done.24, ...), custom_call_target="tpu_custom_call" | custom-call | tf_op jit(solution)/shard_map/payload/pallas_call | solution.py:504
  67.0 2.5 %copy-done = f32[11272,128]{1,0:T(8,128)} copy-done((f32[11272,128]{1,0:T(8,128)}, f32[11272,128]{1,0:T(8,128)S(1)}, u32[]{:S(2)}) %copy-start) | copy-done | bytes 5771288
  69.5 13.1 %all-to-all-start.1 = ((f32[128,8,128]{2,1,0:T(8,128)}), f32[128,8,128]{2,1,0:T(8,128)S(1)}, u32[]{:S(2)}, u32[]{:S(2)}) async-start(f32[128,8,128]{2,1,0:T(8,128)} %bitcast.9), calls=%async_computation.1 | async-start | bytes 1048576 | tf_op jit(solution)/shard_map/all_to_all | solution.py:513
  82.6 2.6 %copy-done.1 = f32[11272,128]{1,0:T(8,128)S(1)} copy-done((f32[11272,128]{1,0:T(8,128)S(1)}, f32[11272,128]{1,0:T(8,128)}, u32[]{:S(2)}) %copy-start.1) | copy-done | bytes 5771288
  85.2 0.0 copy-start.50
  85.3 0.0 copy-start.51
  85.3 0.0 copy-start.53
  85.3 7.0 %outside0.1.refs_2_ = f32[180,2048]{1,0:T(8,128)S(1)} custom-call(s32[4,2048]{1,0:T(4,128)S(1)} %copy-done.22, f32[11272,128]{1,0:T(8,128)S(1)} %copy-done.1, f32[180,2048]{1,0:T(8,128)S(1)} %volume.1.refs_2_, f32[4,2048]{1,0:T(4,128)S(1)} %get-tuple-element.51.refs_3_, bf16[4,384,256]{2,1,0:T(8,128)(2,1)S(1)} %copy-done.10), custom_call_target="tpu_custom_call" | custom-call | tf_op jit(solution)/shard_map/outside0/pallas_call | solution.py:518
  92.3 0.0 copy-start.7
  92.3 1.1 copy-done.7
  93.4 3.1 %all-to-all-done.1 = f32[128,8,128]{2,1,0:T(8,128)S(1)} async-done(((f32[128,8,128]{2,1,0:T(8,128)}), f32[128,8,128]{2,1,0:T(8,128)S(1)}, u32[]{:S(2)}, u32[]{:S(2)}) %all-to-all-start.1) | async-done | bytes 524320 | tf_op jit(solution)/shard_map/all_to_all | solution.py:513
  96.6 2.7 %fault.1 = (f32[512,128]{1,0:T(8,128)}, f32[64,128]{1,0:T(8,128)}) custom-call(f32[1024,128]{1,0:T(8,128)S(1)} %bitcast.19, f32[64,128]{1,0:T(8,128)S(1)} %copy-done.53, f32[64,128]{1,0:T(8,128)S(1)} %bitcast.22, f32[64,128]{1,0:T(8,128)S(1)} %bitcast.25, f32[64,128]{1,0:T(8,128)S(1)} %bitcast.26, f32[128,384]{1,0:T(8,128)S(1)} %get-tuple-element.55.wm, ...), custom_call_target="tpu_custom_call" | custom-call | tf_op jit(solution)/shard_map/fault/pallas_call | solution.py:537
  99.3 6.7 %all-to-all-start.2 = ((f32[128,4,128]{2,1,0:T(4,128)}), f32[128,4,128]{2,1,0:T(4,128)S(1)}, u32[]{:S(2)}, u32[]{:S(2)}) async-start(f32[128,4,128]{2,1,0:T(4,128)} %bitcast.14), calls=%async_computation.2 | async-start | bytes 524288 | tf_op jit(solution)/shard_map/all_to_all | solution.py:548
  106.0 2.6 %copy-done.2 = f32[11272,128]{1,0:T(8,128)S(1)} copy-done((f32[11272,128]{1,0:T(8,128)S(1)}, f32[11272,128]{1,0:T(8,128)}, u32[]{:S(2)}) %copy-start.2) | copy-done | bytes 5771288
  108.6 1.1 copy-done.11
  109.8 7.0 %outside2.1.base = f32[180,2048]{1,0:T(8,128)S(1)} custom-call(s32[4,2048]{1,0:T(4,128)S(1)} %copy-done.22, f32[11272,128]{1,0:T(8,128)S(1)} %copy-done.2, f32[180,2048]{1,0:T(8,128)S(1)} %copy-done.8, f32[4,2048]{1,0:T(4,128)S(1)} %get-tuple-element.51.refs_3_, bf16[4,384,256]{2,1,0:T(8,128)(2,1)S(1)} %copy-done.11), custom_call_target="tpu_custom_call" | custom-call | tf_op jit(solution)/shard_map/outside2/pallas_call | solution.py:518
  116.8 0.5 all-to-all-done.2
  117.4 1.0 copy-done.17
  118.4 6.2 %finish.1 = f32[180,2048]{1,0:T(8,128)} custom-call(s32[512]{0:T(512)S(1)} %copy-done.56, s32[512]{0:T(512)S(1)} %copy-done.59, f32[512,128]{1,0:T(8,128)S(1)} %bitcast.20, f32[180,2048]{1,0:T(8,128)S(1)} %outside2.1.base, f32[4,2048]{1,0:T(4,128)S(1)} %copy-done.36, bf16[4,384,128]{2,1,0:T(8,128)(2,1)S(1)} %copy-done.17), custom_call_target="tpu_custom_call" | custom-call | tf_op jit(solution)/shard_map/finish/pallas_call | solution.py:552
  (83 shorter events, 0.2 us)
Async XLA Ops:
  0.6 0.9 copy-start.18
  1.5 0.9 copy-start.20
  2.4 0.8 copy-start.25
  3.3 0.8 copy-start.27
  4.1 0.7 copy-start.38
  4.8 0.8 copy-start.44
  5.6 0.7 copy-start.54
  6.3 17.7 %copy-start.57 = (s32[6,512]{1,0:T(8,128)S(1)}, s32[6,512]{1,0:T(8,128)}, u32[]{:S(2)}) copy-start(s32[6,512]{1,0:T(8,128)} %index.1) | copy-start | bytes 36868
  10.4 1.4 %copy-start.5 = (f32[180,2048]{1,0:T(8,128)S(1)}, f32[180,2048]{1,0:T(8,128)}, u32[]{:S(2)}) copy-start(f32[180,2048]{1,0:T(8,128)} %u.3) | copy-start | bytes 4423684
  11.7 0.8 copy-start.31
  22.9 1.1 copy-start.14
  24.0 4.6 %copy-start.3 = (f32[4,2048,128]{2,1,0:T(8,128)}, f32[4,2048,128]{2,1,0:T(8,128)S(1)}, u32[]{:S(2)}) copy-start(f32[4,2048,128]{2,1,0:T(8,128)S(1)} %get-tuple-element.38) | copy-start | bytes 12582916
  24.0 15.7 %copy-start.43 = (f32[128,16]{1,0:T(8,128)S(1)}, f32[128,16]{1,0:T(8,128)}, u32[]{:S(2)}) copy-start(f32[128,16]{1,0:T(8,128)} %constant.24.clone.tile) | copy-start | bytes 24580
  24.0 15.7 %copy-start.45 = (f32[3,20,20]{2,1,0:T(8,128)S(1)}, f32[3,20,20]{2,1,0:T(8,128)}, u32[]{:S(2)}) copy-start(f32[3,20,20]{2,1,0:T(8,128)} %kd.1) | copy-start | bytes 14404
  24.0 15.7 %copy-start.55 = (f32[4,20,10]{1,0,2:T(4,128)S(1)}, f32[4,20,10]{1,0,2:T(4,128)}, u32[]{:S(2)}) copy-start(f32[4,20,10]{1,0,2:T(4,128)} %param.39) | copy-start | bytes 9604
  24.0 15.7 %copy-start.58 = (f32[2,9,9]{2,0,1:T(2,128)S(1)}, f32[2,9,9]{2,0,1:T(2,128)}, u32[]{:S(2)}) copy-start(f32[2,9,9]{2,0,1:T(2,128)} %param.40) | copy-start | bytes 1948
  24.0 15.7 %copy-start.60 = (f32[16,10]{1,0:T(8,128)S(1)}, f32[16,10]{1,0:T(8,128)}, u32[]{:S(2)}) copy-start(f32[16,10]{1,0:T(8,128)} %bp.1) | copy-start | bytes 1924
  24.0 15.7 %copy-start.61 = (f32[16,10]{1,0:T(8,128)S(1)}, f32[16,10]{1,0:T(8,128)}, u32[]{:S(2)}) copy-start(f32[16,10]{1,0:T(8,128)} %qg.1) | copy-start | bytes 1924
  28.6 11.1 %copy-start.19 = (f32[180,20]{1,0:T(8,128)S(1)}, f32[180,20]{1,0:T(8,128)}, u32[]{:S(2)}) copy-start(f32[180,20]{1,0:T(8,128)} %constant.21.clone.f) | copy-start | bytes 43204
  28.6 11.1 %copy-start.21 = (f32[180,9]{1,0:T(8,128)S(1)}, f32[180,9]{1,0:T(8,128)}, u32[]{:S(2)}) copy-start(f32[180,9]{1,0:T(8,128)} %constant.20.clone.e) | copy-start | bytes 19444
  28.6 11.2 %copy-start.26 = (f32[128,10]{1,0:T(8,128)S(1)}, f32[128,10]{1,0:T(8,128)}, u32[]{:S(2)}) copy-start(f32[128,10]{1,0:T(8,128)} %constant.23.clone.h) | copy-start | bytes 15364
  28.6 11.2 %copy-start.28 = (f32[128,9]{1,0:T(8,128)S(1)}, f32[128,9]{1,0:T(8,128)}, u32[]{:S(2)}) copy-start(f32[128,9]{1,0:T(8,128)} %constant.22.clone.g) | copy-start | bytes 13828
  28.6 11.2 %copy-start.35 = (f32[4,2048]{1,0:T(4,128)S(1)}, f32[4,2048]{1,0:T(4,128)}, u32[]{:S(2)}) copy-start(f32[4,2048]{1,0:T(4,128)} %area.3) | copy-start | bytes 98308
  28.6 11.2 %copy-start.37 = (f32[2,128,128]{2,1,0:T(8,128)S(1)}, f32[2,128,128]{2,1,0:T(8,128)}, u32[]{:S(2)}) copy-start(f32[2,128,128]{2,1,0:T(8,128)} %constant.26.clone.linear) | copy-start | bytes 393220
  28.6 11.2 %copy-start.39 = (f32[3,9,9]{2,0,1:T(4,128)S(1)}, f32[3,9,9]{2,0,1:T(4,128)}, u32[]{:S(2)}) copy-start(f32[3,9,9]{2,0,1:T(4,128)} %param.35) | copy-start | bytes 2920
  28.7 11.1 %copy-start.42 = (f32[128,4]{1,0:T(8,128)S(1)}, f32[128,4]{1,0:T(8,128)}, u32[]{:S(2)}) copy-start(f32[128,4]{1,0:T(8,128)} %constant.25.clone.side) | copy-start | bytes 6148
  28.7 11.1 %copy-start.56 = (s32[512]{0:T(512)S(1)}, s32[512]{0:T(512)}, u32[]{:S(2)}) copy-start(s32[512]{0:T(512)} %face.2) | copy-start | bytes 6148
  28.7 11.1 %copy-start.62 = (f32[1,128]{1,0:T(1,128)S(1)}, f32[1,128]{1,0:T(1,128)}, u32[]{:S(2)}) copy-start(f32[1,128]{1,0:T(1,128)} %constant.27.clone.slip) | copy-start | bytes 1540
  28.7 19.3 %copy-start.6 = (f32[180,2048]{1,0:T(8,128)S(1)}, f32[180,2048]{1,0:T(8,128)}, u32[]{:S(2)}) copy-start(f32[180,2048]{1,0:T(8,128)} %u.3) | copy-start | bytes 4423684
  28.7 19.3 %copy-start.32 = (f32[3,2048]{1,0:T(4,128)S(1)}, f32[3,2048]{1,0:T(4,128)}, u32[]{:S(2)}) copy-start(f32[3,2048]{1,0:T(4,128)} %t.3) | copy-start | bytes 73732
  28.7 29.2 %all-to-all-start = ((f32[4,512,128]{2,1,0:T(8,128)}), f32[4,512,128]{2,1,0:T(8,128)}, u32[]{:S(2)}, u32[]{:S(2)}) async-start(f32[4,512,128]{2,1,0:T(8,128)} %bitcast.7), calls=%async_computation | async-start | bytes 2097152 | tf_op jit(solution)/shard_map/all_to_all | solution.py:438
  33.7 23.5 %collective-permute-start.1 = (f32[512,128]{1,0:T(8,128)}, f32[512,128]{1,0:T(8,128)S(1)}, u32[]{:S(2)}, u32[]{:S(2)}) collective-permute-start(f32[512,128]{1,0:T(8,128)} %get-tuple-element.46), channel_id=1, source_target_pairs={{4,0},{8,4},{12,8},{16,12},{20,16},{24,20},{28,24},{32,28},{36,32}... | collective-permute-start | bytes 786440 | tf_op jit(solution)/shard_map/ppermute | solution.py:369
  36.6 20.7 %collective-permute-start = (f32[512,128]{1,0:T(8,128)}, f32[512,128]{1,0:T(8,128)S(1)}, u32[]{:S(2)}, u32[]{:S(2)}) collective-permute-start(f32[512,128]{1,0:T(8,128)} %get-tuple-element.39), channel_id=1, source_target_pairs={{0,4},{4,8},{8,12},{12,16},{16,20},{20,24},{24,28},{28,32},{32,36}... | collective-permute-start | bytes 786440 | tf_op jit(solution)/shard_map/ppermute | solution.py:369
  45.8 0.9 copy-start.9
  48.0 4.4 %copy-start.16 = (bf16[4,384,128]{2,1,0:T(8,128)(2,1)}, bf16[4,384,128]{2,1,0:T(8,128)(2,1)S(1)}, u32[]{:S(2)}) copy-start(bf16[4,384,128]{2,1,0:T(8,128)(2,1)S(1)} %get-tuple-element.62.ws) | copy-start | bytes 1179652
  48.0 1.5 %copy-start.15 = (f32[180,2048]{1,0:T(8,128)S(1)}, f32[180,2048]{1,0:T(8,128)}, u32[]{:S(2)}) copy-start(f32[180,2048]{1,0:T(8,128)} %copy-done.14) | copy-start | bytes 4423684
  49.6 2.9 %copy-start.12 = (f32[64,8192]{1,0:T(8,128)S(1)}, f32[64,8192]{1,0:T(8,128)}, u32[]{:S(2)}) copy-start(f32[64,8192]{1,0:T(8,128)} %th.1) | copy-start | bytes 6291460
  49.6 2.9 %copy-start.13 = (f32[64,8192]{1,0:T(8,128)S(1)}, f32[64,8192]{1,0:T(8,128)}, u32[]{:S(2)}) copy-start(f32[64,8192]{1,0:T(8,128)} %fl.1) | copy-start | bytes 6291460
  49.6 2.9 %copy-start.33 = (f32[8192]{0:T(1024)S(1)}, f32[8192]{0:T(1024)}, u32[]{:S(2)}) copy-start(f32[8192]{0:T(1024)} %param.47) | copy-start | bytes 98308
  49.6 2.9 %copy-start.46 = (f32[64,64]{1,0:T(8,128)S(1)}, f32[64,64]{1,0:T(8,128)}, u32[]{:S(2)}) copy-start(f32[64,64]{1,0:T(8,128)} %tr) | copy-start | bytes 49156
  49.6 2.9 %copy-start.47 = (f32[64,64]{1,0:T(8,128)S(1)}, f32[64,64]{1,0:T(8,128)}, u32[]{:S(2)}) copy-start(f32[64,64]{1,0:T(8,128)} %hr.1) | copy-start | bytes 49156
  49.6 2.9 %copy-start.48 = (f32[64,1]{1,0:T(8,128)S(1)}, f32[64,1]{1,0:T(8,128)}, u32[]{:S(2)}) copy-start(f32[64,1]{1,0:T(8,128)} %constant.28.clone.shape) | copy-start | bytes 772
  52.5 5.4 %copy-start.22 = (s32[4,2048]{1,0:T(4,128)S(1)}, s32[4,2048]{1,0:T(4,128)}, u32[]{:S(2)}) copy-start(s32[4,2048]{1,0:T(4,128)} %refs_0_.3) | copy-start | bytes 98308
  52.5 5.4 %copy-start.59 = (s32[512]{0:T(512)S(1)}, s32[512]{0:T(512)}, u32[]{:S(2)}) copy-start(s32[512]{0:T(512)} %seat.3) | copy-start | bytes 6148
  57.9 2.2 %copy-start.4 = (f32[4,2048,128]{2,1,0:T(8,128)S(1)}, f32[4,2048,128]{2,1,0:T(8,128)}, u32[]{:S(2)}) copy-start(f32[4,2048,128]{2,1,0:T(8,128)} %copy-done.3) | copy-start | bytes 12582916
  60.1 0.9 copy-start.24
  61.1 21.5 %copy-start.10 = (bf16[4,384,256]{2,1,0:T(8,128)(2,1)S(1)}, bf16[4,384,256]{2,1,0:T(8,128)(2,1)}, u32[]{:S(2)}) copy-start(bf16[4,384,256]{2,1,0:T(8,128)(2,1)} %copy-done.9) | copy-start | bytes 2359300
  67.0 2.5 %copy-start = (f32[11272,128]{1,0:T(8,128)}, f32[11272,128]{1,0:T(8,128)S(1)}, u32[]{:S(2)}) copy-start(f32[11272,128]{1,0:T(8,128)S(1)} %get-tuple-element.48.refs_1_) | copy-start | bytes 17313796
  69.5 27.1 %all-to-all-start.1 = ((f32[128,8,128]{2,1,0:T(8,128)}), f32[128,8,128]{2,1,0:T(8,128)S(1)}, u32[]{:S(2)}, u32[]{:S(2)}) async-start(f32[128,8,128]{2,1,0:T(8,128)} %bitcast.9), calls=%async_computation.1 | async-start | bytes 1048576 | tf_op jit(solution)/shard_map/all_to_all | solution.py:513
  82.6 2.6 %copy-start.1 = (f32[11272,128]{1,0:T(8,128)S(1)}, f32[11272,128]{1,0:T(8,128)}, u32[]{:S(2)}) copy-start(f32[11272,128]{1,0:T(8,128)} %copy-done) | copy-start | bytes 17313796
  85.2 11.3 %copy-start.30 = (f32[128,384]{1,0:T(8,128)S(1)}, f32[128,384]{1,0:T(8,128)}, u32[]{:S(2)}) copy-start(f32[128,384]{1,0:T(8,128)} %copy-done.29) | copy-start | bytes 589828
  85.2 11.3 %copy-start.34 = (f32[8192]{0:T(1024)S(1)}, f32[8192]{0:T(1024)}, u32[]{:S(2)}) copy-start(f32[8192]{0:T(1024)} %param.47) | copy-start | bytes 98308
  85.2 11.3 %copy-start.41 = (f32[128,128]{1,0:T(8,128)S(1)}, f32[128,128]{1,0:T(8,128)}, u32[]{:S(2)}) copy-start(f32[128,128]{1,0:T(8,128)} %copy-done.40) | copy-start | bytes 196612
  85.2 11.3 %copy-start.49 = (f32[8192]{0:T(1024)S(1)}, f32[8192]{0:T(1024)}, u32[]{:S(2)}) copy-start(f32[8192]{0:T(1024)} %param.48) | copy-start | bytes 98308
  85.2 11.3 %copy-start.50 = (f32[8192]{0:T(1024)S(1)}, f32[8192]{0:T(1024)}, u32[]{:S(2)}) copy-start(f32[8192]{0:T(1024)} %param.49) | copy-start | bytes 98308
  85.3 11.3 %copy-start.51 = (f32[64,128]{1,0:T(8,128)S(1)}, f32[64,128]{1,0:T(8,128)}, u32[]{:S(2)}) copy-start(f32[64,128]{1,0:T(8,128)} %constant.29.clone.pair) | copy-start | bytes 98308
  85.3 11.3 %copy-start.53 = (f32[64,128]{1,0:T(8,128)S(1)}, f32[64,128]{1,0:T(8,128)}, u32[]{:S(2)}) copy-start(f32[64,128]{1,0:T(8,128)} %copy-done.52) | copy-start | bytes 98308
  92.3 1.1 copy-start.7
  96.6 9.4 %copy-start.8 = (f32[180,2048]{1,0:T(8,128)S(1)}, f32[180,2048]{1,0:T(8,128)}, u32[]{:S(2)}) copy-start(f32[180,2048]{1,0:T(8,128)} %copy-done.7) | copy-start | bytes 4423684
  99.3 18.0 %all-to-all-start.2 = ((f32[128,4,128]{2,1,0:T(4,128)}), f32[128,4,128]{2,1,0:T(4,128)S(1)}, u32[]{:S(2)}, u32[]{:S(2)}) async-start(f32[128,4,128]{2,1,0:T(4,128)} %bitcast.14), calls=%async_computation.2 | async-start | bytes 524288 | tf_op jit(solution)/shard_map/all_to_all | solution.py:548
  106.0 2.6 %copy-start.2 = (f32[11272,128]{1,0:T(8,128)S(1)}, f32[11272,128]{1,0:T(8,128)}, u32[]{:S(2)}) copy-start(f32[11272,128]{1,0:T(8,128)} %copy-done) | copy-start | bytes 17313796
  108.6 1.1 copy-start.11
  109.8 7.6 %copy-start.36 = (f32[4,2048]{1,0:T(4,128)S(1)}, f32[4,2048]{1,0:T(4,128)}, u32[]{:S(2)}) copy-start(f32[4,2048]{1,0:T(4,128)} %area.3) | copy-start | bytes 98308
  117.4 1.0 copy-start.17
  (4 other events, 2.6 us)

commit v4 on v3

--- a/solution.py
+++ b/solution.py
@@ -16,7 +16,7 @@
 BF16 = jnp.bfloat16
 VMEM = pltpu.MemorySpace.VMEM
 SMEM = pltpu.MemorySpace.SMEM
-LIMIT = pltpu.CompilerParams(vmem_limit_bytes=24 * 1024 * 1024)
+LIMIT = pltpu.CompilerParams(vmem_limit_bytes=56 * 1024 * 1024)
 
 
 def tables():
@@ -113,8 +113,8 @@
 
 
 def prepare_rest_kernel(
-    face, area, a, kd, sr, rt, bp, qg, e, f, g, h, tile, side, linear, slip,
-    open_area, mi, wf, ws, wm, wp, vm,
+    face, area, sr, rt, bp, qg, e, f, g, h, tile, side, linear, slip,
+    open_area, wf, ws, wm, wp, vm,
 ):
     e_, f_, g_, h_ = e[...], f[...], g[...], h[...]
     eb, fb = e_.astype(BF16), f_.astype(BF16)
@@ -128,12 +128,8 @@
     for r in range(64):
         at = (slice(r // 16, r // 16 + 1), slice(r % 16 * LANES, (r % 16 + 1) * LANES))
         open_area[at] = jnp.where(closed[r : r + 1] > 0.5, 0.0, area[at])
-    mi[...] = jnp.zeros(mi.shape, BF16)
     wf[...] = jnp.zeros(wf.shape, BF16)
     ws[...] = jnp.zeros(ws.shape, BF16)
-    for d in range(3):
-        left = grid_of(eb, a[:, d, :], e_)
-        put(mi, ((), d * PAD, 0), left * grid_of(fb, kd[d], f_), 3 * PAD)
     r0 = grid_of(eb, rt[:, 0, :], g_)
     r1 = grid_of(eb, rt[:, 1, :], g_)
     for n in range(4):
@@ -159,7 +155,11 @@
     )
 
 
-def predictor_kernel(u, t, mp, wt, integral, faces, padded):
+def predictor_kernel(u, t, a, pd, rs, e, f, g, h, integral, faces, padded, mp, wt):
+    @pl.when(pl.program_id(0) == 0)
+    def _():
+        prepare_kernel(a, pd, rs, e, f, g, h, mp, wt)
+
     times = t[...]
     current = u[...]
     total = current
@@ -177,7 +177,16 @@
         faces[face] = rows[:, face * LANES : (face + 1) * LANES]
 
 
-def volume_kernel(u, t, integral, mi, partial):
+def volume_kernel(u, t, integral, a, kd, e, f, partial, mi):
+    @pl.when(pl.program_id(0) == 0)
+    def _():
+        e_, f_ = e[...], f[...]
+        eb, fb = e_.astype(BF16), f_.astype(BF16)
+        mi[...] = jnp.zeros(mi.shape, BF16)
+        for d in range(3):
+            left = grid_of(eb, a[:, d, :], e_)
+            put(mi, ((), d * PAD, 0), left * grid_of(fb, kd[d], f_), 3 * PAD)
+
     partial[...] = u[...] + directional(mi[...], integral[...], t[...])
 
 
@@ -233,7 +242,7 @@
     )
 
 
-def payload_kernel(face, seat, entry, faces, group, lower, upper, payload, table, buffer, sems):
+def payload_kernel(face, seat, entry, faces, group, lower, upper, payload, buffer, table, sems):
     extent = table.shape[0] - 8
     buffer[...] = jnp.zeros(buffer.shape, F32)
     table[extent : extent + 8, :] = jnp.zeros((8, LANES), F32)
@@ -264,11 +273,15 @@
     copy.wait()
 
 
-def outside_kernel(first, entry, table, partial, area, wf, base, outside, held, weights, sems):
+def outside_kernel(
+    first, entry, faces, group, lower, upper, partial, area, wf, base,
+    table, outside, held, weights, sems, others,
+):
     copies = (
-        pltpu.make_async_copy(wf.at[pl.ds(first, 2)], weights, sems.at[0]),
-        pltpu.make_async_copy(partial, held, sems.at[1]),
-    )
+        pltpu.make_async_copy(wf.at[pl.ds(first, 2)], weights, others.at[0]),
+        pltpu.make_async_copy(partial, held, others.at[1]),
+    )
+    fill(table, (faces, group, lower, upper), sems)
     for copy in copies:
         copy.start()
     elems = outside.shape[0]
@@ -357,10 +370,6 @@
 def whole(count, smem=(), left=()):
     space = lambda i: SMEM if i in smem else pl.ANY if i in left else VMEM
     return [pl.BlockSpec(memory_space=space(i)) for i in range(count)]
-
-
-def local(array):
-    return pltpu.with_memory_space_constraint(array, VMEM)
 
 
 def shift(array, axis, by):
@@ -401,30 +410,29 @@
     entry = boundary_entry_index
     elastic = jnp.transpose(elastic_directional_derivs, (1, 0, 2))
 
-    mp, wt = pl.pallas_call(
-        prepare_kernel,
-        in_specs=whole(7),
-        out_specs=whole(2),
-        out_shape=[shaped((6 * PAD, ROWS), BF16), shaped((2, ROWS, 4 * LANES), BF16)],
-        compiler_params=LIMIT,
-        name="prepare",
-    )(
-        elastic, predictor_derivatives, jnp.transpose(interior_restriction, (1, 0, 2)), e, f, g, h
-    )
-
     step = 512
     column = lambda rows: pl.BlockSpec((rows, step), lambda i: (0, i))
     fixed = lambda shape: pl.BlockSpec(shape, lambda i: (0,) * len(shape))
     integral, face_rows = pl.pallas_call(
         predictor_kernel,
         grid=(elems // step,),
-        in_specs=[column(ROWS), column(3), fixed((6 * PAD, ROWS)), fixed((2, ROWS, 4 * LANES))],
+        in_specs=[
+            column(ROWS), column(3), fixed((Q, 3, Q)), fixed((3, NB, NB)), fixed((NJ, 4, NB)),
+            fixed((ROWS, Q)), fixed((ROWS, NB)), fixed((LANES, Q)), fixed((LANES, NJ)),
+        ],
         out_specs=[column(ROWS), pl.BlockSpec((4, step, LANES), lambda i: (0, i, 0))],
         out_shape=[shaped((ROWS, elems)), shaped((4, elems, LANES))],
-        scratch_shapes=[pltpu.VMEM((256, step), F32)],
+        scratch_shapes=[
+            pltpu.VMEM((256, step), F32),
+            pltpu.VMEM((6 * PAD, ROWS), BF16),
+            pltpu.VMEM((2, ROWS, 4 * LANES), BF16),
+        ],
         compiler_params=LIMIT,
         name="predictor",
-    )(modal_unknowns, timestep_metric_scaling, mp, wt)
+    )(
+        modal_unknowns, timestep_metric_scaling, elastic, predictor_derivatives,
+        jnp.transpose(interior_restriction, (1, 0, 2)), e, f, g, h,
+    )
     face_rows = face_rows.reshape(faces_total, LANES)
 
     group_out, lower_out, upper_out = pl.pallas_call(
@@ -442,13 +450,12 @@
     tensors, sensitivity, _ = lax.optimization_barrier(
         (riemann_numerical_tables, thermal_diffusion_resolvent, lower_out)
     )
-    open_area, mi, wf, ws, wm, wp, vm = pl.pallas_call(
+    open_area, wf, ws, wm, wp, vm = pl.pallas_call(
         prepare_rest_kernel,
-        in_specs=whole(16),
-        out_specs=whole(7),
+        in_specs=whole(14),
+        out_specs=whole(6),
         out_shape=[
             shaped((4, elems)),
-            shaped((6 * PAD, ROWS), BF16),
             shaped((4, 2 * PAD, 2 * LANES), BF16),
             shaped((4, 2 * PAD, LANES), BF16),
             shaped((LANES, 3 * LANES)),
@@ -460,8 +467,6 @@
     )(
         rupture_side_index.reshape(1, -1),
         surface_measure_quotient,
-        elastic,
-        interior_gradient_tables,
         jnp.transpose(surface_raise_tables, (2, 0, 1)),
         jnp.transpose(tensors, (1, 0, 2)),
         boundary_polynomials_sampled,
@@ -492,43 +497,53 @@
     partial = pl.pallas_call(
         volume_kernel,
         grid=(elems // step,),
-        in_specs=[column(ROWS), column(3), column(ROWS), fixed((6 * PAD, ROWS))],
+        in_specs=[
+            column(ROWS), column(3), column(ROWS), fixed((Q, 3, Q)), fixed((3, NB, NB)),
+            fixed((ROWS, Q)), fixed((ROWS, NB)),
+        ],
+        scratch_shapes=[pltpu.VMEM((6 * PAD, ROWS), BF16)],
         out_specs=column(ROWS),
         out_shape=shaped((ROWS, elems)),
         compiler_params=LIMIT,
         name="volume",
-    )(modal_unknowns, timestep_metric_scaling, integral, mi)
+    )(
+        modal_unknowns, timestep_metric_scaling, integral, elastic, interior_gradient_tables, e, f
+    )
 
     faults, partial, top = lax.optimization_barrier((rupture_side_index, partial, top))
     extent = faces_total + 3072
-    payload, table = pl.pallas_call(
+    payload = pl.pallas_call(
         payload_kernel,
         in_specs=whole(7, (0, 1, 2), (3, 4, 5, 6)),
-        out_specs=whole(2, (), (0,)),
-        out_shape=[shaped((devices * 8, LANES)), pltpu.VMEM((extent + 8, LANES), F32)],
-        scratch_shapes=[pltpu.VMEM((devices * 8 + 8, LANES), F32), pltpu.SemaphoreType.DMA((4,))],
+        out_specs=whole(1, (), (0,))[0],
+        out_shape=shaped((devices * 8, LANES)),
+        scratch_shapes=[
+            pltpu.VMEM((devices * 8 + 8, LANES), F32),
+            pltpu.VMEM((extent + 8, LANES), F32),
+            pltpu.SemaphoreType.DMA((4,)),
+        ],
         compiler_params=LIMIT,
         name="payload",
-    )(faults, rupture_seat_partition, entry, face_rows, local(group), local(lower), local(upper))
+    )(faults, rupture_seat_partition, entry, face_rows, group, lower, upper)
     arrived = lax.all_to_all(payload, ("wide", "narrow"), split_axis=0, concat_axis=0, tiled=True)
-
-    entry = boundary_entry_index
 
     def half(first, value):
         return pl.pallas_call(
             lambda *refs: outside_kernel(first, *refs),
-            in_specs=whole(5, (0,), (2, 4)),
+            in_specs=whole(8, (0,), (1, 2, 3, 4, 5, 7)),
             out_specs=whole(1)[0],
             out_shape=shaped((ROWS, elems)),
             scratch_shapes=[
+                pltpu.VMEM((extent, LANES), F32),
                 pltpu.VMEM((elems, LANES), F32),
                 pltpu.VMEM((ROWS, elems), F32),
                 pltpu.VMEM((2, 2 * PAD, 2 * LANES), BF16),
+                pltpu.SemaphoreType.DMA((4,)),
                 pltpu.SemaphoreType.DMA((2,)),
             ],
             compiler_params=LIMIT,
             name="outside" + str(first),
-        )(entry, local(table), value, open_area, wf)
+        )(entry, face_rows, group, lower, upper, value, open_area, wf)
 
     partial, payload = lax.optimization_barrier((partial, payload))
     base = half(0, partial)
@@ -542,7 +557,7 @@
         compiler_params=LIMIT,
         name="fault",
     )(
-        local(arrived), top, flat(earlier_sliding_speed), flat(instant_sensitivity_a),
+        arrived, top, flat(earlier_sliding_speed), flat(instant_sensitivity_a),
         flat(aging_memory_theta), wm, wp, vm, pair,
     )
     returned = lax.all_to_all(imposed, ("wide", "narrow"), split_axis=0, concat_axis=0, tiled=True)
@@ -561,7 +576,7 @@
         ],
         compiler_params=LIMIT,
         name="finish",
-    )(rupture_side_index, rupture_seat_partition, local(returned), base, surface_measure_quotient, ws)
+    )(rupture_side_index, rupture_seat_partition, returned, base, surface_measure_quotient, ws)
     return advanced, new_temperature, new_pressure, rate.reshape(points)
 
 

time: 126 us -> 117 us (0.929)
  local copies, waits for them, and re-layouts: 28.3 us -> 2.61 us
  Pallas kernels: 60.7 us -> 80.9 us
  waiting for transfers between devices: 3.65 us -> 0.93 us
    unnamed x126 -> x14, local copies, waits for them, and re-layouts: 28.3 us -> 2.61 us
    pallas_call x2, Pallas kernels: 14.1 us -> 20.8 us  [half(): pl.pallas_call(lambda *refs: outside_kernel(first, *refs), in_specs=whole...]
    pallas_call x1, Pallas kernels: 10.3 us -> 16.1 us  [per_device(): pl.pallas_call(predictor_kernel, grid=(elems // step,), in_specs=[column(...]
    pallas_call x1, Pallas kernels: 2.85 us -> 8.04 us  [per_device(): pl.pallas_call(volume_kernel, grid=(elems // step,), in_specs=[column(ROW...]
    pallas_call x2 -> x1, Pallas kernels: 10 us -> 5.05 us  [per_device(): pl.pallas_call(prepare_rest_kernel, in_specs=whole(14), out_specs=whole(6...]
    all_to_all x1, waiting for transfers between devices: 3.11 us -> 0.01 us  [per_device(): lax.all_to_all(payload, ('wide', 'narrow'), split_axis=0, concat_axis=0,...]
    all_to_all x1, starting transfers between devices: 6.66 us -> 9.76 us  [per_device(): lax.all_to_all(imposed, ('wide', 'narrow'), split_axis=0, concat_axis=0,...]
    all_to_all x1, starting transfers between devices: 13.1 us -> 10.4 us  [per_device(): lax.all_to_all(payload, ('wide', 'narrow'), split_axis=0, concat_axis=0,...]
  transfers between devices with their start and end apart: 5 -> 5, of which waited for: 2 -> 1; matrix products, arithmetic and copies ran while one was open for 0% -> 0% of each run, Pallas kernels for 22% -> 34%
where the time goes in v4:
time: 117 us; the launch traced here: 116 us
  Pallas kernels  80.9 us (69%)
  starting transfers between devices  31.1 us (27%)
  local copies, waits for them, and re-layouts  2.61 us (2%)
    pallas_call x2, Pallas kernels, half(): pl.pallas_call(lambda *refs: outside_kernel(first, *refs), in_specs=whole...  20.8 us
    pallas_call x1, Pallas kernels, per_device(): pl.pallas_call(predictor_kernel, grid=(elems // step,), in_specs=[column(...  16.1 us
    all_to_all x1, starting transfers between devices, per_device(): lax.all_to_all(payload, ('wide', 'narrow'), split_axis=0, concat_axis=0,...  10.4 us
    all_to_all x1, starting transfers between devices, per_device(): lax.all_to_all(imposed, ('wide', 'narrow'), split_axis=0, concat_axis=0,...  9.76 us
    pallas_call x1, Pallas kernels, per_device(): pl.pallas_call(payload_kernel, in_specs=whole(7, (0, 1, 2), (3, 4, 5, 6))...  8.44 us
    pallas_call x1, Pallas kernels, per_device(): pl.pallas_call(volume_kernel, grid=(elems // step,), in_specs=[column(ROW...  8.04 us
    pallas_call x1, Pallas kernels, per_device(): pl.pallas_call(finish_kernel, in_specs=whole(6, (0, 1), (3,)), out_specs=...  6.76 us
    ppermute x2, starting transfers between devices, shift(): return lax.ppermute(array, axis, pairs)  5.95 us
  transfers between devices with their start and end apart: 5, of which 1 were waited for; matrix products, arithmetic and copies ran while one was open for 0% of the time, Pallas kernels for 34%

profile of v4, /device:TPU:1, one launch (start us, length us, event | category | flops | bytes accessed | tf_op | source)
XLA Modules:
  0.0 116.5 jit_solution(12932855025520387702)
XLA Ops:
  0.6 16.1 %predictor.1 = (f32[180,2048]{1,0:T(8,128)}, f32[4,2048,128]{2,1,0:T(8,128)}) custom-call(f32[180,2048]{1,0:T(8,128)} %u.3, f32[3,2048]{1,0:T(4,128)} %t.3, f32[9,3,9]{2,1,0:T(4,128)} %bitcast.31, f32[3,20,20]{2,1,0:T(8,128)} %pd.1, f32[10,4,20]{2,1,0:T(4,128)} %bitcast.35, f32[180,9]{1,0:T(8,128)} %constant.20.clone.e, f32[180,20]{1,0:T(8,128)} %constant.21.clone.f, ...), custom_call_target="tpu_custom_call" | custom-call | tf_op jit(solution)/shard_map/predictor/pallas_call | solution.py:416
  16.8 5.9 %halo_rows.1 = (f32[2048,128]{1,0:T(8,128)}, f32[512,128]{1,0:T(8,128)}, f32[512,128]{1,0:T(8,128)}) custom-call(s32[6,512]{1,0:T(8,128)} %index.1, f32[8192,128]{1,0:T(8,128)} %bitcast.17), custom_call_target="tpu_custom_call" | custom-call | tf_op jit(solution)/shard_map/halo_rows/pallas_call | solution.py:438
  22.7 0.0 copy-start.6
  22.7 0.0 copy-start.5
  22.7 5.0 %all-to-all-start = ((f32[4,512,128]{2,1,0:T(8,128)}), f32[4,512,128]{2,1,0:T(8,128)S(1)}, u32[]{:S(2)}, u32[]{:S(2)}) async-start(f32[4,512,128]{2,1,0:T(8,128)} %bitcast.27), calls=%async_computation | async-start | bytes 2097152 | tf_op jit(solution)/shard_map/all_to_all | solution.py:446
  27.7 0.0 copy-done.6
  27.7 2.9 %collective-permute-start.1 = (f32[512,128]{1,0:T(8,128)S(1)}, f32[512,128]{1,0:T(8,128)S(1)}, u32[]{:S(2)}, u32[]{:S(2)}) collective-permute-start(f32[512,128]{1,0:T(8,128)S(1)} %copy-done.6), channel_id=1, source_target_pairs={{4,0},{8,4},{12,8},{16,12},{20,16},{24,20},{28,24},{32,28},{36,32}... | collective-permute-start | bytes 786440 | tf_op jit(solution)/shard_map/ppermute | solution.py:378
  30.5 0.0 copy-done.5
  30.5 3.1 %collective-permute-start = (f32[512,128]{1,0:T(8,128)S(1)}, f32[512,128]{1,0:T(8,128)S(1)}, u32[]{:S(2)}, u32[]{:S(2)}) collective-permute-start(f32[512,128]{1,0:T(8,128)S(1)} %copy-done.5), channel_id=1, source_target_pairs={{0,4},{4,8},{8,12},{12,16},{16,20},{20,24},{24,28},{28,32},{32,36}... | collective-permute-start | bytes 786440 | tf_op jit(solution)/shard_map/ppermute | solution.py:378
  33.6 8.0 %volume.1.refs_5_ = f32[180,2048]{1,0:T(8,128)} custom-call(f32[180,2048]{1,0:T(8,128)} %u.3, f32[3,2048]{1,0:T(4,128)} %t.3, f32[180,2048]{1,0:T(8,128)} %get-tuple-element.30.integral, f32[9,3,9]{2,1,0:T(4,128)} %bitcast.32, f32[3,20,20]{2,1,0:T(8,128)} %kd.1, f32[180,9]{1,0:T(8,128)} %constant.20.clone.e, f32[180,20]{1,0:T(8,128)} %constant.21.clone.f), custom_call_target="tpu_custom_call" | custom-call | tf_op jit(solution)/shard_map/volume/pallas_call | solution.py:497
  41.7 5.8 %thermal.1 = (f32[64,8192]{1,0:T(8,128)}, f32[64,8192]{1,0:T(8,128)}, f32[64,128]{1,0:T(8,128)}) custom-call(f32[64,8192]{1,0:T(8,128)} %th.1, f32[64,8192]{1,0:T(8,128)} %fl.1, f32[1,8192]{1,0:T(1,128)} %bitcast.29, f32[64,1]{1,0:T(8,128)} %constant.28.clone.shape, f32[64,64]{1,0:T(8,128)} %tr, f32[64,64]{1,0:T(8,128)} %hr.1), custom_call_target="tpu_custom_call" | custom-call | tf_op jit(solution)/shard_map/thermal/pallas_call | solution.py:481
  47.5 0.0 collective-permute-done.1.upper.refs_4_
  47.5 0.0 copy-start.1
  47.5 0.0 collective-permute-done.lower.refs_3_
  47.5 0.0 copy-start.2
  47.5 0.0 all-to-all-done
  47.5 0.0 copy-start
  47.5 0.7 copy-done.1
  48.2 0.1 copy-done.2
  48.3 0.3 copy-done
  48.6 8.4 %payload.1 = f32[1024,128]{1,0:T(8,128)} custom-call(s32[512]{0:T(512)} %face.2, s32[512]{0:T(512)} %seat.3, s32[4,2048]{1,0:T(4,128)} %refs_0_.3, f32[8192,128]{1,0:T(8,128)} %bitcast.18, f32[2048,128]{1,0:T(8,128)} %bitcast.21, f32[512,128]{1,0:T(8,128)} %copy-done.2, f32[512,128]{1,0:T(8,128)} %copy-done.1), custom_call_target="tpu_custom_call" | custom-call | tf_op jit(solution)/shard_map/payload/pallas_call | solution.py:515
  57.1 10.4 %all-to-all-start.1 = ((f32[128,8,128]{2,1,0:T(8,128)}), f32[128,8,128]{2,1,0:T(8,128)S(1)}, u32[]{:S(2)}, u32[]{:S(2)}) async-start(f32[128,8,128]{2,1,0:T(8,128)} %bitcast.25), calls=%async_computation.1 | async-start | bytes 1048576 | tf_op jit(solution)/shard_map/all_to_all | solution.py:528
  67.5 5.1 %prepare_rest.1 = (f32[4,2048]{1,0:T(4,128)}, bf16[4,384,256]{2,1,0:T(8,128)(2,1)}, bf16[4,384,128]{2,1,0:T(8,128)(2,1)}, f32[128,384]{1,0:T(8,128)}, f32[128,384]{1,0:T(8,128)}, /*index=5*/f32[128,128]{1,0:T(8,128)}) custom-call(s32[1,512]{1,0:T(1,128)} %bitcast.37, f32[4,2048]{1,0:T(4,128)} %area.3, f32[10,4,20]{2,1,0:T(4,128)} %bitcast.36, ...), custom_call_target="tpu_custom_call" | custom-call | tf_op jit(solution)/shard_map/prepare_rest/pallas_call | solution.py:453
  72.5 10.4 %outside0.1.refs_5_ = f32[180,2048]{1,0:T(8,128)} custom-call(s32[4,2048]{1,0:T(4,128)} %refs_0_.3, f32[8192,128]{1,0:T(8,128)} %bitcast.19, f32[2048,128]{1,0:T(8,128)} %bitcast.22, f32[512,128]{1,0:T(8,128)} %copy-done.2, f32[512,128]{1,0:T(8,128)} %copy-done.1, f32[180,2048]{1,0:T(8,128)} %volume.1.refs_5_, f32[4,2048]{1,0:T(4,128)} %get-tuple-element.41.refs_6_, ...), custom_call_target="tpu_custom_call" | custom-call | tf_op jit(solution)/shard_map/outside0/pallas_call | solution.py:531
  82.9 0.0 all-to-all-done.1
  82.9 0.0 copy-start.3
  82.9 0.8 copy-done.3
  83.7 4.0 %fault.1 = (f32[512,128]{1,0:T(8,128)}, f32[64,128]{1,0:T(8,128)}) custom-call(f32[1024,128]{1,0:T(8,128)} %bitcast.24, f32[64,128]{1,0:T(8,128)} %get-tuple-element.44.top, f32[64,128]{1,0:T(8,128)} %bitcast.30, f32[64,128]{1,0:T(8,128)} %bitcast.33, f32[64,128]{1,0:T(8,128)} %bitcast.34, f32[128,384]{1,0:T(8,128)} %get-tuple-element.45.wm, ...), custom_call_target="tpu_custom_call" | custom-call | tf_op jit(solution)/shard_map/fault/pallas_call | solution.py:552
  87.7 9.8 %all-to-all-start.2 = ((f32[128,4,128]{2,1,0:T(4,128)}), f32[128,4,128]{2,1,0:T(4,128)S(1)}, u32[]{:S(2)}, u32[]{:S(2)}) async-start(f32[128,4,128]{2,1,0:T(4,128)} %bitcast.28), calls=%async_computation.2 | async-start | bytes 524288 | tf_op jit(solution)/shard_map/all_to_all | solution.py:563
  97.5 10.4 %outside2.1.base = f32[180,2048]{1,0:T(8,128)} custom-call(s32[4,2048]{1,0:T(4,128)} %refs_0_.3, f32[8192,128]{1,0:T(8,128)} %bitcast.20, f32[2048,128]{1,0:T(8,128)} %bitcast.23, f32[512,128]{1,0:T(8,128)} %copy-done.2, f32[512,128]{1,0:T(8,128)} %copy-done.1, f32[180,2048]{1,0:T(8,128)} %outside0.1.refs_5_, f32[4,2048]{1,0:T(4,128)} %get-tuple-element.41.refs_6_, ...), custom_call_target="tpu_custom_call" | custom-call | tf_op jit(solution)/shard_map/outside2/pallas_call | solution.py:531
  107.9 0.9 all-to-all-done.2
  108.8 0.0 copy-start.4
  108.8 0.7 copy-done.4
  109.5 6.8 %finish.1 = f32[180,2048]{1,0:T(8,128)} custom-call(s32[512]{0:T(512)} %face.2, s32[512]{0:T(512)} %seat.3, f32[512,128]{1,0:T(8,128)} %bitcast.26, f32[180,2048]{1,0:T(8,128)} %outside2.1.base, f32[4,2048]{1,0:T(4,128)} %area.3, bf16[4,384,128]{2,1,0:T(8,128)(2,1)} %get-tuple-element.52.ws), custom_call_target="tpu_custom_call" | custom-call | tf_op jit(solution)/shard_map/finish/pallas_call | solution.py:567
Async XLA Ops:
  22.7 5.0 %copy-start.6 = (f32[512,128]{1,0:T(8,128)S(1)}, f32[512,128]{1,0:T(8,128)}, u32[]{:S(2)}) copy-start(f32[512,128]{1,0:T(8,128)} %get-tuple-element.37) | copy-start | bytes 786436
  22.7 7.8 %copy-start.5 = (f32[512,128]{1,0:T(8,128)S(1)}, f32[512,128]{1,0:T(8,128)}, u32[]{:S(2)}) copy-start(f32[512,128]{1,0:T(8,128)} %get-tuple-element.32) | copy-start | bytes 786436
  22.7 24.8 %all-to-all-start = ((f32[4,512,128]{2,1,0:T(8,128)}), f32[4,512,128]{2,1,0:T(8,128)S(1)}, u32[]{:S(2)}, u32[]{:S(2)}) async-start(f32[4,512,128]{2,1,0:T(8,128)} %bitcast.27), calls=%async_computation | async-start | bytes 2097152 | tf_op jit(solution)/shard_map/all_to_all | solution.py:446
  27.7 19.8 %collective-permute-start.1 = (f32[512,128]{1,0:T(8,128)S(1)}, f32[512,128]{1,0:T(8,128)S(1)}, u32[]{:S(2)}, u32[]{:S(2)}) collective-permute-start(f32[512,128]{1,0:T(8,128)S(1)} %copy-done.6), channel_id=1, source_target_pairs={{4,0},{8,4},{12,8},{16,12},{20,16},{24,20},{28,24},{32,28},{36,32}... | collective-permute-start | bytes 786440 | tf_op jit(solution)/shard_map/ppermute | solution.py:378
  30.5 17.0 %collective-permute-start = (f32[512,128]{1,0:T(8,128)S(1)}, f32[512,128]{1,0:T(8,128)S(1)}, u32[]{:S(2)}, u32[]{:S(2)}) collective-permute-start(f32[512,128]{1,0:T(8,128)S(1)} %copy-done.5), channel_id=1, source_target_pairs={{0,4},{4,8},{8,12},{12,16},{16,20},{20,24},{24,28},{28,32},{32,36}... | collective-permute-start | bytes 786440 | tf_op jit(solution)/shard_map/ppermute | solution.py:378
  47.5 0.7 copy-start.1
  47.5 0.8 copy-start.2
  47.5 1.1 copy-start
  57.1 25.8 %all-to-all-start.1 = ((f32[128,8,128]{2,1,0:T(8,128)}), f32[128,8,128]{2,1,0:T(8,128)S(1)}, u32[]{:S(2)}, u32[]{:S(2)}) async-start(f32[128,8,128]{2,1,0:T(8,128)} %bitcast.25), calls=%async_computation.1 | async-start | bytes 1048576 | tf_op jit(solution)/shard_map/all_to_all | solution.py:528
  82.9 0.8 copy-start.3
  87.7 21.1 %all-to-all-start.2 = ((f32[128,4,128]{2,1,0:T(4,128)}), f32[128,4,128]{2,1,0:T(4,128)S(1)}, u32[]{:S(2)}, u32[]{:S(2)}) async-start(f32[128,4,128]{2,1,0:T(4,128)} %bitcast.28), calls=%async_computation.2 | async-start | bytes 524288 | tf_op jit(solution)/shard_map/all_to_all | solution.py:563
  108.8 0.7 copy-start.4

commit v5 on v4

--- a/solution.py
+++ b/solution.py
@@ -155,7 +155,31 @@
     )
 
 
-def predictor_kernel(u, t, a, pd, rs, e, f, g, h, integral, faces, padded, mp, wt):
+def take_rows(index, row, source, target, base):
+    def body(i, carry):
+        first = pl.multiple_of(i * LANES, LANES)
+        listed = index.at[row, pl.ds(first, LANES)]
+        place = target.at[pl.ds(base + first, LANES)]
+        for at in range(0, LANES, 16):
+            rows = [source[pl.ds(listed[at + k], 1), :] for k in range(16)]
+            for k in range(16):
+                place[at + k : at + k + 1, :] = rows[k]
+        return carry
+
+    lax.fori_loop(0, index.shape[1] // LANES, body, 0)
+
+
+def send_kernel(index, faces, group, lower, upper):
+    for peer in range(4):
+        take_rows(index, peer, faces, group, peer * index.shape[1])
+    take_rows(index, 4, faces, lower, 0)
+    take_rows(index, 5, faces, upper, 0)
+
+
+def predictor_kernel(
+    u, t, a, pd, rs, e, f, g, h, index,
+    integral, faces, group, lower, upper, padded, mp, wt, traces,
+):
     @pl.when(pl.program_id(0) == 0)
     def _():
         prepare_kernel(a, pd, rs, e, f, g, h, mp, wt)
@@ -174,7 +198,15 @@
     xh, xl = halves(padded[...].T[:, 0:ROWS])
     rows = single(xh, wt[0]) + (single(xh, wt[1]) + single(xl, wt[0]))
     for face in range(4):
-        faces[face] = rows[:, face * LANES : (face + 1) * LANES]
+        block = rows[:, face * LANES : (face + 1) * LANES]
+        faces[face] = block
+        step = block.shape[0]
+        first = face * (traces.shape[0] // 4) + pl.program_id(0) * step
+        traces[pl.ds(pl.multiple_of(first, step), step), :] = block
+
+    @pl.when(pl.program_id(0) == pl.num_programs(0) - 1)
+    def _():
+        send_kernel(index, traces, group, lower, upper)
 
 
 def volume_kernel(u, t, integral, a, kd, e, f, partial, mi):
@@ -188,27 +220,6 @@
             put(mi, ((), d * PAD, 0), left * grid_of(fb, kd[d], f_), 3 * PAD)
 
     partial[...] = u[...] + directional(mi[...], integral[...], t[...])
-
-
-def take_rows(index, row, source, target, base):
-    def body(i, carry):
-        first = pl.multiple_of(i * LANES, LANES)
-        listed = index.at[row, pl.ds(first, LANES)]
-        place = target.at[pl.ds(base + first, LANES)]
-        for at in range(0, LANES, 16):
-            rows = [source[pl.ds(listed[at + k], 1), :] for k in range(16)]
-            for k in range(16):
-                place[at + k : at + k + 1, :] = rows[k]
-        return carry
-
-    lax.fori_loop(0, index.shape[1] // LANES, body, 0)
-
-
-def send_kernel(index, faces, group, lower, upper):
-    for peer in range(4):
-        take_rows(index, peer, faces, group, peer * index.shape[1])
-    take_rows(index, 4, faces, lower, 0)
-    take_rows(index, 5, faces, upper, 0)
 
 
 def thermal_kernel(th, fl, speed, shape, tr, hr, new_th, new_fl, top):
@@ -413,36 +424,37 @@
     step = 512
     column = lambda rows: pl.BlockSpec((rows, step), lambda i: (0, i))
     fixed = lambda shape: pl.BlockSpec(shape, lambda i: (0,) * len(shape))
-    integral, face_rows = pl.pallas_call(
+    integral, face_rows, group_out, lower_out, upper_out = pl.pallas_call(
         predictor_kernel,
         grid=(elems // step,),
         in_specs=[
             column(ROWS), column(3), fixed((Q, 3, Q)), fixed((3, NB, NB)), fixed((NJ, 4, NB)),
             fixed((ROWS, Q)), fixed((ROWS, NB)), fixed((LANES, Q)), fixed((LANES, NJ)),
-        ],
-        out_specs=[column(ROWS), pl.BlockSpec((4, step, LANES), lambda i: (0, i, 0))],
-        out_shape=[shaped((ROWS, elems)), shaped((4, elems, LANES))],
+            pl.BlockSpec(memory_space=SMEM),
+        ],
+        out_specs=[
+            column(ROWS), pl.BlockSpec((4, step, LANES), lambda i: (0, i, 0)),
+            fixed((2048, LANES)), fixed((512, LANES)), fixed((512, LANES)),
+        ],
+        out_shape=[
+            shaped((ROWS, elems)), shaped((4, elems, LANES)),
+            shaped((2048, LANES)), shaped((512, LANES)), shaped((512, LANES)),
+        ],
         scratch_shapes=[
             pltpu.VMEM((256, step), F32),
             pltpu.VMEM((6 * PAD, ROWS), BF16),
             pltpu.VMEM((2, ROWS, 4 * LANES), BF16),
+            pltpu.VMEM((faces_total, LANES), F32),
         ],
         compiler_params=LIMIT,
         name="predictor",
     )(
         modal_unknowns, timestep_metric_scaling, elastic, predictor_derivatives,
         jnp.transpose(interior_restriction, (1, 0, 2)), e, f, g, h,
+        outbound_ghost_indices,
     )
     face_rows = face_rows.reshape(faces_total, LANES)
 
-    group_out, lower_out, upper_out = pl.pallas_call(
-        send_kernel,
-        in_specs=whole(2, (0,)),
-        out_specs=whole(3),
-        out_shape=[shaped((2048, LANES)), shaped((512, LANES)), shaped((512, LANES))],
-        compiler_params=LIMIT,
-        name="halo_rows",
-    )(outbound_ghost_indices, face_rows)
     group = lax.all_to_all(group_out, "narrow", split_axis=0, concat_axis=0, tiled=True)
     lower = shift(lower_out, "wide", 1)
     upper = shift(upper_out, "wide", -1)

time: 117 us -> 115 us (0.983)
  Pallas kernels: 80.9 us -> 76.8 us
  starting transfers between devices: 31.1 us -> 33.3 us
    pallas_call x1 -> x0, Pallas kernels: 5.91 us -> none  [per_device(): pl.pallas_call(send_kernel, in_specs=whole(2, (0,)), out_specs=whole(3),...]
    pallas_call x1, Pallas kernels: 16.1 us -> 19.4 us  [per_device(): pl.pallas_call(predictor_kernel, grid=(elems // step,), in_specs=[column(...]
    all_to_all x1, starting transfers between devices: 10.4 us -> 12.6 us  [per_device(): lax.all_to_all(payload, ('wide', 'narrow'), split_axis=0, concat_axis=0,...]
    pallas_call x1, Pallas kernels: 8.44 us -> 7.2 us  [per_device(): pl.pallas_call(payload_kernel, in_specs=whole(7, (0, 1, 2), (3, 4, 5, 6))...]
  transfers between devices with their start and end apart: 5 -> 5, of which waited for: 1 -> 1; matrix products, arithmetic and copies ran while one was open for 0% -> 0% of each run, Pallas kernels for 34% -> 35%
where the time goes in v5:
time: 115 us
  Pallas kernels  76.8 us (67%)
  starting transfers between devices  33.3 us (29%)
  local copies, waits for them, and re-layouts  2.64 us (2%)
    pallas_call x2, Pallas kernels, half(): pl.pallas_call(lambda *refs: outside_kernel(first, *refs), in_specs=whole...  20.8 us
    pallas_call x1, Pallas kernels, per_device(): pl.pallas_call(predictor_kernel, grid=(elems // step,), in_specs=[column(...  19.4 us
    all_to_all x1, starting transfers between devices, per_device(): lax.all_to_all(payload, ('wide', 'narrow'), split_axis=0, concat_axis=0,...  12.6 us
    all_to_all x1, starting transfers between devices, per_device(): lax.all_to_all(imposed, ('wide', 'narrow'), split_axis=0, concat_axis=0,...  9.76 us
    pallas_call x1, Pallas kernels, per_device(): pl.pallas_call(volume_kernel, grid=(elems // step,), in_specs=[column(ROW...  8.05 us
    pallas_call x1, Pallas kernels, per_device(): pl.pallas_call(payload_kernel, in_specs=whole(7, (0, 1, 2), (3, 4, 5, 6))...  7.2 us
    pallas_call x1, Pallas kernels, per_device(): pl.pallas_call(finish_kernel, in_specs=whole(6, (0, 1), (3,)), out_specs=...  6.42 us
    ppermute x2, starting transfers between devices, shift(): return lax.ppermute(array, axis, pairs)  5.95 us
  transfers between devices with their start and end apart: 5, of which 1 were waited for; matrix products, arithmetic and copies ran while one was open for 0% of the time, Pallas kernels for 35%

profile of v5, /device:TPU:1, one launch (start us, length us, event | category | flops | bytes accessed | tf_op | source)
XLA Modules:
  0.0 114.6 jit_solution(11873461162857052806)
XLA Ops:
  0.6 19.4 %predictor.1 = (f32[180,2048]{1,0:T(8,128)}, f32[4,2048,128]{2,1,0:T(8,128)}, f32[2048,128]{1,0:T(8,128)}, f32[512,128]{1,0:T(8,128)}, f32[512,128]{1,0:T(8,128)}) custom-call(f32[180,2048]{1,0:T(8,128)} %u.3, f32[3,2048]{1,0:T(4,128)} %t.3, f32[9,3,9]{2,1,0:T(4,128)} %bitcast.30, f32[3,20,20]{2,1,0:T(8,128)} %pd.1, f32[10,4,20]{2,1,0:T(4,128)} %bitcast.34, ...), custom_call_target="tpu_custom_call" | custom-call | tf_op jit(solution)/shard_map/predictor/pallas_call | solution.py:427
  20.1 0.0 copy-start.6
  20.1 0.0 copy-start.5
  20.1 5.0 %all-to-all-start = ((f32[4,512,128]{2,1,0:T(8,128)}), f32[4,512,128]{2,1,0:T(8,128)S(1)}, u32[]{:S(2)}, u32[]{:S(2)}) async-start(f32[4,512,128]{2,1,0:T(8,128)} %bitcast.26), calls=%async_computation | async-start | bytes 2097152 | tf_op jit(solution)/shard_map/all_to_all | solution.py:458
  25.1 0.0 copy-done.6
  25.1 2.9 %collective-permute-start.1 = (f32[512,128]{1,0:T(8,128)S(1)}, f32[512,128]{1,0:T(8,128)S(1)}, u32[]{:S(2)}, u32[]{:S(2)}) collective-permute-start(f32[512,128]{1,0:T(8,128)S(1)} %copy-done.6), channel_id=1, source_target_pairs={{4,0},{8,4},{12,8},{16,12},{20,16},{24,20},{28,24},{32,28},{36,32}... | collective-permute-start | bytes 786440 | tf_op jit(solution)/shard_map/ppermute | solution.py:389
  28.0 0.0 copy-done.5
  28.0 3.1 %collective-permute-start = (f32[512,128]{1,0:T(8,128)S(1)}, f32[512,128]{1,0:T(8,128)S(1)}, u32[]{:S(2)}, u32[]{:S(2)}) collective-permute-start(f32[512,128]{1,0:T(8,128)S(1)} %copy-done.5), channel_id=1, source_target_pairs={{0,4},{4,8},{8,12},{12,16},{16,20},{20,24},{24,28},{28,32},{32,36}... | collective-permute-start | bytes 786440 | tf_op jit(solution)/shard_map/ppermute | solution.py:389
  31.1 8.0 %volume.1.refs_5_ = f32[180,2048]{1,0:T(8,128)} custom-call(f32[180,2048]{1,0:T(8,128)} %u.3, f32[3,2048]{1,0:T(4,128)} %t.3, f32[180,2048]{1,0:T(8,128)} %get-tuple-element.30.integral, f32[9,3,9]{2,1,0:T(4,128)} %bitcast.31, f32[3,20,20]{2,1,0:T(8,128)} %kd.1, f32[180,9]{1,0:T(8,128)} %constant.20.clone.e, f32[180,20]{1,0:T(8,128)} %constant.21.clone.f), custom_call_target="tpu_custom_call" | custom-call | tf_op jit(solution)/shard_map/volume/pallas_call | solution.py:509
  39.1 5.8 %thermal.1 = (f32[64,8192]{1,0:T(8,128)}, f32[64,8192]{1,0:T(8,128)}, f32[64,128]{1,0:T(8,128)}) custom-call(f32[64,8192]{1,0:T(8,128)} %th.1, f32[64,8192]{1,0:T(8,128)} %fl.1, f32[1,8192]{1,0:T(1,128)} %bitcast.28, f32[64,1]{1,0:T(8,128)} %constant.28.clone.shape, f32[64,64]{1,0:T(8,128)} %tr, f32[64,64]{1,0:T(8,128)} %hr.1), custom_call_target="tpu_custom_call" | custom-call | tf_op jit(solution)/shard_map/thermal/pallas_call | solution.py:493
  44.9 0.0 collective-permute-done.1.upper.refs_4_
  44.9 0.0 copy-start.1
  44.9 0.0 collective-permute-done.lower.refs_3_
  44.9 0.0 copy-start.2
  45.0 0.0 all-to-all-done
  45.0 0.0 copy-start
  45.0 0.7 copy-done.1
  45.7 0.1 copy-done.2
  45.8 0.3 copy-done
  46.1 7.2 %payload.1 = f32[1024,128]{1,0:T(8,128)} custom-call(s32[512]{0:T(512)} %face.2, s32[512]{0:T(512)} %seat.3, s32[4,2048]{1,0:T(4,128)} %refs_0_.3, f32[8192,128]{1,0:T(8,128)} %bitcast.17, f32[2048,128]{1,0:T(8,128)} %bitcast.20, f32[512,128]{1,0:T(8,128)} %copy-done.2, f32[512,128]{1,0:T(8,128)} %copy-done.1), custom_call_target="tpu_custom_call" | custom-call | tf_op jit(solution)/shard_map/payload/pallas_call | solution.py:527
  53.3 12.6 %all-to-all-start.1 = ((f32[128,8,128]{2,1,0:T(8,128)}), f32[128,8,128]{2,1,0:T(8,128)S(1)}, u32[]{:S(2)}, u32[]{:S(2)}) async-start(f32[128,8,128]{2,1,0:T(8,128)} %bitcast.24), calls=%async_computation.1 | async-start | bytes 1048576 | tf_op jit(solution)/shard_map/all_to_all | solution.py:540
  65.9 5.1 %prepare_rest.1 = (f32[4,2048]{1,0:T(4,128)}, bf16[4,384,256]{2,1,0:T(8,128)(2,1)}, bf16[4,384,128]{2,1,0:T(8,128)(2,1)}, f32[128,384]{1,0:T(8,128)}, f32[128,384]{1,0:T(8,128)}, /*index=5*/f32[128,128]{1,0:T(8,128)}) custom-call(s32[1,512]{1,0:T(1,128)} %bitcast.36, f32[4,2048]{1,0:T(4,128)} %area.3, f32[10,4,20]{2,1,0:T(4,128)} %bitcast.35, ...), custom_call_target="tpu_custom_call" | custom-call | tf_op jit(solution)/shard_map/prepare_rest/pallas_call | solution.py:465
  71.0 10.4 %outside0.1.refs_5_ = f32[180,2048]{1,0:T(8,128)} custom-call(s32[4,2048]{1,0:T(4,128)} %refs_0_.3, f32[8192,128]{1,0:T(8,128)} %bitcast.18, f32[2048,128]{1,0:T(8,128)} %bitcast.21, f32[512,128]{1,0:T(8,128)} %copy-done.2, f32[512,128]{1,0:T(8,128)} %copy-done.1, f32[180,2048]{1,0:T(8,128)} %volume.1.refs_5_, f32[4,2048]{1,0:T(4,128)} %get-tuple-element.41.refs_6_, ...), custom_call_target="tpu_custom_call" | custom-call | tf_op jit(solution)/shard_map/outside0/pallas_call | solution.py:543
  81.4 0.0 all-to-all-done.1
  81.4 0.0 copy-start.3
  81.4 0.8 copy-done.3
  82.2 4.0 %fault.1 = (f32[512,128]{1,0:T(8,128)}, f32[64,128]{1,0:T(8,128)}) custom-call(f32[1024,128]{1,0:T(8,128)} %bitcast.23, f32[64,128]{1,0:T(8,128)} %get-tuple-element.44.top, f32[64,128]{1,0:T(8,128)} %bitcast.29, f32[64,128]{1,0:T(8,128)} %bitcast.32, f32[64,128]{1,0:T(8,128)} %bitcast.33, f32[128,384]{1,0:T(8,128)} %get-tuple-element.45.wm, ...), custom_call_target="tpu_custom_call" | custom-call | tf_op jit(solution)/shard_map/fault/pallas_call | solution.py:564
  86.2 9.8 %all-to-all-start.2 = ((f32[128,4,128]{2,1,0:T(4,128)}), f32[128,4,128]{2,1,0:T(4,128)S(1)}, u32[]{:S(2)}, u32[]{:S(2)}) async-start(f32[128,4,128]{2,1,0:T(4,128)} %bitcast.27), calls=%async_computation.2 | async-start | bytes 524288 | tf_op jit(solution)/shard_map/all_to_all | solution.py:575
  95.9 10.4 %outside2.1.base = f32[180,2048]{1,0:T(8,128)} custom-call(s32[4,2048]{1,0:T(4,128)} %refs_0_.3, f32[8192,128]{1,0:T(8,128)} %bitcast.19, f32[2048,128]{1,0:T(8,128)} %bitcast.22, f32[512,128]{1,0:T(8,128)} %copy-done.2, f32[512,128]{1,0:T(8,128)} %copy-done.1, f32[180,2048]{1,0:T(8,128)} %outside0.1.refs_5_, f32[4,2048]{1,0:T(4,128)} %get-tuple-element.41.refs_6_, ...), custom_call_target="tpu_custom_call" | custom-call | tf_op jit(solution)/shard_map/outside2/pallas_call | solution.py:543
  106.4 0.9 all-to-all-done.2
  107.3 0.0 copy-start.4
  107.3 0.7 copy-done.4
  108.0 6.4 %finish.1 = f32[180,2048]{1,0:T(8,128)} custom-call(s32[512]{0:T(512)} %face.2, s32[512]{0:T(512)} %seat.3, f32[512,128]{1,0:T(8,128)} %bitcast.25, f32[180,2048]{1,0:T(8,128)} %outside2.1.base, f32[4,2048]{1,0:T(4,128)} %area.3, bf16[4,384,128]{2,1,0:T(8,128)(2,1)} %get-tuple-element.52.ws), custom_call_target="tpu_custom_call" | custom-call | tf_op jit(solution)/shard_map/finish/pallas_call | solution.py:579
Async XLA Ops:
  20.1 5.0 %copy-start.6 = (f32[512,128]{1,0:T(8,128)S(1)}, f32[512,128]{1,0:T(8,128)}, u32[]{:S(2)}) copy-start(f32[512,128]{1,0:T(8,128)} %get-tuple-element.37) | copy-start | bytes 786436
  20.1 7.9 %copy-start.5 = (f32[512,128]{1,0:T(8,128)S(1)}, f32[512,128]{1,0:T(8,128)}, u32[]{:S(2)}) copy-start(f32[512,128]{1,0:T(8,128)} %get-tuple-element.31) | copy-start | bytes 786436
  20.1 24.9 %all-to-all-start = ((f32[4,512,128]{2,1,0:T(8,128)}), f32[4,512,128]{2,1,0:T(8,128)S(1)}, u32[]{:S(2)}, u32[]{:S(2)}) async-start(f32[4,512,128]{2,1,0:T(8,128)} %bitcast.26), calls=%async_computation | async-start | bytes 2097152 | tf_op jit(solution)/shard_map/all_to_all | solution.py:458
  25.1 19.8 %collective-permute-start.1 = (f32[512,128]{1,0:T(8,128)S(1)}, f32[512,128]{1,0:T(8,128)S(1)}, u32[]{:S(2)}, u32[]{:S(2)}) collective-permute-start(f32[512,128]{1,0:T(8,128)S(1)} %copy-done.6), channel_id=1, source_target_pairs={{4,0},{8,4},{12,8},{16,12},{20,16},{24,20},{28,24},{32,28},{36,32}... | collective-permute-start | bytes 786440 | tf_op jit(solution)/shard_map/ppermute | solution.py:389
  28.0 17.0 %collective-permute-start = (f32[512,128]{1,0:T(8,128)S(1)}, f32[512,128]{1,0:T(8,128)S(1)}, u32[]{:S(2)}, u32[]{:S(2)}) collective-permute-start(f32[512,128]{1,0:T(8,128)S(1)} %copy-done.5), channel_id=1, source_target_pairs={{0,4},{4,8},{8,12},{12,16},{16,20},{20,24},{24,28},{28,32},{32,36}... | collective-permute-start | bytes 786440 | tf_op jit(solution)/shard_map/ppermute | solution.py:389
  44.9 0.7 copy-start.1
  44.9 0.8 copy-start.2
  45.0 1.1 copy-start
  53.3 28.1 %all-to-all-start.1 = ((f32[128,8,128]{2,1,0:T(8,128)}), f32[128,8,128]{2,1,0:T(8,128)S(1)}, u32[]{:S(2)}, u32[]{:S(2)}) async-start(f32[128,8,128]{2,1,0:T(8,128)} %bitcast.24), calls=%async_computation.1 | async-start | bytes 1048576 | tf_op jit(solution)/shard_map/all_to_all | solution.py:540
  81.4 0.8 copy-start.3
  86.2 21.1 %all-to-all-start.2 = ((f32[128,4,128]{2,1,0:T(4,128)}), f32[128,4,128]{2,1,0:T(4,128)S(1)}, u32[]{:S(2)}, u32[]{:S(2)}) async-start(f32[128,4,128]{2,1,0:T(4,128)} %bitcast.27), calls=%async_computation.2 | async-start | bytes 524288 | tf_op jit(solution)/shard_map/all_to_all | solution.py:575
  107.3 0.7 copy-start.4
